TPU v7x, 32 devices: a whole 2x2x4 slice. The times are simulated.
32 devices in a mesh: dp: 8 (over y, x, core), tensor: 4 (over z).
Axes of the slice: x: 2, y: 2, z: 4, core: 2. Of those that a mesh axis runs over, the one named last changes fastest.
Arguments:
- layer_input: bfloat16 [16384, 768], P(('dp', 'tensor')), may hold values from -12 to 12
- segments: int32 [16384], P('dp'), may hold values from 0 to 63, never falling along the last dimension, each value on 1 to 1024 neighbouring positions
- w_qkv: bfloat16 [3, 768, 768], P(None, None, 'tensor'), may hold values from -0.21875 to 0.21875
- bias_qv: bfloat16 [2, 768], P(None, 'tensor'), may hold values from -1.5 to 1.5
- w_out: bfloat16 [768, 768], P('tensor'), may hold values from -1.25 to 1.25
- b_out: bfloat16 [768], replicated, may hold values from -1.5 to 1.5
- gain_attn: bfloat16 [768], replicated, may hold values from 0.5 to 1.5
- shift_attn: bfloat16 [768], replicated, may hold values from -1.5 to 1.5
- w_in: bfloat16 [768, 3072], P(None, 'tensor'), may hold values from -0.21875 to 0.21875
- b_in: bfloat16 [3072], P('tensor'), may hold values from -1.5 to 1.5
- w_down: bfloat16 [3072, 768], P('tensor'), may hold values from -0.109375 to 0.109375
- b_down: bfloat16 [768], replicated, may hold values from -1.5 to 1.5
- gain_ffn: bfloat16 [768], replicated, may hold values from 0.5 to 1.5
- shift_ffn: bfloat16 [768], replicated, may hold values from -1.5 to 1.5
- act_scale: float32 [4], replicated, may hold values from 4 to 77
- out_grad: bfloat16 [16384, 768], P(('dp', 'tensor')), may hold values from -6 to 6
Outputs:
- layer_output: bfloat16 [16384, 768], P(('dp', 'tensor'))
- input_grad: float32 [16384, 768], P(('dp', 'tensor'))
- grad_qkv: float32 [3, 768, 768], P(None, None, 'tensor')
- grad_bias_qv: float32 [2, 768], P(None, 'tensor')
- grad_out: float32 [768, 768], P('tensor')
- grad_b_out: float32 [768], replicated
- grad_gain_attn: float32 [768], replicated
- grad_shift_attn: float32 [768], replicated
- grad_in: float32 [768, 3072], P(None, 'tensor')
- grad_b_in: float32 [3072], P('tensor')
- grad_down: float32 [3072, 768], P('tensor')
- grad_b_down: float32 [768], replicated
- grad_gain_ffn: float32 [768], replicated
- grad_shift_ffn: float32 [768], replicated
- new_scale: float32 [4], replicated
- batch_max: float32 [4], replicated
Inputs may be any that keep to these rules, and one draw needn't show every extreme that they name: `segments`: segment ids never fall along the tokens; each document has 1 to 1024 tokens and one has exactly 1024; attention stays within each row of 1024 tokens.
All inputs are finite; a program needn't handle non-finite values.
Results may differ from a plain program's by a relative error of at most 0.013.
The roundings to bfloat16 on the way count: a program that leaves them out, or rounds other values in their place, can miss the bound.
Values may be sent and summed in bfloat16 or wider, within the bound.
No kernel may reach another device: no remote copies, remote signals or barrier semaphores. Data moves between devices by JAX's collectives and lax.ppermute only.
A program may use at most 192 MiB of HBM per device.

v0:
```python
import functools
import math

import jax
import jax.numpy as jnp
from jax import lax
from jax.experimental import pallas as pl
from jax.experimental.pallas import tpu as pltpu
from jax.sharding import PartitionSpec as P

HEAD = 64
LEN = 1024
HALF = LEN // 2
BLOCK = 256

EPSILON = 1e-12
DECAY = 0.9999
MASKED = -1e30
ORDER = (0, 1, 3, 2)
JOINT = ("dp", "tensor")
BF16 = jnp.bfloat16
F32 = jnp.float32


def norm_forward(resid, gain, shift):
    row_mean = jnp.mean(resid, axis=-1, keepdims=True)
    centred = resid - row_mean
    spread = jnp.mean(centred * centred, axis=-1, keepdims=True)
    inverse = lax.rsqrt(spread + EPSILON)
    normed = centred * inverse
    return (normed * gain + shift, normed, inverse)


def norm_backward(upstream, normed, inverse, gain):
    scaled = upstream * gain
    mean_first = jnp.mean(scaled, axis=-1, keepdims=True)
    mean_second = jnp.mean(scaled * normed, axis=-1, keepdims=True)
    return inverse * (scaled - mean_first - normed * mean_second)


def nt(a, b):
    return lax.dot_general(a, b, (((1,), (1,)), ((), ())), preferred_element_type=F32)


def nn(a, b):
    return lax.dot_general(a, b, (((1,), (0,)), ((), ())), preferred_element_type=F32)


def tn(a, b):
    return lax.dot_general(a, b, (((0,), (0,)), ((), ())), preferred_element_type=F32)


def attend_kernel(q_ref, k_ref, v_ref, seg_col_ref, seg_row_ref, ctx_ref, lse_ref):
    low = lax.broadcasted_iota(jnp.int32, (BLOCK, 2 * HEAD), 1) < HEAD
    keys = k_ref[...]
    values = v_ref[...]
    for block in range(LEN // BLOCK):
        rows = pl.ds(block * BLOCK, BLOCK)
        queries = q_ref[rows, :] * jnp.asarray(HEAD**-0.5, BF16)
        same = seg_col_ref[rows, :] == seg_row_ref[...]
        parts, logs = [], []
        for head in range(2):
            own = low if head == 0 else jnp.logical_not(low)
            scores = nt(jnp.where(own, queries, jnp.zeros_like(queries)), keys)
            scores = jnp.where(same, scores, MASKED)
            top = jnp.max(scores, axis=-1, keepdims=True)
            exponent = jnp.exp(scores - top)
            total = jnp.sum(exponent, axis=-1, keepdims=True)
            attention = (exponent * (1.0 / total)).astype(BF16)
            parts.append(nn(attention, values))
            logs.append(top + jnp.log(total))
        ctx_ref[rows, :] = jnp.where(low, parts[0], parts[1])
        lse_ref[0, :, rows] = jnp.transpose(jnp.concatenate(logs, axis=1))


def attend(proj, seg_col, seg_row, pairs_of_heads):
    n = pairs_of_heads
    return pl.pallas_call(
        attend_kernel,
        grid=(n,),
        in_specs=[
            pl.BlockSpec((LEN, 2 * HEAD), lambda i: (0, 3 * i)),
            pl.BlockSpec((LEN, 2 * HEAD), lambda i: (0, 3 * i + 1)),
            pl.BlockSpec((LEN, 2 * HEAD), lambda i: (0, 3 * i + 2)),
            pl.BlockSpec((LEN, 1), lambda i: (0, 0)),
            pl.BlockSpec((1, LEN), lambda i: (0, 0)),
        ],
        out_specs=[
            pl.BlockSpec((LEN, 2 * HEAD), lambda i: (0, i)),
            pl.BlockSpec((1, 2, LEN), lambda i: (i, 0, 0)),
        ],
        out_shape=[
            jax.ShapeDtypeStruct((LEN, n * 2 * HEAD), F32),
            jax.ShapeDtypeStruct((n, 2, LEN), F32),
        ],
        name="attend",
    )(proj, proj, proj, seg_col, seg_row)


def attend_back_kernel(
    q_ref,
    k_ref,
    v_ref,
    rows_ref,
    back_ref,
    ctx_ref,
    lse_ref,
    seg_col_ref,
    seg_row_ref,
    limit_ref,
    grad_ref,
    sum_ref,
    acc_ref,
    grads_ref,
    inner_ref,
):
    low = lax.broadcasted_iota(jnp.int32, (BLOCK, 2 * HEAD), 1) < HEAD
    for block in range(LEN // BLOCK):
        rows = pl.ds(block * BLOCK, BLOCK)
        context = ctx_ref[rows, :]
        grad = nt(rows_ref[rows, :], back_ref[...])
        grad = jnp.where(jnp.abs(context) <= limit_ref[0], grad, 0.0).astype(BF16)
        grads_ref[rows, :] = grad
        both = grad.astype(F32) * context
        inner = [
            jnp.sum(jnp.where(own, both, 0.0), axis=1, keepdims=True)
            for own in (low, jnp.logical_not(low))
        ]
        inner_ref[:, rows] = jnp.transpose(jnp.concatenate(inner, axis=1))
    queries = q_ref[...]
    grads = grads_ref[...]
    value_sum = jnp.zeros((1, 2 * HEAD), F32)
    for block in range(LEN // BLOCK):
        rows = pl.ds(block * BLOCK, BLOCK)
        keys = k_ref[rows, :]
        scaled_keys = keys * jnp.asarray(HEAD**-0.5, BF16)
        values = v_ref[rows, :]
        same = seg_col_ref[rows, :] == seg_row_ref[...]
        value_parts, key_parts = [], []
        for head in range(2):
            own = low if head == 0 else jnp.logical_not(low)
            zero = jnp.zeros_like(keys)
            scores = nt(jnp.where(own, scaled_keys, zero), queries)
            logs = lse_ref[0, head : head + 1, :]
            attention = jnp.where(same, jnp.exp(scores - logs), 0.0)
            value_parts.append(nn(attention.astype(BF16), grads))
            grad_attention = nt(jnp.where(own, values, zero), grads)
            inner = inner_ref[head : head + 1, :]
            grad_score = (attention * (grad_attention - inner) * HEAD**-0.5).astype(BF16)
            key_parts.append(nn(grad_score, queries))
            part = tn(grad_score, jnp.where(own, keys, zero))
            if block == 0 and head == 0:
                acc_ref[...] = part
            else:
                acc_ref[...] += part
        grad_value = jnp.where(low, value_parts[0], value_parts[1])
        value_sum += jnp.sum(grad_value, axis=0, keepdims=True)
        grad_ref[rows, 4 * HEAD :] = grad_value.astype(BF16)
        grad_ref[rows, 2 * HEAD : 4 * HEAD] = jnp.where(low, key_parts[0], key_parts[1]).astype(BF16)
    grad_query = acc_ref[...]
    grad_ref[:, : 2 * HEAD] = grad_query.astype(BF16)
    sum_ref[0, 0:1, :] = jnp.sum(grad_query, axis=0, keepdims=True)
    sum_ref[0, 1:2, :] = value_sum


def attend_back(proj, grad_rows, w_back, context, lse, seg_col, seg_row, limit, first, count):
    width = w_back.shape[1]
    return pl.pallas_call(
        attend_back_kernel,
        grid=(count,),
        in_specs=[
            pl.BlockSpec((LEN, 2 * HEAD), lambda i: (0, 3 * (first + i))),
            pl.BlockSpec((LEN, 2 * HEAD), lambda i: (0, 3 * (first + i) + 1)),
            pl.BlockSpec((LEN, 2 * HEAD), lambda i: (0, 3 * (first + i) + 2)),
            pl.BlockSpec((LEN, width), lambda i: (0, 0)),
            pl.BlockSpec((2 * HEAD, width), lambda i: (first + i, 0)),
            pl.BlockSpec((LEN, 2 * HEAD), lambda i: (0, first + i)),
            pl.BlockSpec((1, 2, LEN), lambda i: (first + i, 0, 0)),
            pl.BlockSpec((LEN, 1), lambda i: (0, 0)),
            pl.BlockSpec((1, LEN), lambda i: (0, 0)),
            pl.BlockSpec(memory_space=pltpu.SMEM),
        ],
        out_specs=[
            pl.BlockSpec((LEN, 6 * HEAD), lambda i: (0, i)),
            pl.BlockSpec((1, 2, 2 * HEAD), lambda i: (i, 0, 0)),
        ],
        out_shape=[
            jax.ShapeDtypeStruct((LEN, count * 6 * HEAD), BF16),
            jax.ShapeDtypeStruct((count, 2, 2 * HEAD), F32),
        ],
        scratch_shapes=[
            pltpu.VMEM((LEN, 2 * HEAD), F32),
            pltpu.VMEM((LEN, 2 * HEAD), BF16),
            pltpu.VMEM((2, LEN), F32),
        ],
        name="attend_back",
    )(proj, proj, proj, grad_rows, w_back, context, lse, seg_col, seg_row, limit)


class Links:
    def __init__(self, dp, depths):
        self.dp, self.depths = dp, depths
        self.planes = dp // 2
        place = lax.axis_index("dp")
        self.half, self.plane = place % 2, place // 2
        self.depth = lax.axis_index("tensor")
        self.square = self.planes == 4 and depths == 4

    def permute(self, array, move):
        pairs = []
        for place in range(self.dp):
            for depth in range(self.depths):
                to = move(place // 2, place % 2, depth)
                if to is not None:
                    plane, half, level = to
                    pairs.append(
                        (place * self.depths + depth, (2 * plane + half) * self.depths + level)
                    )
        return lax.ppermute(array, JOINT, pairs)

    def rows_home(self, array):
        return self.permute(
            array, lambda e, c, z: (e, z % 2, z - z % 2 + c) if c != z % 2 else None
        )

    def at_home(self, own, moved):
        return jnp.where(self.depth % 2 == self.half, own, moved)

    def other_half(self, array):
        return self.permute(array, lambda e, c, z: (e, 1 - c, z))

    def across(self, array, step, only=None):
        return self.permute(
            array,
            lambda e, c, z: (e ^ step, c, z) if only is None or only(c, z) else None,
        )

    def along(self, array, step):
        return self.permute(array, lambda e, c, z: (e, c, z ^ step))

    def spread_near(self, piece, only=None):
        return self.across(piece, 1, only), self.across(piece, 2, only)

    def spread_far(self, piece, near, only=None):
        first, second = near
        cut = piece.shape[-2] // 16 * 8
        third_low = self.across(second[..., :cut, :], 1, only)
        third_high = self.across(first[..., cut:, :], 2, only)
        return [piece, first, second, jnp.concatenate([third_low, third_high], axis=-2)]

    def spread(self, piece, only=None):
        return [piece] + [self.across(piece, step, only) for step in (1, 2, 3)]

    def in_order(self, pieces):
        stack = jnp.stack(pieces)
        return jnp.stack(
            [lax.dynamic_index_in_dim(stack, j ^ self.plane, 0, False) for j in range(4)]
        )

    @property
    def inside(self):
        return self.depth // 2 == self.half

    @property
    def even(self):
        return self.depth % 2 == 0

    def pair_near(self, array):
        return self.permute(array, lambda e, c, z: (e, c, z ^ 1) if z // 2 == c else None)

    def pair_out(self, array):
        return self.permute(array, lambda e, c, z: (e, c, z ^ 2) if z // 2 == c else None)

    def pair_back(self, array):
        return self.permute(array, lambda e, c, z: (e, c, z ^ 2) if z // 2 != c else None)

    def pair_cross(self, array):
        return self.permute(array, lambda e, c, z: (e, c, z ^ 3) if z // 2 != c else None)

    def halves_in_order(self, mine):
        other = self.other_half(mine)
        first = self.half == 0
        return jnp.stack([jnp.where(first, mine, other), jnp.where(first, other, mine)])

    def even_first(self, mine, other):
        return jnp.stack([jnp.where(self.even, mine, other), jnp.where(self.even, other, mine)])


def exact_parts(values):
    high = lax.reduce_precision(values, 8, 7)
    rest = values - high
    middle = lax.reduce_precision(rest, 8, 7)
    return jnp.concatenate([high, middle, rest - middle]).astype(BF16)


def exact_sum(parts):
    rows = parts.shape[0] // 3
    parts = parts.astype(F32)
    return parts[:rows] + parts[rows : 2 * rows] + parts[2 * rows :]


def merge(both, other):
    last = lax.broadcasted_iota(jnp.int32, both.shape, 0) == 6
    return jnp.where(last, jnp.maximum(both, other), both + other)


def sync(*values):
    return lax.optimization_barrier(values)


def plain_all(links, grads):
    blank = jnp.zeros((4, 2) + grads.shape[1:], F32)
    full = lax.dynamic_update_slice_in_dim(blank, grads[:, None].astype(F32), links.half, 1)
    shard = lax.psum_scatter(full, "tensor", scatter_dimension=0, tiled=False)
    return lax.psum(shard, "dp")


def plain_pair(links, grads):
    blank = jnp.zeros((4,) + grads.shape[:1] + grads.shape[2:], F32)
    own = grads.swapaxes(0, 1).astype(F32)
    full = lax.dynamic_update_slice_in_dim(blank, own, 2 * links.half, 0)
    shard = lax.psum_scatter(full, "tensor", scatter_dimension=0, tiled=False)
    return lax.psum(shard, "dp")


def on_device(
    sizes,
    layer_input,
    segments,
    w_qkv,
    bias_qv,
    w_out,
    b_out,
    gain_attn,
    shift_attn,
    w_in,
    b_in,
    w_down,
    b_down,
    gain_ffn,
    shift_ffn,
    act_scale,
    out_grad,
):
    links = Links(*sizes)
    width = layer_input.shape[1]
    local = w_qkv.shape[2]
    heads = local // HEAD
    chunk = HEAD // 4
    units = w_in.shape[1]
    quarter = units // 8
    gain_first = gain_attn.astype(F32)
    gain_second = gain_ffn.astype(F32)

    per = 3 * heads * chunk
    more = heads * chunk

    rows = jnp.concatenate([jnp.swapaxes(w_qkv, 1, 2), w_out[None]])
    rows = rows.reshape(4, heads, 4, chunk, width)
    rows = rows.transpose(2, 0, 1, 3, 4).reshape(4, per + more, width)
    tail = bias_qv.reshape(2, heads, 4, chunk).transpose(2, 0, 1, 3).reshape(4, 1, 2 * more)
    tail = jnp.pad(tail, ((0, 0), (0, 7), (0, width - tail.shape[2])))
    attn_pack = jnp.concatenate([rows, tail], axis=1)
    if links.square:
        attn_mine = lax.dynamic_index_in_dim(attn_pack, links.plane, 0, False)
        attn_next = links.pair_near(attn_mine)
    x_home = links.at_home(layer_input, links.rows_home(layer_input))
    seg_rows = segments.reshape(2, LEN)
    seg_mine = lax.dynamic_index_in_dim(seg_rows, links.depth // 2, 0, False).reshape(8, LEN // 8)
    seg_next = links.other_half(seg_mine)
    seg_home = links.at_home(seg_mine, seg_next).reshape(2, HALF)
    seg_home = jnp.where(links.half == 0, seg_home, seg_home[::-1]).reshape(LEN)
    seg_col, seg_row = seg_home[:, None], seg_home[None, :]
    ffn_half = jnp.concatenate(
        [
            lax.dynamic_index_in_dim(w_in.T.reshape(2, 4, quarter, width), links.half, 0, False),
            lax.dynamic_index_in_dim(w_down.reshape(2, 4, quarter, width), links.half, 0, False),
            jnp.pad(
                lax.dynamic_index_in_dim(b_in.reshape(2, 4, 1, quarter), links.half, 0, False),
                ((0, 0), (0, 7), (0, width - quarter)),
            ),
        ],
        axis=1,
    )
    if links.square:
        ffn_own = jnp.stack(
            [lax.dynamic_index_in_dim(ffn_half, j ^ links.plane, 0, False) for j in ORDER]
        )
        ffn_one = links.along(ffn_own[0], 1)
        attn_both = links.even_first(attn_mine, attn_next)
        attn_far = links.pair_out(attn_both)
        attn_far, ffn_one, ffn_mine = sync(attn_far, ffn_one, ffn_own[0])
        attn_both = jnp.where(links.inside, attn_both, attn_far)
        attn_near = links.spread_near(attn_both)
        ffn_two = links.along(ffn_mine, 2)
        attn_near, ffn_two, ffn_mine = sync(attn_near, ffn_two, ffn_mine)
        ffn_three = links.along(ffn_mine, 3)
        attn_full = links.spread_far(attn_both, attn_near)
        attn_full, ffn_three = sync(attn_full, ffn_three)
        attn_full = jnp.stack(attn_full)
        ffn_in = jnp.stack([ffn_one, ffn_two, ffn_three])
    else:
        attn_full = lax.all_gather(attn_pack, "tensor", axis=0, tiled=False)
        attn_full = lax.dynamic_slice_in_dim(attn_full, 2 * links.half, 2, 0).swapaxes(0, 1)
        ffn_in = lax.all_gather(ffn_half, "tensor", axis=0, tiled=False)

    x_full = x_home.astype(F32)
    x_quant = jnp.clip(x_full, -act_scale[0], act_scale[0]).astype(BF16)
    x_rows = jnp.concatenate([x_quant, links.other_half(x_quant)])

    weights = attn_full[:, :, : per + more].reshape(4, 2, 4, heads, chunk, width)
    weights = weights.transpose(2, 1, 3, 0, 4, 5).reshape(4, heads, 2 * HEAD, width)
    w_proj = weights[:3].swapaxes(0, 1).reshape(6 * local, width)
    w_back = weights[3].reshape(2 * local, width)
    biases = attn_full[:, :, per + more, : 2 * more].reshape(4, 2, 2, heads, chunk)
    biases = biases.transpose(2, 1, 3, 0, 4).reshape(2, 2 * local).astype(F32)
    bias_all = jnp.stack([biases[0], jnp.zeros_like(biases[0]), biases[1]])
    bias_all = bias_all.reshape(3, heads, 2 * HEAD).swapaxes(0, 1).reshape(6 * local)

    proj = (nt(x_rows, w_proj) + bias_all).astype(BF16)
    proj, ffn_in, out_grad = sync(proj, ffn_in, out_grad)
    if links.square:
        ffn_near = links.spread_near(ffn_in)
    upstream = links.rows_home(out_grad)
    context, lse = attend(proj, seg_col, seg_row, heads)
    context, upstream = sync(context, upstream)
    upstream = links.at_home(out_grad, upstream).astype(F32)
    ctx_quant = jnp.clip(context, -act_scale[1], act_scale[1]).astype(BF16)
    attn_part = nn(ctx_quant, w_back)
    if links.square:
        attn_part, ffn_near = sync(attn_part, ffn_near)
        pieces = links.spread_far(ffn_in, ffn_near)
        ffn_full = jnp.stack(
            [jnp.concatenate([ffn_own[i][None], pieces[j]]) for i, j in enumerate(ORDER)]
        )
    else:
        ffn_full = ffn_in.swapaxes(0, 1)
    attn_out = attn_part[:HALF] + links.other_half(attn_part[HALF:]) + b_out.astype(F32)
    hidden, normed_attn, inverse_attn = norm_forward(
        x_full + attn_out, gain_first, shift_attn.astype(F32)
    )
    hid_quant = jnp.clip(hidden, -act_scale[2], act_scale[2]).astype(BF16)
    hid_rows = jnp.concatenate([hid_quant, links.other_half(hid_quant)])

    w_up = ffn_full[:, :, :quarter].reshape(2 * units, width)
    w_low = ffn_full[:, :, quarter : 2 * quarter].reshape(2 * units, width)
    b_up = ffn_full[:, :, 2 * quarter, :quarter].reshape(2 * units).astype(F32)
    pre_act = nt(hid_rows, w_up) + b_up
    normal_cdf = 0.5 * (1.0 + lax.erf(pre_act * 0.5**0.5))
    activated = pre_act * normal_cdf
    slope = normal_cdf + pre_act * jnp.exp(-0.5 * pre_act * pre_act) / math.sqrt(2.0 * math.pi)
    slope = jnp.where(jnp.abs(activated) <= act_scale[3], slope, 0.0)
    act_quant = jnp.clip(activated, -act_scale[3], act_scale[3]).astype(BF16)
    ffn_part = nn(act_quant, w_low)
    ffn_out = ffn_part[:HALF] + links.other_half(ffn_part[HALF:])
    final, normed_ffn, inverse_ffn = norm_forward(
        hidden + ffn_out + b_down.astype(F32), gain_second, shift_ffn.astype(F32)
    )
    final = final.astype(BF16)
    layer_output = links.rows_home(final)
    maxima = jnp.stack(
        [
            jnp.max(jnp.abs(x_full)),
            jnp.max(jnp.abs(context)),
            jnp.max(jnp.abs(hidden)),
            jnp.max(jnp.max(jnp.abs(activated), axis=0)),
        ]
    )

    grad_gain_ffn = jnp.sum(upstream * normed_ffn, axis=0)
    grad_shift_ffn = jnp.sum(upstream, axis=0)
    grad_second = norm_backward(upstream, normed_ffn, inverse_ffn, gain_second)
    grad_b_down = jnp.sum(grad_second, axis=0)
    grad_final = grad_second.astype(BF16)
    grad_rows = jnp.concatenate([grad_final, links.other_half(grad_final)])
    down = tn(act_quant, grad_rows).astype(BF16).reshape(4, 4, quarter, width)
    grad_pre = nt(grad_rows, w_low) * slope
    grad_b_in = jnp.sum(grad_pre, axis=0)
    grad_pre_b = grad_pre.astype(BF16)
    up = tn(grad_pre_b, hid_rows).astype(BF16).reshape(4, 4, quarter, width)
    tail = jnp.pad(
        grad_b_in.astype(BF16).reshape(4, 4, 1, quarter),
        ((0, 0), (0, 0), (0, 7), (0, width - quarter)),
    )
    ffn_grads = jnp.concatenate([up, down, tail], axis=2)
    if links.square:
        ffn_grads, grad_pre_b = sync(ffn_grads, grad_pre_b)
        ffn_x = links.across(ffn_grads[1:3, :2], 1)
        ffn_y = links.across(ffn_grads[2:4, 2:], 2)
    hid_part = nn(grad_pre_b, w_up)
    grad_hid = hid_part[:HALF] + links.other_half(hid_part[HALF:])

    grad_hidden = grad_second + grad_hid * (jnp.abs(hidden) <= act_scale[2]).astype(F32)
    grad_gain_attn = jnp.sum(grad_hidden * normed_attn, axis=0)
    grad_shift_attn = jnp.sum(grad_hidden, axis=0)
    grad_first = norm_backward(grad_hidden, normed_attn, inverse_attn, gain_first)
    grad_b_out = jnp.sum(grad_first, axis=0)
    grad_attn = grad_first.astype(BF16)
    grad_attn_rows = jnp.concatenate([grad_attn, links.other_half(grad_attn)])
    sums = [grad_b_out, grad_gain_attn, grad_shift_attn, grad_b_down, grad_gain_ffn, grad_shift_ffn]
    sums = jnp.stack([*sums, jnp.pad(maxima, (0, width - 4)), jnp.zeros(width)])

    out = tn(ctx_quant, grad_attn_rows).astype(BF16).reshape(2, heads, 4, chunk, width)
    out = out.transpose(2, 0, 1, 3, 4).reshape(4, 2, more, width)
    limit = act_scale[1:2]

    def back(first, count):
        return attend_back(
            proj, grad_attn_rows, w_back, context, lse, seg_col, seg_row, limit, first, count
        )

    if links.square:
        early, early_sums = back(0, 1)
        sums = merge(sums, links.other_half(sums))
        early, grad_attn_rows, ffn_x, ffn_y, layer_output, sums = sync(
            early, grad_attn_rows, ffn_x, ffn_y, layer_output, sums
        )
        low = [ffn_grads[0, :2] + ffn_x[0].astype(F32), ffn_grads[3, :2] + ffn_x[1].astype(F32)]
        high = [ffn_grads[0, 2:] + ffn_y[1].astype(F32), ffn_grads[1, 2:] + ffn_y[0].astype(F32)]
        ffn_y = links.across(low[1].astype(BF16), 2)
        ffn_x = links.across(high[1].astype(BF16), 1)
        early_w = tn(early, x_rows).astype(BF16)
        late, late_sums = back(1, heads - 1)
        late, ffn_x, ffn_y = sync(late, ffn_x, ffn_y)
        ffn_low = low[0] + ffn_y.astype(F32)
        ffn_in = links.along((high[0] + ffn_x.astype(F32)).astype(BF16), 2)
        grad_w = jnp.concatenate([early_w, tn(late, x_rows).astype(BF16)])
        proj_sums = jnp.concatenate([early_sums, late_sums])
    else:
        late, proj_sums = back(0, heads)
        grad_w = tn(late, x_rows).astype(BF16)
    grad_w = grad_w.reshape(heads, 3, 2, 4, chunk, width).transpose(1, 0, 2, 3, 4, 5)
    grad_w = grad_w.reshape(3, 2, heads, 4, chunk, width).transpose(3, 1, 0, 2, 4, 5)
    grad_w = grad_w.reshape(4, 2, per, width)
    grad_b = jnp.stack([proj_sums[:, 0], proj_sums[:, 1]]).reshape(2, 2, heads, 4, chunk)
    grad_b = grad_b.transpose(3, 1, 0, 2, 4).reshape(4, 2, 1, 2 * more).astype(BF16)
    grad_b = jnp.pad(grad_b, ((0, 0), (0, 0), (0, 7), (0, width - 2 * more)))
    grad_w = jnp.concatenate([grad_w, out, grad_b], axis=2)
    if links.square:
        grad_w, late = sync(grad_w, late)
        tall = grad_w.shape[2]
        grad_w = grad_w.reshape(4, 2 * tall, width)
        sums_sent = exact_parts(sums)
        proj_in = [
            links.across(jnp.concatenate([grad_w[step], sums_sent]), step) for step in (1, 2, 3)
        ]
        x_part = nn(early, w_proj[: 6 * HEAD]) + nn(late, w_proj[6 * HEAD :])
    else:
        x_part = nn(late, w_proj)
    grad_x = x_part[:HALF] + links.other_half(x_part[HALF:])
    input_grad = grad_first + grad_x * (jnp.abs(x_full) <= act_scale[0]).astype(F32)
    input_grad = input_grad.astype(BF16)
    input_grad = links.at_home(input_grad, links.rows_home(input_grad)).astype(F32)

    if links.square:
        proj_in, x_part = sync(proj_in, x_part)
        total = grad_w[0].astype(F32)
        for part in proj_in:
            total = total + part[: 2 * tall].astype(F32)
            sums = merge(sums, exact_sum(part[2 * tall :]))
        mine = jnp.where(links.even, total[:tall], total[tall:])
        other = jnp.where(links.even, total[tall:], total[:tall])
        sums_sent = exact_parts(sums)
        other = jnp.concatenate([other.astype(BF16), sums_sent])
        proj_in = [
            links.pair_near(other),
            links.pair_back(jnp.concatenate([mine.astype(BF16), sums_sent])),
            links.pair_cross(other),
        ]
        ffn_in, total = sync(ffn_in, total)
        ffn_low = ffn_low + ffn_in.astype(F32)
        ffn_in = links.along(ffn_low[1].astype(BF16), 1)
        for part in proj_in:
            mine = mine + part[:tall].astype(F32)
            sums = merge(sums, exact_sum(part[tall:]))
        proj_all = links.spread(mine.astype(BF16), lambda c, z: z // 2 == c)
        ffn_mine = (ffn_low[0] + ffn_in.astype(F32)).astype(BF16)
        ffn_all = links.spread(ffn_mine)
        proj_all, ffn_all = sync(proj_all, ffn_all)
        proj_all = jnp.concatenate([*proj_all, exact_parts(sums)])
        proj_all = jnp.where(links.inside, proj_all, links.other_half(proj_all))
        ffn_all = links.halves_in_order(links.in_order(ffn_all))
        sums = exact_sum(proj_all[4 * tall :])
        proj_grads = links.in_order(list(proj_all[: 4 * tall].reshape(4, tall, width)))
    else:
        ffn_all = plain_all(links, ffn_grads.swapaxes(0, 1))
        proj_grads = plain_pair(links, grad_w)
        sums = jnp.concatenate([lax.psum(sums[:6], JOINT), lax.pmax(sums[6:], JOINT)])
    maxima = sums[6, :4]
    new_scale = DECAY * act_scale + (1.0 - DECAY) * maxima

    up_grads, down_grads = ffn_all[:, :, :quarter], ffn_all[:, :, quarter : 2 * quarter]
    out_grads = proj_grads[:, per : per + more]
    grad_qkv = proj_grads[:, :per].reshape(4, 3, heads, chunk, width)
    grad_qkv = grad_qkv.transpose(1, 4, 2, 0, 3).reshape(3, width, local).astype(F32)
    grad_bias_qv = (
        proj_grads[:, per + more, : 2 * more]
        .reshape(4, 2, heads, chunk)
        .transpose(1, 2, 0, 3)
        .reshape(2, local)
        .astype(F32)
    )
    grad_out = out_grads.reshape(4, heads, chunk, width).transpose(1, 0, 2, 3)
    return (
        links.at_home(final, layer_output),
        input_grad,
        grad_qkv,
        grad_bias_qv,
        grad_out.reshape(local, width).astype(F32),
        sums[0],
        sums[1],
        sums[2],
        up_grads.reshape(units, width).astype(F32).T,
        ffn_all[:, :, 2 * quarter, :quarter].reshape(units).astype(F32),
        down_grads.reshape(units, width).astype(F32),
        sums[3],
        sums[4],
        sums[5],
        new_scale,
        maxima,
    )


def solution(mesh):
    in_specs = (
        P(("dp", "tensor"), None),
        P("dp"),
        P(None, None, "tensor"),
        P(None, "tensor"),
        P("tensor", None),
        P(),
        P(),
        P(),
        P(None, "tensor"),
        P("tensor"),
        P("tensor", None),
        P(),
        P(),
        P(),
        P(),
        P(("dp", "tensor"), None),
    )
    out_specs = (
        P(("dp", "tensor"), None),
        P(("dp", "tensor"), None),
        P(None, None, "tensor"),
        P(None, "tensor"),
        P("tensor", None),
        P(),
        P(),
        P(),
        P(None, "tensor"),
        P("tensor"),
        P("tensor", None),
        P(),
        P(),
        P(),
        P(),
        P(),
    )
    sizes = (mesh.shape["dp"], mesh.shape["tensor"])
    return jax.shard_map(
        functools.partial(on_device, sizes),
        mesh=mesh,
        in_specs=in_specs,
        out_specs=out_specs,
        check_vma=False,
    )
```

profile of v0, /device:TPU:1, one launch (start us, length us, event | category | flops | bytes accessed | tf_op | source)
XLA Modules:
  0.0 348.9 jit_solution(12034308844462202309)
XLA Ops:
  11.9 9.4 %collective-permute-start = (bf16[512,768]{1,0:T(8,128)(2,1)S(1)}, bf16[512,768]{1,0:T(8,128)(2,1)}, u32[]{:S(2)}, u32[]{:S(2)}) collective-permute-start(bf16[512,768]{1,0:T(8,128)(2,1)S(1)} %copy-done.33), channel_id=1, source_target_pairs={{1,4},{3,6},{4,1},{6,3},{9,12},{11,14},{12,9},{14,11},{17,20},{19,... | collective-permute-start | bytes 2359304 | tf_op jit(solution)/shard_map/ppermute | solution.py:219
  21.3 9.3 %collective-permute-done.3 = bf16[2,200,768]{2,1,0:T(8,128)(2,1)} collective-permute-done((bf16[2,200,768]{2,1,0:T(8,128)(2,1)S(1)}, bf16[2,200,768]{2,1,0:T(8,128)(2,1)}, u32[]{:S(2)}, u32[]{:S(2)}) %collective-permute-start.3) | collective-permute-done | bytes 614432 | tf_op jit(solution)/shard_map/ppermute | solution.py:219
  34.2 4.2 %collective-permute-start.7 = (bf16[200,768]{1,0:T(8,128)(2,1)S(1)}, bf16[200,768]{1,0:T(8,128)(2,1)S(1)}, u32[]{:S(2)}, u32[]{:S(2)}) collective-permute-start(bf16[200,768]{1,0:T(8,128)(2,1)S(1)} %bitcast.215), channel_id=1, source_target_pairs={{0,2},{1,3},{2,0},{3,1},{4,6},{5,7},{6,4},{7,5},{8,10},{9,11},{10,... | collective-permute-start | bytes 921608 | tf_op jit(solution)/shard_map/ppermute | solution.py:219
  40.3 11.5 %collective-permute-done.7 = bf16[200,768]{1,0:T(8,128)(2,1)S(1)} collective-permute-done((bf16[200,768]{1,0:T(8,128)(2,1)S(1)}, bf16[200,768]{1,0:T(8,128)(2,1)S(1)}, u32[]{:S(2)}, u32[]{:S(2)}) %collective-permute-start.7) | collective-permute-done | bytes 307232 | tf_op jit(solution)/shard_map/ppermute | solution.py:219
  61.4 4.9 %collective-permute-done.10 = bf16[200,768]{1,0:T(8,128)(2,1)S(1)} collective-permute-done((bf16[200,768]{1,0:T(8,128)(2,1)S(1)}, bf16[200,768]{1,0:T(8,128)(2,1)S(1)}, u32[]{:S(2)}, u32[]{:S(2)}) %collective-permute-start.10) | collective-permute-done | bytes 307232 | tf_op jit(solution)/shard_map/ppermute | solution.py:219
  69.6 5.4 %add_convert_fusion.q_ref.k_ref.v_ref = bf16[1024,1152]{1,0:T(8,128)(2,1)} fusion(bf16[1152,768]{1,0:T(8,128)(2,1)S(1)} %bitcast.212, f32[1152]{0:T(1024)S(1)} %add.282, bf16[512,768]{1,0:T(8,128)(2,1)} %collective-permute-done.1, bf16[512,768]{1,0:T(8,128)(2,1)} %fusion.20), kind=kOutput, calls=%fused_computation.16 | convolution fusion | flops 1817444352 | bytes 5706240 | tf_op jit(solution)/shard_map/dot_general | solution.py:42
  74.9 5.4 %collective-permute-start.12 = (bf16[512,768]{1,0:T(8,128)(2,1)}, bf16[512,768]{1,0:T(8,128)(2,1)}, u32[]{:S(2)}, u32[]{:S(2)}) collective-permute-start(bf16[512,768]{1,0:T(8,128)(2,1)} %param.31), channel_id=1, source_target_pairs={{1,4},{3,6},{4,1},{6,3},{9,12},{11,14},{12,9},{14,11},{17,20},{19,... | collective-permute-start | bytes 2359304 | tf_op jit(solution)/shard_map/ppermute | solution.py:219
  85.4 18.1 %attend.1 = (f32[1024,384]{1,0:T(8,128)}, f32[3,2,1024]{2,1,0:T(2,128)}) custom-call(bf16[1024,1152]{1,0:T(8,128)(2,1)} %add_convert_fusion.q_ref.k_ref.v_ref, bf16[1024,1152]{1,0:T(8,128)(2,1)} %add_convert_fusion.q_ref.k_ref.v_ref, bf16[1024,1152]{1,0:T(8,128)(2,1)} %add_convert_fusion.q_ref.k_ref.v_ref, s32[1024,1]{1,0:T(8,128)} %bitcast.181, ...), custom_call_target="tpu_custom_call" | custom-call | tf_op jit(solution)/shard_map/attend/pallas_call | solution.py:78
  103.5 3.0 fusion.44
  129.0 6.1 %minimum_convert_fusion = (bf16[1024,1536]{1,0:T(8,128)(2,1)S(1)}, f32[1024,1536]{1,0:T(8,128)S(1)}) fusion(f32[1536]{0:T(1024)S(1)} %reshape.276, bf16[]{:T(256)S(6)} %neg.14, f32[]{:T(128)} %bitcast.36, bf16[1536,768]{1,0:T(8,128)(2,1)S(1)} %bitcast.205, bf16[512,768]{1,0:T(8,128)(2,1)} %collective-permute-done.16, bf16[512,768]{1,0:T(8,128)(2,1)} %minimum_convert_fusion.1), kind=kOutput, calls=%fused_computation.9 | convolution fusion | flops 2434793472 | bytes 13375494 | tf_op jit(solution)/shard_map/dot_general | solution.py:42
  150.7 7.7 %fusion.68 = (bf16[1024,1536]{1,0:T(8,128)(2,1)}, bf16[1536]{0:T(1024)(128)(2,1)S(1)}) fusion(f32[]{:T(128)} %bitcast.36, f32[1024,1536]{1,0:T(8,128)S(1)} %get-tuple-element.253, f32[1536]{0:T(1024)S(1)} %reshape.276, bf16[1536,768]{1,0:T(8,128)(2,1)S(1)} %bitcast.204, bf16[512,768]{1,0:T(8,128)(2,1)S(1)} %collective-permute-done.20, ...), kind=kOutput, calls=%fused_computation.266 | convolution fusion | flops 2444229120 | bytes 13378564 | tf_op jit(solution)/shard_map/dot_general | solution.py:42
  158.4 4.7 %convolution_convert_fusion = bf16[1536,768]{1,0:T(8,128)(2,1)S(1)} fusion(bf16[1024,1536]{1,0:T(8,128)(2,1)} %copy-done.54, bf16[512,768]{1,0:T(8,128)(2,1)S(1)} %collective-permute-done.20, bf16[512,768]{1,0:T(8,128)(2,1)S(1)} %convert_element_type.325), kind=kOutput, calls=%fused_computation.17 | convolution fusion | flops 2420244480 | bytes 7077888 | tf_op jit(solution)/shard_map/dot_general | solution.py:50
  163.2 4.3 %convolution_convert_fusion.1 = bf16[1536,768]{1,0:T(8,128)(2,1)S(1)} fusion(bf16[1024,1536]{1,0:T(8,128)(2,1)S(1)} %copy-done.55, bf16[512,768]{1,0:T(8,128)(2,1)} %collective-permute-done.16, bf16[512,768]{1,0:T(8,128)(2,1)} %minimum_convert_fusion.1), kind=kOutput, calls=%fused_computation.18 | convolution fusion | flops 2420244480 | bytes 7077888 | tf_op jit(solution)/shard_map/dot_general | solution.py:50
  193.9 10.2 %attend_back.2 = (bf16[1024,384]{1,0:T(8,128)(2,1)}, f32[1,2,128]{2,1,0:T(2,128)}) custom-call(bf16[1024,1152]{1,0:T(8,128)(2,1)} %add_convert_fusion.q_ref.k_ref.v_ref, bf16[1024,1152]{1,0:T(8,128)(2,1)} %add_convert_fusion.q_ref.k_ref.v_ref, bf16[1024,1152]{1,0:T(8,128)(2,1)} %add_convert_fusion.q_ref.k_ref.v_ref, ...), custom_call_target="tpu_custom_call" | custom-call | tf_op jit(solution)/shard_map/attend_back/pallas_call | solution.py:168
  204.1 3.2 collective-permute-done.23
  212.9 17.7 %attend_back.3 = (bf16[1024,768]{1,0:T(8,128)(2,1)}, f32[2,2,128]{2,1,0:T(2,128)}) custom-call(bf16[1024,1152]{1,0:T(8,128)(2,1)} %add_convert_fusion.q_ref.k_ref.v_ref, bf16[1024,1152]{1,0:T(8,128)(2,1)} %add_convert_fusion.q_ref.k_ref.v_ref, bf16[1024,1152]{1,0:T(8,128)(2,1)} %add_convert_fusion.q_ref.k_ref.v_ref, ...), custom_call_target="tpu_custom_call" | custom-call | tf_op jit(solution)/shard_map/attend_back/pallas_call | solution.py:168
  249.0 10.8 %collective-permute-done.31 = bf16[424,768]{1,0:T(8,128)(2,1)S(1)} collective-permute-done((bf16[424,768]{1,0:T(8,128)(2,1)S(1)}, bf16[424,768]{1,0:T(8,128)(2,1)S(1)}, u32[]{:S(2)}, u32[]{:S(2)}) %collective-permute-start.31) | collective-permute-done | bytes 651296 | tf_op jit(solution)/shard_map/ppermute | solution.py:219
  260.2 13.9 %collective-permute-done.33 = bf16[424,768]{1,0:T(8,128)(2,1)S(1)} collective-permute-done((bf16[424,768]{1,0:T(8,128)(2,1)S(1)}, bf16[424,768]{1,0:T(8,128)(2,1)S(1)}, u32[]{:S(2)}, u32[]{:S(2)}) %collective-permute-start.33) | collective-permute-done | bytes 651296 | tf_op jit(solution)/shard_map/ppermute | solution.py:219
  277.4 4.9 %collective-permute-start.35 = (bf16[224,768]{1,0:T(8,128)(2,1)S(1)}, bf16[224,768]{1,0:T(8,128)(2,1)S(1)}, u32[]{:S(2)}, u32[]{:S(2)}) collective-permute-start(bf16[224,768]{1,0:T(8,128)(2,1)S(1)} %get-tuple-element.236), channel_id=1, source_target_pairs={{2,0},{3,1},{4,6},{5,7},{10,8},{11,9},{12,14},{13,15},{18,16},{19,... | collective-permute-start | bytes 1032200 | tf_op jit(solution)/shard_map/ppermute | solution.py:219
  286.3 3.8 %collective-permute-done.35 = bf16[224,768]{1,0:T(8,128)(2,1)S(1)} collective-permute-done((bf16[224,768]{1,0:T(8,128)(2,1)S(1)}, bf16[224,768]{1,0:T(8,128)(2,1)S(1)}, u32[]{:S(2)}, u32[]{:S(2)}) %collective-permute-start.35) | collective-permute-done | bytes 344096 | tf_op jit(solution)/shard_map/ppermute | solution.py:219
  291.4 3.3 collective-permute-done.36
  298.1 19.0 %collective-permute-start.45 = (bf16[824,768]{1,0:T(8,128)(2,1)S(1)}, bf16[824,768]{1,0:T(8,128)(2,1)S(1)}, u32[]{:S(2)}, u32[]{:S(2)}) collective-permute-start(bf16[824,768]{1,0:T(8,128)(2,1)S(1)} %constant_dynamic-update-slice_fusion), channel_id=1, source_target_pairs={{0,4},{1,5},{2,6},{3,7},{4,0},{5,1},{6,2},{7,3},{8,12},{9,13},{10,... | collective-permute-start | bytes 3797000 | tf_op jit(solution)/shard_map/ppermute | solution.py:219
  318.2 4.5 %collective-permute-start.30 = (bf16[512,768]{1,0:T(8,128)(2,1)S(1)}, bf16[512,768]{1,0:T(8,128)(2,1)S(1)}, u32[]{:S(2)}, u32[]{:S(2)}) collective-permute-start(bf16[512,768]{1,0:T(8,128)(2,1)S(1)} %fusion.24), channel_id=1, source_target_pairs={{1,4},{3,6},{4,1},{6,3},{9,12},{11,14},{12,9},{14,11},{17,20},{19,... | collective-permute-start | bytes 2359304 | tf_op jit(solution)/shard_map/ppermute | solution.py:219
  325.0 7.1 %collective-permute-done.30 = bf16[512,768]{1,0:T(8,128)(2,1)S(1)} collective-permute-done((bf16[512,768]{1,0:T(8,128)(2,1)S(1)}, bf16[512,768]{1,0:T(8,128)(2,1)S(1)}, u32[]{:S(2)}, u32[]{:S(2)}) %collective-permute-start.30) | collective-permute-done | bytes 786464 | tf_op jit(solution)/shard_map/ppermute | solution.py:219
  (383 shorter events, 151.2 us)
Async XLA Ops:
  7.3 23.3 %collective-permute-start.3 = (bf16[2,200,768]{2,1,0:T(8,128)(2,1)S(1)}, bf16[2,200,768]{2,1,0:T(8,128)(2,1)}, u32[]{:S(2)}, u32[]{:S(2)}) collective-permute-start(bf16[2,200,768]{2,1,0:T(8,128)(2,1)S(1)} %pad_maximum_fusion.27), channel_id=1, source_target_pairs={{0,2},{1,3},{6,4},{7,5},{8,10},{9,11},{14,12},{15,13},{16,18},{17,... | collective-permute-start | bytes 1843208 | tf_op jit(solution)/shard_map/ppermute | solution.py:219
  11.9 41.4 %collective-permute-start = (bf16[512,768]{1,0:T(8,128)(2,1)S(1)}, bf16[512,768]{1,0:T(8,128)(2,1)}, u32[]{:S(2)}, u32[]{:S(2)}) collective-permute-start(bf16[512,768]{1,0:T(8,128)(2,1)S(1)} %copy-done.33), channel_id=1, source_target_pairs={{1,4},{3,6},{4,1},{6,3},{9,12},{11,14},{12,9},{14,11},{17,20},{19,... | collective-permute-start | bytes 2359304 | tf_op jit(solution)/shard_map/ppermute | solution.py:219
  31.7 20.1 %collective-permute-start.5 = (bf16[2,200,768]{2,1,0:T(8,128)(2,1)S(1)}, bf16[2,200,768]{2,1,0:T(8,128)(2,1)S(1)}, u32[]{:S(2)}, u32[]{:S(2)}) collective-permute-start(bf16[2,200,768]{2,1,0:T(8,128)(2,1)S(1)} %broadcast_select_fusion.4), channel_id=1, source_target_pairs={{0,8},{1,9},{2,10},{3,11},{4,12},{5,13},{6,14},{7,15},{8,0},{9,1},... | collective-permute-start | bytes 1843208 | tf_op jit(solution)/shard_map/ppermute | solution.py:219
  33.0 19.6 %collective-permute-start.6 = (bf16[2,200,768]{2,1,0:T(8,128)(2,1)S(1)}, bf16[2,200,768]{2,1,0:T(8,128)(2,1)S(1)}, u32[]{:S(2)}, u32[]{:S(2)}) collective-permute-start(bf16[2,200,768]{2,1,0:T(8,128)(2,1)S(1)} %broadcast_select_fusion.4), channel_id=1, source_target_pairs={{0,16},{1,17},{2,18},{3,19},{4,20},{5,21},{6,22},{7,23},{8,24},{9,... | collective-permute-start | bytes 1843208 | tf_op jit(solution)/shard_map/ppermute | solution.py:219
  34.2 17.6 %collective-permute-start.7 = (bf16[200,768]{1,0:T(8,128)(2,1)S(1)}, bf16[200,768]{1,0:T(8,128)(2,1)S(1)}, u32[]{:S(2)}, u32[]{:S(2)}) collective-permute-start(bf16[200,768]{1,0:T(8,128)(2,1)S(1)} %bitcast.215), channel_id=1, source_target_pairs={{0,2},{1,3},{2,0},{3,1},{4,6},{5,7},{6,4},{7,5},{8,10},{9,11},{10,... | collective-permute-start | bytes 921608 | tf_op jit(solution)/shard_map/ppermute | solution.py:219
  57.8 11.8 %collective-permute-start.1 = (bf16[512,768]{1,0:T(8,128)(2,1)}, bf16[512,768]{1,0:T(8,128)(2,1)}, u32[]{:S(2)}, u32[]{:S(2)}) collective-permute-start(bf16[512,768]{1,0:T(8,128)(2,1)} %fusion.20), channel_id=1, source_target_pairs={{0,4},{1,5},{2,6},{3,7},{4,0},{5,1},{6,2},{7,3},{8,12},{9,13},{10,... | collective-permute-start | bytes 2359304 | tf_op jit(solution)/shard_map/ppermute | solution.py:219
  74.9 28.6 %collective-permute-start.12 = (bf16[512,768]{1,0:T(8,128)(2,1)}, bf16[512,768]{1,0:T(8,128)(2,1)}, u32[]{:S(2)}, u32[]{:S(2)}) collective-permute-start(bf16[512,768]{1,0:T(8,128)(2,1)} %param.31), channel_id=1, source_target_pairs={{1,4},{3,6},{4,1},{6,3},{9,12},{11,14},{12,9},{14,11},{17,20},{19,... | collective-permute-start | bytes 2359304 | tf_op jit(solution)/shard_map/ppermute | solution.py:219
  80.4 26.2 %collective-permute-start.13 = (bf16[3,200,768]{2,1,0:T(8,128)(2,1)S(1)}, bf16[3,200,768]{2,1,0:T(8,128)(2,1)}, u32[]{:S(2)}, u32[]{:S(2)}) collective-permute-start(bf16[3,200,768]{2,1,0:T(8,128)(2,1)S(1)} %pad_maximum_fusion.26), channel_id=1, source_target_pairs={{0,8},{1,9},{2,10},{3,11},{4,12},{5,13},{6,14},{7,15},{8,0},{9,1},... | collective-permute-start | bytes 2764808 | tf_op jit(solution)/shard_map/ppermute | solution.py:219
  81.8 24.8 %collective-permute-start.14 = (bf16[3,200,768]{2,1,0:T(8,128)(2,1)S(1)}, bf16[3,200,768]{2,1,0:T(8,128)(2,1)}, u32[]{:S(2)}, u32[]{:S(2)}) collective-permute-start(bf16[3,200,768]{2,1,0:T(8,128)(2,1)S(1)} %pad_maximum_fusion.26), channel_id=1, source_target_pairs={{0,16},{1,17},{2,18},{3,19},{4,20},{5,21},{6,22},{7,23},{8,24},{9,... | collective-permute-start | bytes 2764808 | tf_op jit(solution)/shard_map/ppermute | solution.py:219
  111.5 12.8 %collective-permute-start.18 = (bf16[3,104,768]{2,1,0:T(8,128)(2,1)S(1)}, bf16[3,104,768]{2,1,0:T(8,128)(2,1)S(1)}, u32[]{:S(2)}, u32[]{:S(2)}) collective-permute-start(bf16[3,104,768]{2,1,0:T(8,128)(2,1)S(1)} %slice.342), channel_id=1, source_target_pairs={{0,16},{1,17},{2,18},{3,19},{4,20},{5,21},{6,22},{7,23},{8,24},{9,... | collective-permute-start | bytes 1437704 | tf_op jit(solution)/shard_map/ppermute | solution.py:219
  173.9 30.3 %collective-permute-start.25 = (bf16[512,768]{1,0:T(8,128)(2,1)}, bf16[512,768]{1,0:T(8,128)(2,1)}, u32[]{:S(2)}, u32[]{:S(2)}) collective-permute-start(bf16[512,768]{1,0:T(8,128)(2,1)} %get-tuple-element.215), channel_id=1, source_target_pairs={{1,4},{3,6},{4,1},{6,3},{9,12},{11,14},{12,9},{14,11},{17,20},{19,... | collective-permute-start | bytes 2359304 | tf_op jit(solution)/shard_map/ppermute | solution.py:219
  178.3 29.1 %collective-permute-start.23 = (bf16[2,2,200,768]{3,2,1,0:T(8,128)(2,1)}, bf16[2,2,200,768]{3,2,1,0:T(8,128)(2,1)}, u32[]{:S(2)}, u32[]{:S(2)}) collective-permute-start(bf16[2,2,200,768]{3,2,1,0:T(8,128)(2,1)} %get-tuple-element.206), channel_id=1, source_target_pairs={{0,8},{1,9},{2,10},{3,11},{4,12},{5,13},{6,14},{7,15},{8,0},{9,1},... | collective-permute-start | bytes 3686408 | tf_op jit(solution)/shard_map/ppermute | solution.py:219
  178.4 29.3 %collective-permute-start.24 = (bf16[2,2,200,768]{3,2,1,0:T(8,128)(2,1)}, bf16[2,2,200,768]{3,2,1,0:T(8,128)(2,1)}, u32[]{:S(2)}, u32[]{:S(2)}) collective-permute-start(bf16[2,2,200,768]{3,2,1,0:T(8,128)(2,1)} %get-tuple-element.205), channel_id=1, source_target_pairs={{0,16},{1,17},{2,18},{3,19},{4,20},{5,21},{6,22},{7,23},{8,24},{9,... | collective-permute-start | bytes 3686408 | tf_op jit(solution)/shard_map/ppermute | solution.py:219
  210.6 26.4 %collective-permute-start.27 = (bf16[2,200,768]{2,1,0:T(8,128)(2,1)}, bf16[2,200,768]{2,1,0:T(8,128)(2,1)}, u32[]{:S(2)}, u32[]{:S(2)}) collective-permute-start(bf16[2,200,768]{2,1,0:T(8,128)(2,1)} %get-tuple-element.204), channel_id=1, source_target_pairs={{0,8},{1,9},{2,10},{3,11},{4,12},{5,13},{6,14},{7,15},{8,0},{9,1},... | collective-permute-start | bytes 1843208 | tf_op jit(solution)/shard_map/ppermute | solution.py:219
  212.0 25.0 %collective-permute-start.28 = (bf16[2,200,768]{2,1,0:T(8,128)(2,1)}, bf16[2,200,768]{2,1,0:T(8,128)(2,1)}, u32[]{:S(2)}, u32[]{:S(2)}) collective-permute-start(bf16[2,200,768]{2,1,0:T(8,128)(2,1)} %get-tuple-element.203), channel_id=1, source_target_pairs={{0,16},{1,17},{2,18},{3,19},{4,20},{5,21},{6,22},{7,23},{8,24},{9,... | collective-permute-start | bytes 1843208 | tf_op jit(solution)/shard_map/ppermute | solution.py:219
  238.9 35.8 %collective-permute-start.40 = (bf16[2,200,768]{2,1,0:T(8,128)(2,1)S(1)}, bf16[2,200,768]{2,1,0:T(8,128)(2,1)S(1)}, u32[]{:S(2)}, u32[]{:S(2)}) collective-permute-start(bf16[2,200,768]{2,1,0:T(8,128)(2,1)S(1)} %fusion.32), channel_id=1, source_target_pairs={{0,2},{1,3},{2,0},{3,1},{4,6},{5,7},{6,4},{7,5},{8,10},{9,11},{10,... | collective-permute-start | bytes 1843208 | tf_op jit(solution)/shard_map/ppermute | solution.py:219
  243.9 15.9 %collective-permute-start.31 = (bf16[424,768]{1,0:T(8,128)(2,1)S(1)}, bf16[424,768]{1,0:T(8,128)(2,1)S(1)}, u32[]{:S(2)}, u32[]{:S(2)}) collective-permute-start(bf16[424,768]{1,0:T(8,128)(2,1)S(1)} %get-tuple-element.240), channel_id=1, source_target_pairs={{0,8},{1,9},{2,10},{3,11},{4,12},{5,13},{6,14},{7,15},{8,0},{9,1},... | collective-permute-start | bytes 1953800 | tf_op jit(solution)/shard_map/ppermute | solution.py:219
  244.6 15.7 %collective-permute-start.32 = (bf16[424,768]{1,0:T(8,128)(2,1)S(1)}, bf16[424,768]{1,0:T(8,128)(2,1)S(1)}, u32[]{:S(2)}, u32[]{:S(2)}) collective-permute-start(bf16[424,768]{1,0:T(8,128)(2,1)S(1)} %get-tuple-element.239), channel_id=1, source_target_pairs={{0,16},{1,17},{2,18},{3,19},{4,20},{5,21},{6,22},{7,23},{8,24},{9,... | collective-permute-start | bytes 1953800 | tf_op jit(solution)/shard_map/ppermute | solution.py:219
  244.7 29.4 %collective-permute-start.33 = (bf16[424,768]{1,0:T(8,128)(2,1)S(1)}, bf16[424,768]{1,0:T(8,128)(2,1)S(1)}, u32[]{:S(2)}, u32[]{:S(2)}) collective-permute-start(bf16[424,768]{1,0:T(8,128)(2,1)S(1)} %get-tuple-element.238), channel_id=1, source_target_pairs={{0,24},{1,25},{2,26},{3,27},{4,28},{5,29},{6,30},{7,31},{8,16},{9,... | collective-permute-start | bytes 1953800 | tf_op jit(solution)/shard_map/ppermute | solution.py:219
  277.4 12.8 %collective-permute-start.35 = (bf16[224,768]{1,0:T(8,128)(2,1)S(1)}, bf16[224,768]{1,0:T(8,128)(2,1)S(1)}, u32[]{:S(2)}, u32[]{:S(2)}) collective-permute-start(bf16[224,768]{1,0:T(8,128)(2,1)S(1)} %get-tuple-element.236), channel_id=1, source_target_pairs={{2,0},{3,1},{4,6},{5,7},{10,8},{11,9},{12,14},{13,15},{18,16},{19,... | collective-permute-start | bytes 1032200 | tf_op jit(solution)/shard_map/ppermute | solution.py:219
  282.2 12.5 %collective-permute-start.36 = (bf16[224,768]{1,0:T(8,128)(2,1)S(1)}, bf16[224,768]{1,0:T(8,128)(2,1)S(1)}, u32[]{:S(2)}, u32[]{:S(2)}) collective-permute-start(bf16[224,768]{1,0:T(8,128)(2,1)S(1)} %get-tuple-element.237), channel_id=1, source_target_pairs={{2,1},{3,0},{4,7},{5,6},{10,9},{11,8},{12,15},{13,14},{18,17},{19,... | collective-permute-start | bytes 1032200 | tf_op jit(solution)/shard_map/ppermute | solution.py:219
  283.7 33.5 %collective-permute-start.29 = (f32[512,768]{1,0:T(8,128)S(1)}, f32[512,768]{1,0:T(8,128)S(1)}, u32[]{:S(2)}, u32[]{:S(2)}) collective-permute-start(f32[512,768]{1,0:T(8,128)S(1)} %slice.438), channel_id=1, source_target_pairs={{0,4},{1,5},{2,6},{3,7},{4,0},{5,1},{6,2},{7,3},{8,12},{9,13},{10,... | collective-permute-start | bytes 4718600 | tf_op jit(solution)/shard_map/ppermute | solution.py:219
  298.1 35.2 %collective-permute-start.45 = (bf16[824,768]{1,0:T(8,128)(2,1)S(1)}, bf16[824,768]{1,0:T(8,128)(2,1)S(1)}, u32[]{:S(2)}, u32[]{:S(2)}) collective-permute-start(bf16[824,768]{1,0:T(8,128)(2,1)S(1)} %constant_dynamic-update-slice_fusion), channel_id=1, source_target_pairs={{0,4},{1,5},{2,6},{3,7},{4,0},{5,1},{6,2},{7,3},{8,12},{9,13},{10,... | collective-permute-start | bytes 3797000 | tf_op jit(solution)/shard_map/ppermute | solution.py:219
  318.2 13.9 %collective-permute-start.30 = (bf16[512,768]{1,0:T(8,128)(2,1)S(1)}, bf16[512,768]{1,0:T(8,128)(2,1)S(1)}, u32[]{:S(2)}, u32[]{:S(2)}) collective-permute-start(bf16[512,768]{1,0:T(8,128)(2,1)S(1)} %fusion.24), channel_id=1, source_target_pairs={{1,4},{3,6},{4,1},{6,3},{9,12},{11,14},{12,9},{14,11},{17,20},{19,... | collective-permute-start | bytes 2359304 | tf_op jit(solution)/shard_map/ppermute | solution.py:219
  (81 other events, 504.9 us)
where the time goes:
time: 356 us; the launch traced here: 349 us
  starting transfers between devices  83.2 us (23%)
  waiting for transfers between devices  78.6 us (22%)
  other arithmetic  57.2 us (16%)
  matrix products  46.8 us (13%)
  Pallas kernels  46.1 us (13%)
  local copies, waits for them, and re-layouts  31.7 us (9%)
  between operations  5.34 us (2%)
    ppermute x47, starting transfers between devices, permute(): return lax.ppermute(array, JOINT, pairs)  83.2 us
    ppermute x47, waiting for transfers between devices, permute(): return lax.ppermute(array, JOINT, pairs)  78.6 us
    pallas_call x2, Pallas kernels, attend_back(): pl.pallas_call(attend_back_kernel, grid=(count,), in_specs=[pl.BlockSpec(...  28 us
    dot_general x3, matrix products, nt(): lax.dot_general(a, b, (((1,), (1,)), ((), ())), preferred_element_type=F32)  19.1 us
    pallas_call x1, Pallas kernels, attend(): pl.pallas_call(attend_kernel, grid=(n,), in_specs=[pl.BlockSpec((LEN, 2 *...  18.1 us
    dot_general x5, matrix products, tn(): lax.dot_general(a, b, (((0,), (0,)), ((), ())), preferred_element_type=F32)  17.1 us
    unnamed x124, local copies, waits for them, and re-layouts  13.3 us
    dot_general x5, matrix products, nn(): lax.dot_general(a, b, (((1,), (0,)), ((), ())), preferred_element_type=F32)  10.6 us
  transfers between devices with their start and end apart: 47, of which 18 were waited for; matrix products, arithmetic and copies ran while one was open for 19% of the time, Pallas kernels for 13%

commit v1 on v0

--- a/solution.py
+++ b/solution.py
@@ -73,6 +73,15 @@
         lse_ref[0, :, rows] = jnp.transpose(jnp.concatenate(logs, axis=1))
 
 
+def attention_cost(pairs_of_heads, products):
+    scores = 2 * pairs_of_heads * LEN * LEN
+    return pl.CostEstimate(
+        flops=2 * 4 * HEAD * products * scores,
+        transcendentals=scores,
+        bytes_accessed=8 * pairs_of_heads * LEN * HEAD * products,
+    )
+
+
 def attend(proj, seg_col, seg_row, pairs_of_heads):
     n = pairs_of_heads
     return pl.pallas_call(
@@ -101,7 +110,10 @@
     q_ref,
     k_ref,
     v_ref,
-    rows_ref,
+    go_ref,
+    go_other_ref,
+    x_ref,
+    x_other_ref,
     back_ref,
     ctx_ref,
     lse_ref,
@@ -109,24 +121,29 @@
     seg_row_ref,
     limit_ref,
     grad_ref,
+    pack_ref,
     sum_ref,
     acc_ref,
     grads_ref,
+    quant_ref,
     inner_ref,
 ):
     low = lax.broadcasted_iota(jnp.int32, (BLOCK, 2 * HEAD), 1) < HEAD
-    for block in range(LEN // BLOCK):
-        rows = pl.ds(block * BLOCK, BLOCK)
-        context = ctx_ref[rows, :]
-        grad = nt(rows_ref[rows, :], back_ref[...])
-        grad = jnp.where(jnp.abs(context) <= limit_ref[0], grad, 0.0).astype(BF16)
-        grads_ref[rows, :] = grad
-        both = grad.astype(F32) * context
-        inner = [
-            jnp.sum(jnp.where(own, both, 0.0), axis=1, keepdims=True)
-            for own in (low, jnp.logical_not(low))
-        ]
-        inner_ref[:, rows] = jnp.transpose(jnp.concatenate(inner, axis=1))
+    limit = limit_ref[0]
+    for half, rows_ref in enumerate((go_ref, go_other_ref)):
+        for block in range(HALF // BLOCK):
+            rows = pl.ds(half * HALF + block * BLOCK, BLOCK)
+            context = ctx_ref[rows, :]
+            quant_ref[rows, :] = jnp.clip(context, -limit, limit).astype(BF16)
+            grad = nt(rows_ref[pl.ds(block * BLOCK, BLOCK), :], back_ref[...])
+            grad = jnp.where(jnp.abs(context) <= limit, grad, 0.0).astype(BF16)
+            grads_ref[rows, :] = grad
+            both = grad.astype(F32) * context
+            inner = [
+                jnp.sum(jnp.where(own, both, 0.0), axis=1, keepdims=True)
+                for own in (low, jnp.logical_not(low))
+            ]
+            inner_ref[:, rows] = jnp.transpose(jnp.concatenate(inner, axis=1))
     queries = q_ref[...]
     grads = grads_ref[...]
     value_sum = jnp.zeros((1, 2 * HEAD), F32)
@@ -161,40 +178,124 @@
     grad_ref[:, : 2 * HEAD] = grad_query.astype(BF16)
     sum_ref[0, 0:1, :] = jnp.sum(grad_query, axis=0, keepdims=True)
     sum_ref[0, 1:2, :] = value_sum
-
-
-def attend_back(proj, grad_rows, w_back, context, lse, seg_col, seg_row, limit, first, count):
+    chunk = HEAD // 4
+    sides = ((slice(0, HALF), x_ref, go_ref), (slice(HALF, LEN), x_other_ref, go_other_ref))
+    for kind in range(4):
+        lanes = slice(2 * kind * HEAD, 2 * (kind + 1) * HEAD)
+        total = None
+        for rows, x_side, go_side in sides:
+            if kind < 3:
+                part = tn(grad_ref[rows, lanes], x_side[...])
+            else:
+                part = tn(quant_ref[rows, :], go_side[...])
+            total = part if total is None else total + part
+        total = total.astype(BF16)
+        for head in range(2):
+            for j in range(4):
+                at = head * HEAD + j * chunk
+                into = (head * 4 + kind) * chunk
+                pack_ref[j, into : into + chunk, :] = total[at : at + chunk, :]
+
+
+def attend_back(
+    first, n, before, proj, go, go_other, x, x_other, w_back, context, lse, seg_col, seg_row, limit
+):
     width = w_back.shape[1]
+    earlier = [] if before is None else [before]
+
+    def body(*refs):
+        attend_back_kernel(*refs[:13], *refs[13 + len(earlier) :])
+
+    def whole(array):
+        return pl.BlockSpec(array.shape, lambda i: (0,) * array.ndim)
+
     return pl.pallas_call(
-        attend_back_kernel,
-        grid=(count,),
+        body,
+        grid=(n,),
         in_specs=[
             pl.BlockSpec((LEN, 2 * HEAD), lambda i: (0, 3 * (first + i))),
             pl.BlockSpec((LEN, 2 * HEAD), lambda i: (0, 3 * (first + i) + 1)),
             pl.BlockSpec((LEN, 2 * HEAD), lambda i: (0, 3 * (first + i) + 2)),
-            pl.BlockSpec((LEN, width), lambda i: (0, 0)),
+            *[whole(array) for array in (go, go_other, x, x_other)],
             pl.BlockSpec((2 * HEAD, width), lambda i: (first + i, 0)),
             pl.BlockSpec((LEN, 2 * HEAD), lambda i: (0, first + i)),
             pl.BlockSpec((1, 2, LEN), lambda i: (first + i, 0, 0)),
-            pl.BlockSpec((LEN, 1), lambda i: (0, 0)),
-            pl.BlockSpec((1, LEN), lambda i: (0, 0)),
+            whole(seg_col),
+            whole(seg_row),
             pl.BlockSpec(memory_space=pltpu.SMEM),
+            *[pl.BlockSpec(memory_space=pl.ANY) for _ in earlier],
         ],
         out_specs=[
             pl.BlockSpec((LEN, 6 * HEAD), lambda i: (0, i)),
+            pl.BlockSpec((4, 2 * HEAD, width), lambda i: (0, first + i, 0)),
             pl.BlockSpec((1, 2, 2 * HEAD), lambda i: (i, 0, 0)),
         ],
         out_shape=[
-            jax.ShapeDtypeStruct((LEN, count * 6 * HEAD), BF16),
-            jax.ShapeDtypeStruct((count, 2, 2 * HEAD), F32),
+            jax.ShapeDtypeStruct((LEN, n * 6 * HEAD), BF16),
+            jax.ShapeDtypeStruct((4, *w_back.shape), BF16),
+            jax.ShapeDtypeStruct((n, 2, 2 * HEAD), F32),
         ],
         scratch_shapes=[
             pltpu.VMEM((LEN, 2 * HEAD), F32),
             pltpu.VMEM((LEN, 2 * HEAD), BF16),
+            pltpu.VMEM((LEN, 2 * HEAD), BF16),
             pltpu.VMEM((2, LEN), F32),
         ],
+        cost_estimate=attention_cost(n, 9) if first else None,
+        input_output_aliases={13: 1} if earlier else {},
         name="attend_back",
-    )(proj, proj, proj, grad_rows, w_back, context, lse, seg_col, seg_row, limit)
+    )(
+        *(proj, proj, proj, go, go_other, x, x_other, w_back, context, lse),
+        *(seg_col, seg_row, limit, *earlier),
+    )
+
+
+def unpack_kernel(where_ref, own_ref, other_ref, qkv_ref, out_ref):
+    inside, plane = where_ref[0], where_ref[1]
+    kind = pl.program_id(0)
+    chunk = HEAD // 4
+    tall = own_ref.shape[0] // 4
+    heads = tall // HEAD
+
+    def rows_of(ref):
+        parts = []
+        for head in range(heads):
+            for j in range(4):
+                at = (j ^ plane) * tall + head * HEAD + kind * chunk
+                parts.append(ref[pl.ds(pl.multiple_of(at, chunk), chunk), :])
+        return jnp.concatenate(parts, axis=0).astype(F32)
+
+    for flag, ref in ((1, own_ref), (0, other_ref)):
+
+        @pl.when(jnp.logical_and(inside == flag, kind < 3))
+        def _(ref=ref):
+            qkv_ref[0] = rows_of(ref)
+
+        @pl.when(jnp.logical_and(inside == flag, kind == 3))
+        def _(ref=ref):
+            out_ref[...] = rows_of(ref)
+
+
+def unpack(inside, plane, own, other, tall):
+    width = own.shape[1]
+    return pl.pallas_call(
+        unpack_kernel,
+        grid=(4,),
+        in_specs=[
+            pl.BlockSpec(memory_space=pltpu.SMEM),
+            pl.BlockSpec((4 * tall, width), lambda i: (0, 0)),
+            pl.BlockSpec((4 * tall, width), lambda i: (0, 0)),
+        ],
+        out_specs=[
+            pl.BlockSpec((1, tall, width), lambda i: (jnp.minimum(i, 2), 0, 0)),
+            pl.BlockSpec((tall, width), lambda i: (0, 0)),
+        ],
+        out_shape=[
+            jax.ShapeDtypeStruct((3, tall, width), F32),
+            jax.ShapeDtypeStruct((tall, width), F32),
+        ],
+        name="unpack",
+    )(jnp.stack([inside.astype(jnp.int32), plane]), own, other)
 
 
 class Links:
@@ -269,7 +370,16 @@
         return self.permute(array, lambda e, c, z: (e, c, z ^ 1) if z // 2 == c else None)
 
     def pair_out(self, array):
-        return self.permute(array, lambda e, c, z: (e, c, z ^ 2) if z // 2 == c else None)
+        def far(step):
+            return lambda e, c, z: (e, c, z ^ step) if z // 2 == c else None
+
+        return [self.permute(array, far(step)) for step in (2, 3, 1)]
+
+    def pair_of(self, mine, arrived):
+        same, cross, near = arrived
+        a = jnp.where(self.inside, mine, same)
+        b = jnp.where(self.inside, near, cross)
+        return self.even_first(a, b)
 
     def pair_back(self, array):
         return self.permute(array, lambda e, c, z: (e, c, z ^ 2) if z // 2 != c else None)
@@ -281,6 +391,12 @@
         other = self.other_half(mine)
         first = self.half == 0
         return jnp.stack([jnp.where(first, mine, other), jnp.where(first, other, mine)])
+
+    def natural(self, array):
+        swapped = array[..., jnp.array([1, 0, 3, 2]), :]
+        array = jnp.where(self.plane % 2 == 1, swapped, array)
+        swapped = array[..., jnp.array([2, 3, 0, 1]), :]
+        return jnp.where(self.plane // 2 == 1, swapped, array)
 
     def even_first(self, mine, other):
         return jnp.stack([jnp.where(self.even, mine, other), jnp.where(self.even, other, mine)])
@@ -363,8 +479,7 @@
     attn_pack = jnp.concatenate([rows, tail], axis=1)
     if links.square:
         attn_mine = lax.dynamic_index_in_dim(attn_pack, links.plane, 0, False)
-        attn_next = links.pair_near(attn_mine)
-    x_home = links.at_home(layer_input, links.rows_home(layer_input))
+        attn_in = links.pair_out(attn_mine)
     seg_rows = segments.reshape(2, LEN)
     seg_mine = lax.dynamic_index_in_dim(seg_rows, links.depth // 2, 0, False).reshape(8, LEN // 8)
     seg_next = links.other_half(seg_mine)
@@ -386,27 +501,29 @@
         ffn_own = jnp.stack(
             [lax.dynamic_index_in_dim(ffn_half, j ^ links.plane, 0, False) for j in ORDER]
         )
-        ffn_one = links.along(ffn_own[0], 1)
-        attn_both = links.even_first(attn_mine, attn_next)
-        attn_far = links.pair_out(attn_both)
-        attn_far, ffn_one, ffn_mine = sync(attn_far, ffn_one, ffn_own[0])
-        attn_both = jnp.where(links.inside, attn_both, attn_far)
+        attn_in, ffn_mine, x_home = sync(attn_in, ffn_own[0], layer_input)
+        attn_both = links.pair_of(attn_mine, attn_in)
         attn_near = links.spread_near(attn_both)
-        ffn_two = links.along(ffn_mine, 2)
-        attn_near, ffn_two, ffn_mine = sync(attn_near, ffn_two, ffn_mine)
-        ffn_three = links.along(ffn_mine, 3)
+        x_home = links.rows_home(x_home)
+        ffn_in = [links.along(ffn_mine, 2)]
+        attn_near, ffn_in, ffn_mine = sync(attn_near, ffn_in, ffn_mine)
         attn_full = links.spread_far(attn_both, attn_near)
-        attn_full, ffn_three = sync(attn_full, ffn_three)
+        ffn_in.append(links.along(ffn_mine, 3))
+        attn_full, ffn_in, ffn_mine, x_home = sync(attn_full, ffn_in, ffn_mine, x_home)
+        ffn_in.append(links.along(ffn_mine, 1))
         attn_full = jnp.stack(attn_full)
-        ffn_in = jnp.stack([ffn_one, ffn_two, ffn_three])
+        ffn_in = jnp.stack([ffn_in[2], ffn_in[0], ffn_in[1]])
     else:
         attn_full = lax.all_gather(attn_pack, "tensor", axis=0, tiled=False)
         attn_full = lax.dynamic_slice_in_dim(attn_full, 2 * links.half, 2, 0).swapaxes(0, 1)
         ffn_in = lax.all_gather(ffn_half, "tensor", axis=0, tiled=False)
+        x_home = links.rows_home(layer_input)
+    x_home = links.at_home(layer_input, x_home)
 
     x_full = x_home.astype(F32)
     x_quant = jnp.clip(x_full, -act_scale[0], act_scale[0]).astype(BF16)
-    x_rows = jnp.concatenate([x_quant, links.other_half(x_quant)])
+    x_other = links.other_half(x_quant)
+    x_rows = jnp.concatenate([x_quant, x_other])
 
     weights = attn_full[:, :, : per + more].reshape(4, 2, 4, heads, chunk, width)
     weights = weights.transpose(2, 1, 3, 0, 4, 5).reshape(4, heads, 2 * HEAD, width)
@@ -426,16 +543,16 @@
     context, upstream = sync(context, upstream)
     upstream = links.at_home(out_grad, upstream).astype(F32)
     ctx_quant = jnp.clip(context, -act_scale[1], act_scale[1]).astype(BF16)
-    attn_part = nn(ctx_quant, w_back)
+    attn_part, attn_sent = nn(ctx_quant[:HALF], w_back), nn(ctx_quant[HALF:], w_back)
     if links.square:
-        attn_part, ffn_near = sync(attn_part, ffn_near)
+        attn_part, attn_sent, ffn_near = sync(attn_part, attn_sent, ffn_near)
         pieces = links.spread_far(ffn_in, ffn_near)
         ffn_full = jnp.stack(
             [jnp.concatenate([ffn_own[i][None], pieces[j]]) for i, j in enumerate(ORDER)]
         )
     else:
         ffn_full = ffn_in.swapaxes(0, 1)
-    attn_out = attn_part[:HALF] + links.other_half(attn_part[HALF:]) + b_out.astype(F32)
+    attn_out = attn_part + links.other_half(attn_sent) + b_out.astype(F32)
     hidden, normed_attn, inverse_attn = norm_forward(
         x_full + attn_out, gain_first, shift_attn.astype(F32)
     )
@@ -451,26 +568,22 @@
     slope = normal_cdf + pre_act * jnp.exp(-0.5 * pre_act * pre_act) / math.sqrt(2.0 * math.pi)
     slope = jnp.where(jnp.abs(activated) <= act_scale[3], slope, 0.0)
     act_quant = jnp.clip(activated, -act_scale[3], act_scale[3]).astype(BF16)
-    ffn_part = nn(act_quant, w_low)
-    ffn_out = ffn_part[:HALF] + links.other_half(ffn_part[HALF:])
+    ffn_sent, ffn_part = nn(act_quant[HALF:], w_low), nn(act_quant[:HALF], w_low)
+    ffn_out = ffn_part + links.other_half(ffn_sent)
     final, normed_ffn, inverse_ffn = norm_forward(
         hidden + ffn_out + b_down.astype(F32), gain_second, shift_ffn.astype(F32)
     )
     final = final.astype(BF16)
     layer_output = links.rows_home(final)
-    maxima = jnp.stack(
-        [
-            jnp.max(jnp.abs(x_full)),
-            jnp.max(jnp.abs(context)),
-            jnp.max(jnp.abs(hidden)),
-            jnp.max(jnp.max(jnp.abs(activated), axis=0)),
-        ]
-    )
-
-    grad_gain_ffn = jnp.sum(upstream * normed_ffn, axis=0)
-    grad_shift_ffn = jnp.sum(upstream, axis=0)
+    lanes = lax.broadcasted_iota(jnp.int32, (1, width), 1)
+    maxima = jnp.zeros((1, width), F32)
+    for at, array in enumerate((x_full, context, hidden, activated)):
+        maxima = jnp.where(lanes == at, jnp.max(jnp.abs(array)), maxima)
+
+    grad_gain_ffn = jnp.sum(upstream * normed_ffn, axis=0, keepdims=True)
+    grad_shift_ffn = jnp.sum(upstream, axis=0, keepdims=True)
     grad_second = norm_backward(upstream, normed_ffn, inverse_ffn, gain_second)
-    grad_b_down = jnp.sum(grad_second, axis=0)
+    grad_b_down = jnp.sum(grad_second, axis=0, keepdims=True)
     grad_final = grad_second.astype(BF16)
     grad_rows = jnp.concatenate([grad_final, links.other_half(grad_final)])
     down = tn(act_quant, grad_rows).astype(BF16).reshape(4, 4, quarter, width)
@@ -487,73 +600,74 @@
         ffn_grads, grad_pre_b = sync(ffn_grads, grad_pre_b)
         ffn_x = links.across(ffn_grads[1:3, :2], 1)
         ffn_y = links.across(ffn_grads[2:4, 2:], 2)
-    hid_part = nn(grad_pre_b, w_up)
-    grad_hid = hid_part[:HALF] + links.other_half(hid_part[HALF:])
+    hid_sent, hid_part = nn(grad_pre_b[HALF:], w_up), nn(grad_pre_b[:HALF], w_up)
+    grad_hid = hid_part + links.other_half(hid_sent)
 
     grad_hidden = grad_second + grad_hid * (jnp.abs(hidden) <= act_scale[2]).astype(F32)
-    grad_gain_attn = jnp.sum(grad_hidden * normed_attn, axis=0)
-    grad_shift_attn = jnp.sum(grad_hidden, axis=0)
+    grad_gain_attn = jnp.sum(grad_hidden * normed_attn, axis=0, keepdims=True)
+    grad_shift_attn = jnp.sum(grad_hidden, axis=0, keepdims=True)
     grad_first = norm_backward(grad_hidden, normed_attn, inverse_attn, gain_first)
-    grad_b_out = jnp.sum(grad_first, axis=0)
+    grad_b_out = jnp.sum(grad_first, axis=0, keepdims=True)
     grad_attn = grad_first.astype(BF16)
-    grad_attn_rows = jnp.concatenate([grad_attn, links.other_half(grad_attn)])
+    go_other = links.other_half(grad_attn)
     sums = [grad_b_out, grad_gain_attn, grad_shift_attn, grad_b_down, grad_gain_ffn, grad_shift_ffn]
-    sums = jnp.stack([*sums, jnp.pad(maxima, (0, width - 4)), jnp.zeros(width)])
-
-    out = tn(ctx_quant, grad_attn_rows).astype(BF16).reshape(2, heads, 4, chunk, width)
-    out = out.transpose(2, 0, 1, 3, 4).reshape(4, 2, more, width)
-    limit = act_scale[1:2]
-
-    def back(first, count):
+    sums = jnp.concatenate([*sums, maxima, jnp.zeros((1, width), F32)])
+
+    def back(first, count, before):
         return attend_back(
-            proj, grad_attn_rows, w_back, context, lse, seg_col, seg_row, limit, first, count
+            first,
+            count,
+            before,
+            proj,
+            grad_attn,
+            go_other,
+            x_quant,
+            x_other,
+            w_back,
+            context,
+            lse,
+            seg_col,
+            seg_row,
+            act_scale[1:2],
         )
 
+    def bias_rows(pairs):
+        return pairs.reshape(heads, 2, 2, 4, chunk).swapaxes(0, 1)
+
     if links.square:
-        early, early_sums = back(0, 1)
-        sums = merge(sums, links.other_half(sums))
-        early, grad_attn_rows, ffn_x, ffn_y, layer_output, sums = sync(
-            early, grad_attn_rows, ffn_x, ffn_y, layer_output, sums
+        tall = 2 * heads * HEAD // 2
+        many = heads - 1
+        early, grad_w, early_b = back(0, many, None)
+        early, go_other, ffn_x, ffn_y, layer_output = sync(
+            early, go_other, ffn_x, ffn_y, layer_output
         )
         low = [ffn_grads[0, :2] + ffn_x[0].astype(F32), ffn_grads[3, :2] + ffn_x[1].astype(F32)]
         high = [ffn_grads[0, 2:] + ffn_y[1].astype(F32), ffn_grads[1, 2:] + ffn_y[0].astype(F32)]
-        ffn_y = links.across(low[1].astype(BF16), 2)
-        ffn_x = links.across(high[1].astype(BF16), 1)
-        early_w = tn(early, x_rows).astype(BF16)
-        late, late_sums = back(1, heads - 1)
-        late, ffn_x, ffn_y = sync(late, ffn_x, ffn_y)
+        ffn_y, ffn_x = low[1].astype(BF16), high[1].astype(BF16)
+        go_other, ffn_x, ffn_y = sync(go_other, ffn_x, ffn_y)
+        ffn_y, ffn_x = links.across(ffn_y, 2), links.across(ffn_x, 1)
+        late, grad_w, late_b = back(many, 1, grad_w)
+        late, grad_w, late_b, ffn_x, ffn_y = sync(late, grad_w, late_b, ffn_x, ffn_y)
+        sums = merge(sums, links.other_half(sums))
+        bias_sums = links.natural(bias_rows(jnp.concatenate([early_b, late_b])))
+        sums = jnp.concatenate([sums[:7], bias_sums.reshape(1, width)])
+        sums_sent = exact_parts(sums)
         ffn_low = low[0] + ffn_y.astype(F32)
         ffn_in = links.along((high[0] + ffn_x.astype(F32)).astype(BF16), 2)
-        grad_w = jnp.concatenate([early_w, tn(late, x_rows).astype(BF16)])
-        proj_sums = jnp.concatenate([early_sums, late_sums])
-    else:
-        late, proj_sums = back(0, heads)
-        grad_w = tn(late, x_rows).astype(BF16)
-    grad_w = grad_w.reshape(heads, 3, 2, 4, chunk, width).transpose(1, 0, 2, 3, 4, 5)
-    grad_w = grad_w.reshape(3, 2, heads, 4, chunk, width).transpose(3, 1, 0, 2, 4, 5)
-    grad_w = grad_w.reshape(4, 2, per, width)
-    grad_b = jnp.stack([proj_sums[:, 0], proj_sums[:, 1]]).reshape(2, 2, heads, 4, chunk)
-    grad_b = grad_b.transpose(3, 1, 0, 2, 4).reshape(4, 2, 1, 2 * more).astype(BF16)
-    grad_b = jnp.pad(grad_b, ((0, 0), (0, 0), (0, 7), (0, width - 2 * more)))
-    grad_w = jnp.concatenate([grad_w, out, grad_b], axis=2)
-    if links.square:
-        grad_w, late = sync(grad_w, late)
-        tall = grad_w.shape[2]
-        grad_w = grad_w.reshape(4, 2 * tall, width)
-        sums_sent = exact_parts(sums)
         proj_in = [
             links.across(jnp.concatenate([grad_w[step], sums_sent]), step) for step in (1, 2, 3)
         ]
-        x_part = nn(early, w_proj[: 6 * HEAD]) + nn(late, w_proj[6 * HEAD :])
+        grad_proj, ffn_low = sync(jnp.concatenate([early, late], axis=1), ffn_low)
     else:
-        x_part = nn(late, w_proj)
-    grad_x = x_part[:HALF] + links.other_half(x_part[HALF:])
+        grad_proj, grad_w, bias_sums = back(0, heads, None)
+        bias_sums = bias_rows(bias_sums)
+    x_sent, x_part = nn(grad_proj[HALF:], w_proj), nn(grad_proj[:HALF], w_proj)
+    grad_x = x_part + links.other_half(x_sent)
     input_grad = grad_first + grad_x * (jnp.abs(x_full) <= act_scale[0]).astype(F32)
-    input_grad = input_grad.astype(BF16)
-    input_grad = links.at_home(input_grad, links.rows_home(input_grad)).astype(F32)
+    input_part = input_grad.astype(BF16)
 
     if links.square:
-        proj_in, x_part = sync(proj_in, x_part)
+        proj_in, input_part = sync(proj_in, input_part)
         total = grad_w[0].astype(F32)
         for part in proj_in:
             total = total + part[: 2 * tall].astype(F32)
@@ -573,40 +687,45 @@
         for part in proj_in:
             mine = mine + part[:tall].astype(F32)
             sums = merge(sums, exact_sum(part[tall:]))
-        proj_all = links.spread(mine.astype(BF16), lambda c, z: z // 2 == c)
+        mine, input_part = sync(mine.astype(BF16), input_part)
+        proj_all = links.spread(mine, lambda c, z: z // 2 == c)
         ffn_mine = (ffn_low[0] + ffn_in.astype(F32)).astype(BF16)
         ffn_all = links.spread(ffn_mine)
         proj_all, ffn_all = sync(proj_all, ffn_all)
         proj_all = jnp.concatenate([*proj_all, exact_parts(sums)])
-        proj_all = jnp.where(links.inside, proj_all, links.other_half(proj_all))
+        proj_other = links.other_half(proj_all)
+        sums = exact_sum(jnp.where(links.inside, proj_all[4 * tall :], proj_other[4 * tall :]))
+        grad_qkv, grad_out = unpack(links.inside, links.plane, proj_all, proj_other, tall)
+        grad_qkv = jnp.swapaxes(grad_qkv, 1, 2)
         ffn_all = links.halves_in_order(links.in_order(ffn_all))
-        sums = exact_sum(proj_all[4 * tall :])
-        proj_grads = links.in_order(list(proj_all[: 4 * tall].reshape(4, tall, width)))
     else:
         ffn_all = plain_all(links, ffn_grads.swapaxes(0, 1))
-        proj_grads = plain_pair(links, grad_w)
-        sums = jnp.concatenate([lax.psum(sums[:6], JOINT), lax.pmax(sums[6:], JOINT)])
+        grads = plain_pair(links, grad_w.reshape(4, 2, -1, width))
+        grads = grads.reshape(4, heads, 4, chunk, width).transpose(2, 1, 0, 3, 4)
+        grads = grads.reshape(4, local, width)
+        grad_qkv, grad_out = jnp.swapaxes(grads[:3], 1, 2), grads[3]
+        sums = jnp.concatenate([lax.psum(sums[:6], JOINT), lax.pmax(sums[6:7], JOINT)])
+        both = jnp.zeros((4, 2, local), F32)
+        both = lax.dynamic_update_slice_in_dim(
+            both, bias_sums.reshape(2, 2, local).swapaxes(0, 1), 2 * links.half, 0
+        )
+        both = lax.psum(both, JOINT)
+        both = lax.dynamic_slice_in_dim(both, links.depth - links.depth % 2, 2, 0)
+        sums = jnp.concatenate([sums, both.swapaxes(0, 1).reshape(1, width)])
+    input_grad = links.at_home(input_part, links.rows_home(input_part)).astype(F32)
     maxima = sums[6, :4]
     new_scale = DECAY * act_scale + (1.0 - DECAY) * maxima
 
     up_grads, down_grads = ffn_all[:, :, :quarter], ffn_all[:, :, quarter : 2 * quarter]
-    out_grads = proj_grads[:, per : per + more]
-    grad_qkv = proj_grads[:, :per].reshape(4, 3, heads, chunk, width)
-    grad_qkv = grad_qkv.transpose(1, 4, 2, 0, 3).reshape(3, width, local).astype(F32)
-    grad_bias_qv = (
-        proj_grads[:, per + more, : 2 * more]
-        .reshape(4, 2, heads, chunk)
-        .transpose(1, 2, 0, 3)
-        .reshape(2, local)
-        .astype(F32)
-    )
-    grad_out = out_grads.reshape(4, heads, chunk, width).transpose(1, 0, 2, 3)
+    grad_bias_qv = lax.dynamic_index_in_dim(
+        sums[7].reshape(2, 2, local), links.depth % 2, 1, False
+    )
     return (
         links.at_home(final, layer_output),
         input_grad,
         grad_qkv,
         grad_bias_qv,
-        grad_out.reshape(local, width).astype(F32),
+        grad_out,
         sums[0],
         sums[1],
         sums[2],

time: 356 us -> 349 us (0.980)
  starting transfers between devices: 83.2 us -> 68.1 us
  waiting for transfers between devices: 78.6 us -> 88.2 us
  Pallas kernels: 46.1 us -> 53.7 us
  other arithmetic: 57.2 us -> 52.8 us
    ppermute x47 -> x48, starting transfers between devices: 83.2 us -> 68.1 us  [permute(): return lax.ppermute(array, JOINT, pairs)]
    ppermute x47 -> x48, waiting for transfers between devices: 78.6 us -> 88.2 us  [permute(): return lax.ppermute(array, JOINT, pairs)]
    dot_general x5 -> x2, matrix products: 17.1 us -> 9.47 us  [tn(): lax.dot_general(a, b, (((0,), (0,)), ((), ())), preferred_element_type=F32)]
    pallas_call x2 -> x3, Pallas kernels: 28 us -> 35.6 us  [the longest x2 31.8 us: attend_back(): pl.pallas_call(body, grid=(n,), in_specs=[pl.BlockSpec((LEN, 2 * HEAD), l...]
    dot_general x5 -> x8, matrix products: 10.6 us -> 16.3 us  [nn(): lax.dot_general(a, b, (((1,), (0,)), ((), ())), preferred_element_type=F32)]
    slice x10 -> x0, local copies, waits for them, and re-layouts: 3.82 us -> none  [the longest x3 2.02 us: on_device(): x_part = nn(early, w_proj[:6 * HEAD]) + nn(late, w_proj[6 * HEAD:])]
    unnamed x124 -> x137, local copies, waits for them, and re-layouts: 13.3 us -> 14.9 us
  transfers between devices with their start and end apart: 47 -> 48, of which waited for: 18 -> 20; matrix products, arithmetic and copies ran while one was open for 19% -> 20% of each run, Pallas kernels for 13% -> 16%
where the time goes in v1:
time: 349 us; the launch traced here: 343 us
  waiting for transfers between devices  88.2 us (25%)
  starting transfers between devices  68.1 us (20%)
  Pallas kernels  53.7 us (15%)
  other arithmetic  52.8 us (15%)
  matrix products  44.2 us (13%)
  local copies, waits for them, and re-layouts  30.6 us (9%)
  between operations  4.95 us (1%)
    ppermute x48, waiting for transfers between devices, permute(): return lax.ppermute(array, JOINT, pairs)  88.2 us
    ppermute x48, starting transfers between devices, permute(): return lax.ppermute(array, JOINT, pairs)  68.1 us
    pallas_call x2, Pallas kernels, attend_back(): pl.pallas_call(body, grid=(n,), in_specs=[pl.BlockSpec((LEN, 2 * HEAD), l...  31.8 us
    dot_general x3, matrix products, nt(): lax.dot_general(a, b, (((1,), (1,)), ((), ())), preferred_element_type=F32)  18.5 us
    pallas_call x1, Pallas kernels, attend(): pl.pallas_call(attend_kernel, grid=(n,), in_specs=[pl.BlockSpec((LEN, 2 *...  18.1 us
    dot_general x8, matrix products, nn(): lax.dot_general(a, b, (((1,), (0,)), ((), ())), preferred_element_type=F32)  16.3 us
    unnamed x137, local copies, waits for them, and re-layouts  14.9 us
    dot_general x2, matrix products, tn(): lax.dot_general(a, b, (((0,), (0,)), ((), ())), preferred_element_type=F32)  9.47 us
  transfers between devices with their start and end apart: 48, of which 20 were waited for; matrix products, arithmetic and copies ran while one was open for 20% of the time, Pallas kernels for 16%

profile of v1, /device:TPU:1, one launch (start us, length us, event | category | flops | bytes accessed | tf_op | source)
XLA Modules:
  0.0 342.6 jit_solution(10573634035356809241)
XLA Ops:
  9.6 7.5 %collective-permute-done.1 = bf16[200,768]{1,0:T(8,128)(2,1)} collective-permute-done((bf16[200,768]{1,0:T(8,128)(2,1)S(1)}, bf16[200,768]{1,0:T(8,128)(2,1)}, u32[]{:S(2)}, u32[]{:S(2)}) %collective-permute-start.1) | collective-permute-done | bytes 307232 | tf_op jit(solution)/shard_map/ppermute | solution.py:320
  17.2 7.9 %collective-permute-done = bf16[200,768]{1,0:T(8,128)(2,1)} collective-permute-done((bf16[200,768]{1,0:T(8,128)(2,1)S(1)}, bf16[200,768]{1,0:T(8,128)(2,1)}, u32[]{:S(2)}, u32[]{:S(2)}) %collective-permute-start) | collective-permute-done | bytes 307232 | tf_op jit(solution)/shard_map/ppermute | solution.py:320
  33.8 10.4 %collective-permute-done.5 = bf16[200,768]{1,0:T(8,128)(2,1)S(1)} collective-permute-done((bf16[200,768]{1,0:T(8,128)(2,1)S(1)}, bf16[200,768]{1,0:T(8,128)(2,1)S(1)}, u32[]{:S(2)}, u32[]{:S(2)}) %collective-permute-start.5) | collective-permute-done | bytes 307232 | tf_op jit(solution)/shard_map/ppermute | solution.py:320
  47.4 3.9 %collective-permute-done.6 = bf16[2,96,768]{2,1,0:T(8,128)(2,1)} collective-permute-done((bf16[2,96,768]{2,1,0:T(8,128)(2,1)S(1)}, bf16[2,96,768]{2,1,0:T(8,128)(2,1)}, u32[]{:S(2)}, u32[]{:S(2)}) %collective-permute-start.6) | collective-permute-done | bytes 294944 | tf_op jit(solution)/shard_map/ppermute | solution.py:320
  52.4 4.0 %collective-permute-done.8 = bf16[200,768]{1,0:T(8,128)(2,1)} collective-permute-done((bf16[200,768]{1,0:T(8,128)(2,1)S(1)}, bf16[200,768]{1,0:T(8,128)(2,1)}, u32[]{:S(2)}, u32[]{:S(2)}) %collective-permute-start.8) | collective-permute-done | bytes 307232 | tf_op jit(solution)/shard_map/ppermute | solution.py:320
  57.2 6.3 %collective-permute-start.11 = (bf16[200,768]{1,0:T(8,128)(2,1)S(1)}, bf16[200,768]{1,0:T(8,128)(2,1)}, u32[]{:S(2)}, u32[]{:S(2)}) collective-permute-start(bf16[200,768]{1,0:T(8,128)(2,1)S(1)} %bitcast.184), channel_id=1, source_target_pairs={{0,1},{1,0},{2,3},{3,2},{4,5},{5,4},{6,7},{7,6},{8,9},{9,8},{10,11... | collective-permute-start | bytes 921608 | tf_op jit(solution)/shard_map/ppermute | solution.py:320
  72.8 4.8 %add_convert_fusion.q_ref.k_ref.v_ref.refs_0_.refs_1_.refs_2_ = bf16[1024,1152]{1,0:T(8,128)(2,1)} fusion(bf16[1152,768]{1,0:T(8,128)(2,1)S(1)} %bitcast.178, f32[1152]{0:T(1024)S(1)} %add.286, bf16[512,768]{1,0:T(8,128)(2,1)} %collective-permute-done.10.refs_6_, bf16[512,768]{1,0:T(8,128)(2,1)S(1)} %fusion.18.refs_5_), kind=kOutput, calls=%fused_computation.16 | convolution fusion | flops 1817444352 | bytes 5706240 | tf_op jit(solution)/shard_map/dot_general | solution.py:42
  77.6 4.9 %collective-permute-start.13 = (bf16[512,768]{1,0:T(8,128)(2,1)}, bf16[512,768]{1,0:T(8,128)(2,1)}, u32[]{:S(2)}, u32[]{:S(2)}) collective-permute-start(bf16[512,768]{1,0:T(8,128)(2,1)} %param.33), channel_id=1, source_target_pairs={{1,4},{3,6},{4,1},{6,3},{9,12},{11,14},{12,9},{14,11},{17,20},{19,... | collective-permute-start | bytes 2359304 | tf_op jit(solution)/shard_map/ppermute | solution.py:320
  87.7 18.1 %attend.1 = (f32[1024,384]{1,0:T(8,128)}, f32[3,2,1024]{2,1,0:T(2,128)}) custom-call(bf16[1024,1152]{1,0:T(8,128)(2,1)} %add_convert_fusion.q_ref.k_ref.v_ref.refs_0_.refs_1_.refs_2_, bf16[1024,1152]{1,0:T(8,128)(2,1)} %add_convert_fusion.q_ref.k_ref.v_ref.refs_0_.refs_1_.refs_2_, ...), custom_call_target="tpu_custom_call" | custom-call | tf_op jit(solution)/shard_map/attend/pallas_call | solution.py:87
  136.4 5.9 %minimum_convert_fusion = (bf16[1024,1536]{1,0:T(8,128)(2,1)S(1)}, f32[1024,1536]{1,0:T(8,128)S(1)}) fusion(f32[1536]{0:T(1024)S(1)} %reshape.258, bf16[]{:T(256)S(6)} %neg.14, f32[]{:T(128)} %bitcast.36, bf16[1536,768]{1,0:T(8,128)(2,1)S(1)} %bitcast.173, bf16[512,768]{1,0:T(8,128)(2,1)} %collective-permute-done.17, bf16[512,768]{1,0:T(8,128)(2,1)} %minimum_convert_fusion.1), kind=kOutput, calls=%fused_computation.11 | convolution fusion | flops 2434793472 | bytes 13375494 | tf_op jit(solution)/shard_map/dot_general | solution.py:42
  156.0 7.7 %fusion.75 = (bf16[1024,1536]{1,0:T(8,128)(2,1)}, bf16[1536]{0:T(1024)(128)(2,1)S(1)}) fusion(f32[]{:T(128)} %bitcast.36, f32[1024,1536]{1,0:T(8,128)S(1)} %get-tuple-element.265, f32[1536]{0:T(1024)S(1)} %reshape.258, bf16[1536,768]{1,0:T(8,128)(2,1)S(1)} %bitcast.172, bf16[512,768]{1,0:T(8,128)(2,1)S(1)} %collective-permute-done.21, ...), kind=kOutput, calls=%fused_computation.262 | convolution fusion | flops 2444229120 | bytes 13378564 | tf_op jit(solution)/shard_map/dot_general | solution.py:42
  163.8 5.1 %convolution_convert_fusion = bf16[1536,768]{1,0:T(8,128)(2,1)S(1)} fusion(bf16[1024,1536]{1,0:T(8,128)(2,1)} %copy-done.60, bf16[512,768]{1,0:T(8,128)(2,1)} %copy-done.59, bf16[512,768]{1,0:T(8,128)(2,1)} %copy-done.30), kind=kOutput, calls=%fused_computation.17 | convolution fusion | flops 2420244480 | bytes 7077888 | tf_op jit(solution)/shard_map/dot_general | solution.py:50
  169.0 4.3 %convolution_convert_fusion.1 = bf16[1536,768]{1,0:T(8,128)(2,1)S(1)} fusion(bf16[1024,1536]{1,0:T(8,128)(2,1)S(1)} %copy-done.61, bf16[512,768]{1,0:T(8,128)(2,1)} %collective-permute-done.17, bf16[512,768]{1,0:T(8,128)(2,1)} %minimum_convert_fusion.1), kind=kOutput, calls=%fused_computation.18 | convolution fusion | flops 2420244480 | bytes 7077888 | tf_op jit(solution)/shard_map/dot_general | solution.py:50
  193.1 20.1 %attend_back.2 = (bf16[1024,768]{1,0:T(8,128)(2,1)}, bf16[4,384,768]{2,1,0:T(8,128)(2,1)}, f32[2,2,128]{2,1,0:T(2,128)}) custom-call(bf16[1024,1152]{1,0:T(8,128)(2,1)} %add_convert_fusion.q_ref.k_ref.v_ref.refs_0_.refs_1_.refs_2_, bf16[1024,1152]{1,0:T(8,128)(2,1)} %add_convert_fusion.q_ref.k_ref.v_ref.refs_0_.refs_1_.refs_2_, ...), custom_call_target="tpu_custom_call" | custom-call | tf_op jit(solution)/shard_map/attend_back/pallas_call | solution.py:212
  217.0 11.7 %attend_back.3 = (bf16[1024,384]{1,0:T(8,128)(2,1)}, bf16[4,384,768]{2,1,0:T(8,128)(2,1)}, f32[1,2,128]{2,1,0:T(2,128)}) custom-call(bf16[1024,1152]{1,0:T(8,128)(2,1)} %add_convert_fusion.q_ref.k_ref.v_ref.refs_0_.refs_1_.refs_2_, bf16[1024,1152]{1,0:T(8,128)(2,1)} %add_convert_fusion.q_ref.k_ref.v_ref.refs_0_.refs_1_.refs_2_, ...), custom_call_target="tpu_custom_call", output_to_operand_aliasing={{1}: (13, {})} | custom-call | flops 9663676416 | bytes 4718592 | tf_op jit(solution)/shard_map/attend_back/pallas_call | solution.py:212
  246.3 4.2 %add_convert_fusion.1 = bf16[512,768]{1,0:T(8,128)(2,1)} fusion(f32[512,768]{1,0:T(8,128)S(1)} %get-tuple-element.216, f32[512,768]{1,0:T(8,128)} %collective-permute-done.33, bf16[512,768]{1,0:T(8,128)(2,1)S(1)} %copy-done.11, bf16[1152,768]{1,0:T(8,128)(2,1)S(1)} %bitcast.180, bf16[1024,1152]{1,0:T(8,128)(2,1)S(1)} %copy-done.16, f32[]{:T(128)} %bitcast.17), kind=kOutput, calls=%fused_computation.55 | convolution fusion | flops 908722176 | bytes 7667716 | tf_op jit(solution)/shard_map/dot_general | solution.py:46
  250.6 9.7 %collective-permute-done.32 = bf16[408,768]{1,0:T(8,128)(2,1)S(1)} collective-permute-done((bf16[408,768]{1,0:T(8,128)(2,1)S(1)}, bf16[408,768]{1,0:T(8,128)(2,1)S(1)}, u32[]{:S(2)}, u32[]{:S(2)}) %collective-permute-start.32) | collective-permute-done | bytes 626720 | tf_op jit(solution)/shard_map/ppermute | solution.py:320
  260.3 13.7 %collective-permute-done.31 = bf16[408,768]{1,0:T(8,128)(2,1)S(1)} collective-permute-done((bf16[408,768]{1,0:T(8,128)(2,1)S(1)}, bf16[408,768]{1,0:T(8,128)(2,1)S(1)}, u32[]{:S(2)}, u32[]{:S(2)}) %collective-permute-start.31) | collective-permute-done | bytes 626720 | tf_op jit(solution)/shard_map/ppermute | solution.py:320
  292.2 3.6 %collective-permute-done.36 = bf16[216,768]{1,0:T(8,128)(2,1)S(1)} collective-permute-done((bf16[216,768]{1,0:T(8,128)(2,1)S(1)}, bf16[216,768]{1,0:T(8,128)(2,1)S(1)}, u32[]{:S(2)}, u32[]{:S(2)}) %collective-permute-start.36) | collective-permute-done | bytes 331808 | tf_op jit(solution)/shard_map/ppermute | solution.py:320
  298.2 3.7 %collective-permute-done.44 = bf16[200,768]{1,0:T(8,128)(2,1)S(1)} collective-permute-done((bf16[200,768]{1,0:T(8,128)(2,1)S(1)}, bf16[200,768]{1,0:T(8,128)(2,1)S(1)}, u32[]{:S(2)}, u32[]{:S(2)}) %collective-permute-start.44) | collective-permute-done | bytes 307232 | tf_op jit(solution)/shard_map/ppermute | solution.py:320
  304.1 9.7 %collective-permute-start.46 = (bf16[792,768]{1,0:T(8,128)(2,1)S(1)}, bf16[792,768]{1,0:T(8,128)(2,1)}, u32[]{:S(2)}, u32[]{:S(2)}) collective-permute-start(bf16[792,768]{1,0:T(8,128)(2,1)S(1)} %get-tuple-element.202.own_ref), channel_id=1, source_target_pairs={{0,4},{1,5},{2,6},{3,7},{4,0},{5,1},{6,2},{7,3},{8,12},{9,13},{10,... | collective-permute-start | bytes 3649544 | tf_op jit(solution)/shard_map/ppermute | solution.py:320
  313.9 4.8 %collective-permute-start.37 = (bf16[512,768]{1,0:T(8,128)(2,1)S(1)}, bf16[512,768]{1,0:T(8,128)(2,1)S(1)}, u32[]{:S(2)}, u32[]{:S(2)}) collective-permute-start(bf16[512,768]{1,0:T(8,128)(2,1)S(1)} %copy-done.31), channel_id=1, source_target_pairs={{1,4},{3,6},{4,1},{6,3},{9,12},{11,14},{12,9},{14,11},{17,20},{19,... | collective-permute-start | bytes 2359304 | tf_op jit(solution)/shard_map/ppermute | solution.py:320
  322.8 5.5 %collective-permute-done.37 = bf16[512,768]{1,0:T(8,128)(2,1)S(1)} collective-permute-done((bf16[512,768]{1,0:T(8,128)(2,1)S(1)}, bf16[512,768]{1,0:T(8,128)(2,1)S(1)}, u32[]{:S(2)}, u32[]{:S(2)}) %collective-permute-start.37) | collective-permute-done | bytes 786464 | tf_op jit(solution)/shard_map/ppermute | solution.py:320
  331.7 3.8 %unpack.1 = (f32[3,192,768]{2,1,0:T(8,128)}, f32[192,768]{1,0:T(8,128)}) custom-call(s32[2]{0:T(128)} %pad_add_fusion.where_ref, bf16[792,768]{1,0:T(8,128)(2,1)} %copy-done.19, bf16[792,768]{1,0:T(8,128)(2,1)} %collective-permute-done.46.other_ref), custom_call_target="tpu_custom_call" | custom-call | tf_op jit(solution)/shard_map/unpack/pallas_call | solution.py:281
  (375 shorter events, 156.0 us)
Async XLA Ops:
  5.2 19.9 %collective-permute-start = (bf16[200,768]{1,0:T(8,128)(2,1)S(1)}, bf16[200,768]{1,0:T(8,128)(2,1)}, u32[]{:S(2)}, u32[]{:S(2)}) collective-permute-start(bf16[200,768]{1,0:T(8,128)(2,1)S(1)} %fusion.54), channel_id=1, source_target_pairs={{0,2},{1,3},{6,4},{7,5},{8,10},{9,11},{14,12},{15,13},{16,18},{17,... | collective-permute-start | bytes 921608 | tf_op jit(solution)/shard_map/ppermute | solution.py:320
  26.3 17.9 %collective-permute-start.4 = (bf16[2,200,768]{2,1,0:T(8,128)(2,1)S(1)}, bf16[2,200,768]{2,1,0:T(8,128)(2,1)S(1)}, u32[]{:S(2)}, u32[]{:S(2)}) collective-permute-start(bf16[2,200,768]{2,1,0:T(8,128)(2,1)S(1)} %pad_maximum_fusion.23), channel_id=1, source_target_pairs={{0,16},{1,17},{2,18},{3,19},{4,20},{5,21},{6,22},{7,23},{8,24},{9,... | collective-permute-start | bytes 1843208 | tf_op jit(solution)/shard_map/ppermute | solution.py:320
  27.6 17.3 %collective-permute-start.3 = (bf16[2,200,768]{2,1,0:T(8,128)(2,1)S(1)}, bf16[2,200,768]{2,1,0:T(8,128)(2,1)S(1)}, u32[]{:S(2)}, u32[]{:S(2)}) collective-permute-start(bf16[2,200,768]{2,1,0:T(8,128)(2,1)S(1)} %pad_maximum_fusion.23), channel_id=1, source_target_pairs={{0,8},{1,9},{2,10},{3,11},{4,12},{5,13},{6,14},{7,15},{8,0},{9,1},... | collective-permute-start | bytes 1843208 | tf_op jit(solution)/shard_map/ppermute | solution.py:320
  28.8 23.6 %collective-permute-start.9 = (bf16[512,768]{1,0:T(8,128)(2,1)}, bf16[512,768]{1,0:T(8,128)(2,1)S(1)}, u32[]{:S(2)}, u32[]{:S(2)}) collective-permute-start(bf16[512,768]{1,0:T(8,128)(2,1)} %param.18), channel_id=1, source_target_pairs={{1,4},{3,6},{4,1},{6,3},{9,12},{11,14},{12,9},{14,11},{17,20},{19,... | collective-permute-start | bytes 2359304 | tf_op jit(solution)/shard_map/ppermute | solution.py:320
  30.7 13.5 %collective-permute-start.5 = (bf16[200,768]{1,0:T(8,128)(2,1)S(1)}, bf16[200,768]{1,0:T(8,128)(2,1)S(1)}, u32[]{:S(2)}, u32[]{:S(2)}) collective-permute-start(bf16[200,768]{1,0:T(8,128)(2,1)S(1)} %bitcast.182), channel_id=1, source_target_pairs={{0,2},{1,3},{2,0},{3,1},{4,6},{5,7},{6,4},{7,5},{8,10},{9,11},{10,... | collective-permute-start | bytes 921608 | tf_op jit(solution)/shard_map/ppermute | solution.py:320
  77.6 28.2 %collective-permute-start.13 = (bf16[512,768]{1,0:T(8,128)(2,1)}, bf16[512,768]{1,0:T(8,128)(2,1)}, u32[]{:S(2)}, u32[]{:S(2)}) collective-permute-start(bf16[512,768]{1,0:T(8,128)(2,1)} %param.33), channel_id=1, source_target_pairs={{1,4},{3,6},{4,1},{6,3},{9,12},{11,14},{12,9},{14,11},{17,20},{19,... | collective-permute-start | bytes 2359304 | tf_op jit(solution)/shard_map/ppermute | solution.py:320
  83.9 26.4 %collective-permute-start.15 = (bf16[3,200,768]{2,1,0:T(8,128)(2,1)}, bf16[3,200,768]{2,1,0:T(8,128)(2,1)}, u32[]{:S(2)}, u32[]{:S(2)}) collective-permute-start(bf16[3,200,768]{2,1,0:T(8,128)(2,1)} %pad_maximum_fusion.22), channel_id=1, source_target_pairs={{0,16},{1,17},{2,18},{3,19},{4,20},{5,21},{6,22},{7,23},{8,24},{9,... | collective-permute-start | bytes 2764808 | tf_op jit(solution)/shard_map/ppermute | solution.py:320
  85.2 25.1 %collective-permute-start.14 = (bf16[3,200,768]{2,1,0:T(8,128)(2,1)}, bf16[3,200,768]{2,1,0:T(8,128)(2,1)}, u32[]{:S(2)}, u32[]{:S(2)}) collective-permute-start(bf16[3,200,768]{2,1,0:T(8,128)(2,1)} %pad_maximum_fusion.22), channel_id=1, source_target_pairs={{0,8},{1,9},{2,10},{3,11},{4,12},{5,13},{6,14},{7,15},{8,0},{9,1},... | collective-permute-start | bytes 2764808 | tf_op jit(solution)/shard_map/ppermute | solution.py:320
  176.8 36.4 %collective-permute-start.26 = (bf16[512,768]{1,0:T(8,128)(2,1)}, bf16[512,768]{1,0:T(8,128)(2,1)}, u32[]{:S(2)}, u32[]{:S(2)}) collective-permute-start(bf16[512,768]{1,0:T(8,128)(2,1)} %get-tuple-element.235), channel_id=1, source_target_pairs={{1,4},{3,6},{4,1},{6,3},{9,12},{11,14},{12,9},{14,11},{17,20},{19,... | collective-permute-start | bytes 2359304 | tf_op jit(solution)/shard_map/ppermute | solution.py:320
  180.6 32.7 %collective-permute-start.25 = (bf16[2,2,200,768]{3,2,1,0:T(8,128)(2,1)}, bf16[2,2,200,768]{3,2,1,0:T(8,128)(2,1)}, u32[]{:S(2)}, u32[]{:S(2)}) collective-permute-start(bf16[2,2,200,768]{3,2,1,0:T(8,128)(2,1)} %get-tuple-element.226), channel_id=1, source_target_pairs={{0,16},{1,17},{2,18},{3,19},{4,20},{5,21},{6,22},{7,23},{8,24},{9,... | collective-permute-start | bytes 3686408 | tf_op jit(solution)/shard_map/ppermute | solution.py:320
  180.8 32.5 %collective-permute-start.24 = (bf16[2,2,200,768]{3,2,1,0:T(8,128)(2,1)}, bf16[2,2,200,768]{3,2,1,0:T(8,128)(2,1)}, u32[]{:S(2)}, u32[]{:S(2)}) collective-permute-start(bf16[2,2,200,768]{3,2,1,0:T(8,128)(2,1)} %get-tuple-element.227), channel_id=1, source_target_pairs={{0,8},{1,9},{2,10},{3,11},{4,12},{5,13},{6,14},{7,15},{8,0},{9,1},... | collective-permute-start | bytes 3686408 | tf_op jit(solution)/shard_map/ppermute | solution.py:320
  192.7 47.4 %collective-permute-start.29 = (f32[8,768]{1,0:T(8,128)S(1)}, f32[8,768]{1,0:T(8,128)S(1)}, u32[]{:S(2)}, u32[]{:S(2)}) collective-permute-start(f32[8,768]{1,0:T(8,128)S(1)} %concatenate.103), channel_id=1, source_target_pairs={{0,4},{1,5},{2,6},{3,7},{4,0},{5,1},{6,2},{7,3},{8,12},{9,13},{10,... | collective-permute-start | bytes 73736 | tf_op jit(solution)/shard_map/ppermute | solution.py:320
  215.2 15.4 %collective-permute-start.27 = (bf16[2,200,768]{2,1,0:T(8,128)(2,1)S(1)}, bf16[2,200,768]{2,1,0:T(8,128)(2,1)}, u32[]{:S(2)}, u32[]{:S(2)}) collective-permute-start(bf16[2,200,768]{2,1,0:T(8,128)(2,1)S(1)} %get-tuple-element.124), channel_id=1, source_target_pairs={{0,8},{1,9},{2,10},{3,11},{4,12},{5,13},{6,14},{7,15},{8,0},{9,1},... | collective-permute-start | bytes 1843208 | tf_op jit(solution)/shard_map/ppermute | solution.py:320
  215.7 15.1 %collective-permute-start.28 = (bf16[2,200,768]{2,1,0:T(8,128)(2,1)S(1)}, bf16[2,200,768]{2,1,0:T(8,128)(2,1)}, u32[]{:S(2)}, u32[]{:S(2)}) collective-permute-start(bf16[2,200,768]{2,1,0:T(8,128)(2,1)S(1)} %get-tuple-element.125), channel_id=1, source_target_pairs={{0,16},{1,17},{2,18},{3,19},{4,20},{5,21},{6,22},{7,23},{8,24},{9,... | collective-permute-start | bytes 1843208 | tf_op jit(solution)/shard_map/ppermute | solution.py:320
  243.6 16.7 %collective-permute-start.32 = (bf16[408,768]{1,0:T(8,128)(2,1)S(1)}, bf16[408,768]{1,0:T(8,128)(2,1)S(1)}, u32[]{:S(2)}, u32[]{:S(2)}) collective-permute-start(bf16[408,768]{1,0:T(8,128)(2,1)S(1)} %get-tuple-element.250), channel_id=1, source_target_pairs={{0,24},{1,25},{2,26},{3,27},{4,28},{5,29},{6,30},{7,31},{8,16},{9,... | collective-permute-start | bytes 1880072 | tf_op jit(solution)/shard_map/ppermute | solution.py:320
  245.6 28.4 %collective-permute-start.31 = (bf16[408,768]{1,0:T(8,128)(2,1)S(1)}, bf16[408,768]{1,0:T(8,128)(2,1)S(1)}, u32[]{:S(2)}, u32[]{:S(2)}) collective-permute-start(bf16[408,768]{1,0:T(8,128)(2,1)S(1)} %get-tuple-element.251), channel_id=1, source_target_pairs={{0,16},{1,17},{2,18},{3,19},{4,20},{5,21},{6,22},{7,23},{8,24},{9,... | collective-permute-start | bytes 1880072 | tf_op jit(solution)/shard_map/ppermute | solution.py:320
  245.8 28.2 %collective-permute-start.30 = (bf16[408,768]{1,0:T(8,128)(2,1)S(1)}, bf16[408,768]{1,0:T(8,128)(2,1)S(1)}, u32[]{:S(2)}, u32[]{:S(2)}) collective-permute-start(bf16[408,768]{1,0:T(8,128)(2,1)S(1)} %get-tuple-element.252), channel_id=1, source_target_pairs={{0,8},{1,9},{2,10},{3,11},{4,12},{5,13},{6,14},{7,15},{8,0},{9,1},... | collective-permute-start | bytes 1880072 | tf_op jit(solution)/shard_map/ppermute | solution.py:320
  246.3 29.4 %collective-permute-start.41 = (bf16[2,200,768]{2,1,0:T(8,128)(2,1)S(1)}, bf16[2,200,768]{2,1,0:T(8,128)(2,1)S(1)}, u32[]{:S(2)}, u32[]{:S(2)}) collective-permute-start(bf16[2,200,768]{2,1,0:T(8,128)(2,1)S(1)} %copy-done.32), channel_id=1, source_target_pairs={{0,2},{1,3},{2,0},{3,1},{4,6},{5,7},{6,4},{7,5},{8,10},{9,11},{10,... | collective-permute-start | bytes 1843208 | tf_op jit(solution)/shard_map/ppermute | solution.py:320
  279.7 16.0 %collective-permute-start.36 = (bf16[216,768]{1,0:T(8,128)(2,1)S(1)}, bf16[216,768]{1,0:T(8,128)(2,1)S(1)}, u32[]{:S(2)}, u32[]{:S(2)}) collective-permute-start(bf16[216,768]{1,0:T(8,128)(2,1)S(1)} %get-tuple-element.249), channel_id=1, source_target_pairs={{2,1},{3,0},{4,7},{5,6},{10,9},{11,8},{12,15},{13,14},{18,17},{19,... | collective-permute-start | bytes 995336 | tf_op jit(solution)/shard_map/ppermute | solution.py:320
  281.1 14.7 %collective-permute-start.34 = (bf16[216,768]{1,0:T(8,128)(2,1)S(1)}, bf16[216,768]{1,0:T(8,128)(2,1)S(1)}, u32[]{:S(2)}, u32[]{:S(2)}) collective-permute-start(bf16[216,768]{1,0:T(8,128)(2,1)S(1)} %get-tuple-element.249), channel_id=1, source_target_pairs={{0,1},{1,0},{6,7},{7,6},{8,9},{9,8},{14,15},{15,14},{16,17},{17,16... | collective-permute-start | bytes 995336 | tf_op jit(solution)/shard_map/ppermute | solution.py:320
  285.2 16.7 %collective-permute-start.44 = (bf16[200,768]{1,0:T(8,128)(2,1)S(1)}, bf16[200,768]{1,0:T(8,128)(2,1)S(1)}, u32[]{:S(2)}, u32[]{:S(2)}) collective-permute-start(bf16[200,768]{1,0:T(8,128)(2,1)S(1)} %fusion.47), channel_id=1, source_target_pairs={{0,16},{1,17},{2,18},{3,19},{4,20},{5,21},{6,22},{7,23},{8,24},{9,... | collective-permute-start | bytes 921608 | tf_op jit(solution)/shard_map/ppermute | solution.py:320
  304.1 25.4 %collective-permute-start.46 = (bf16[792,768]{1,0:T(8,128)(2,1)S(1)}, bf16[792,768]{1,0:T(8,128)(2,1)}, u32[]{:S(2)}, u32[]{:S(2)}) collective-permute-start(bf16[792,768]{1,0:T(8,128)(2,1)S(1)} %get-tuple-element.202.own_ref), channel_id=1, source_target_pairs={{0,4},{1,5},{2,6},{3,7},{4,0},{5,1},{6,2},{7,3},{8,12},{9,13},{10,... | collective-permute-start | bytes 3649544 | tf_op jit(solution)/shard_map/ppermute | solution.py:320
  313.9 14.4 %collective-permute-start.37 = (bf16[512,768]{1,0:T(8,128)(2,1)S(1)}, bf16[512,768]{1,0:T(8,128)(2,1)S(1)}, u32[]{:S(2)}, u32[]{:S(2)}) collective-permute-start(bf16[512,768]{1,0:T(8,128)(2,1)S(1)} %copy-done.31), channel_id=1, source_target_pairs={{1,4},{3,6},{4,1},{6,3},{9,12},{11,14},{12,9},{14,11},{17,20},{19,... | collective-permute-start | bytes 2359304 | tf_op jit(solution)/shard_map/ppermute | solution.py:320
  320.7 15.3 %collective-permute-start.47 = (bf16[4,200,768]{2,1,0:T(8,128)(2,1)}, bf16[4,200,768]{2,1,0:T(8,128)(2,1)}, u32[]{:S(2)}, u32[]{:S(2)}) collective-permute-start(bf16[4,200,768]{2,1,0:T(8,128)(2,1)} %pad_maximum_fusion.7), channel_id=1, source_target_pairs={{0,4},{1,5},{2,6},{3,7},{4,0},{5,1},{6,2},{7,3},{8,12},{9,13},{10,... | collective-permute-start | bytes 3686408 | tf_op jit(solution)/shard_map/ppermute | solution.py:320
  (88 other events, 594.1 us)

commit v2 on v1

--- a/solution.py
+++ b/solution.py
@@ -505,14 +505,10 @@
         attn_both = links.pair_of(attn_mine, attn_in)
         attn_near = links.spread_near(attn_both)
         x_home = links.rows_home(x_home)
-        ffn_in = [links.along(ffn_mine, 2)]
-        attn_near, ffn_in, ffn_mine = sync(attn_near, ffn_in, ffn_mine)
-        attn_full = links.spread_far(attn_both, attn_near)
-        ffn_in.append(links.along(ffn_mine, 3))
-        attn_full, ffn_in, ffn_mine, x_home = sync(attn_full, ffn_in, ffn_mine, x_home)
-        ffn_in.append(links.along(ffn_mine, 1))
-        attn_full = jnp.stack(attn_full)
-        ffn_in = jnp.stack([ffn_in[2], ffn_in[0], ffn_in[1]])
+        ffn_two = links.along(ffn_mine, 2)
+        attn_near, ffn_two, ffn_mine = sync(attn_near, ffn_two, ffn_mine)
+        attn_full = jnp.stack(links.spread_far(attn_both, attn_near))
+        ffn_in = jnp.stack([links.along(ffn_mine, 1), ffn_two, links.along(ffn_mine, 3)])
     else:
         attn_full = lax.all_gather(attn_pack, "tensor", axis=0, tiled=False)
         attn_full = lax.dynamic_slice_in_dim(attn_full, 2 * links.half, 2, 0).swapaxes(0, 1)
@@ -557,7 +553,10 @@
         x_full + attn_out, gain_first, shift_attn.astype(F32)
     )
     hid_quant = jnp.clip(hidden, -act_scale[2], act_scale[2]).astype(BF16)
-    hid_rows = jnp.concatenate([hid_quant, links.other_half(hid_quant)])
+    hid_other = links.other_half(hid_quant)
+    tops = [jnp.max(jnp.abs(array)) for array in (x_full, context, hidden)]
+    hid_other, tops = sync(hid_other, tops)
+    hid_rows = jnp.concatenate([hid_quant, hid_other])
 
     w_up = ffn_full[:, :, :quarter].reshape(2 * units, width)
     w_low = ffn_full[:, :, quarter : 2 * quarter].reshape(2 * units, width)
@@ -577,8 +576,8 @@
     layer_output = links.rows_home(final)
     lanes = lax.broadcasted_iota(jnp.int32, (1, width), 1)
     maxima = jnp.zeros((1, width), F32)
-    for at, array in enumerate((x_full, context, hidden, activated)):
-        maxima = jnp.where(lanes == at, jnp.max(jnp.abs(array)), maxima)
+    for at, value in enumerate((*tops, jnp.max(jnp.abs(activated)))):
+        maxima = jnp.where(lanes == at, value, maxima)
 
     grad_gain_ffn = jnp.sum(upstream * normed_ffn, axis=0, keepdims=True)
     grad_shift_ffn = jnp.sum(upstream, axis=0, keepdims=True)
@@ -638,9 +637,7 @@
         tall = 2 * heads * HEAD // 2
         many = heads - 1
         early, grad_w, early_b = back(0, many, None)
-        early, go_other, ffn_x, ffn_y, layer_output = sync(
-            early, go_other, ffn_x, ffn_y, layer_output
-        )
+        early, go_other, ffn_x, ffn_y = sync(early, go_other, ffn_x, ffn_y)
         low = [ffn_grads[0, :2] + ffn_x[0].astype(F32), ffn_grads[3, :2] + ffn_x[1].astype(F32)]
         high = [ffn_grads[0, 2:] + ffn_y[1].astype(F32), ffn_grads[1, 2:] + ffn_y[0].astype(F32)]
         ffn_y, ffn_x = low[1].astype(BF16), high[1].astype(BF16)
@@ -667,7 +664,6 @@
     input_part = input_grad.astype(BF16)
 
     if links.square:
-        proj_in, input_part = sync(proj_in, input_part)
         total = grad_w[0].astype(F32)
         for part in proj_in:
             total = total + part[: 2 * tall].astype(F32)

time: 349 us -> 331 us (0.948)
  local copies, waits for them, and re-layouts: 30.6 us -> 25.5 us
  waiting for transfers between devices: 88.2 us -> 83.9 us
  matrix products: 44.2 us -> 40.4 us
  other arithmetic: 52.8 us -> 49.1 us
    ppermute x48, waiting for transfers between devices: 88.2 us -> 83.9 us  [permute(): return lax.ppermute(array, JOINT, pairs)]
    unnamed x137 -> x133, local copies, waits for them, and re-layouts: 14.9 us -> 13.1 us
  transfers between devices with their start and end apart: 48 -> 48, of which waited for: 20 -> 18; matrix products, arithmetic and copies ran while one was open for 20% -> 17% of each run, Pallas kernels for 16% -> 16%
where the time goes in v2:
time: 331 us; the launch traced here: 326 us
  waiting for transfers between devices  83.9 us (25%)
  starting transfers between devices  67.9 us (21%)
  Pallas kernels  53.6 us (16%)
  other arithmetic  49.1 us (15%)
  matrix products  40.4 us (12%)
  local copies, waits for them, and re-layouts  25.5 us (8%)
  between operations  5.27 us (2%)
    ppermute x48, waiting for transfers between devices, permute(): return lax.ppermute(array, JOINT, pairs)  83.9 us
    ppermute x48, starting transfers between devices, permute(): return lax.ppermute(array, JOINT, pairs)  67.9 us
    pallas_call x2, Pallas kernels, attend_back(): pl.pallas_call(body, grid=(n,), in_specs=[pl.BlockSpec((LEN, 2 * HEAD), l...  31.6 us
    pallas_call x1, Pallas kernels, attend(): pl.pallas_call(attend_kernel, grid=(n,), in_specs=[pl.BlockSpec((LEN, 2 *...  18.1 us
    dot_general x3, matrix products, nt(): lax.dot_general(a, b, (((1,), (1,)), ((), ())), preferred_element_type=F32)  17.4 us
    dot_general x8, matrix products, nn(): lax.dot_general(a, b, (((1,), (0,)), ((), ())), preferred_element_type=F32)  14.7 us
    unnamed x133, local copies, waits for them, and re-layouts  13.1 us
    dot_general x2, matrix products, tn(): lax.dot_general(a, b, (((0,), (0,)), ((), ())), preferred_element_type=F32)  8.27 us
  transfers between devices with their start and end apart: 48, of which 18 were waited for; matrix products, arithmetic and copies ran while one was open for 17% of the time, Pallas kernels for 16%

profile of v2, /device:TPU:1, one launch (start us, length us, event | category | flops | bytes accessed | tf_op | source)
XLA Modules:
  0.0 325.5 jit_solution(3627544318983644478)
XLA Ops:
  9.6 7.4 %collective-permute-done.1 = bf16[200,768]{1,0:T(8,128)(2,1)S(1)} collective-permute-done((bf16[200,768]{1,0:T(8,128)(2,1)S(1)}, bf16[200,768]{1,0:T(8,128)(2,1)S(1)}, u32[]{:S(2)}, u32[]{:S(2)}) %collective-permute-start.1) | collective-permute-done | bytes 307232 | tf_op jit(solution)/shard_map/ppermute | solution.py:320
  17.0 8.0 %collective-permute-done = bf16[200,768]{1,0:T(8,128)(2,1)} collective-permute-done((bf16[200,768]{1,0:T(8,128)(2,1)S(1)}, bf16[200,768]{1,0:T(8,128)(2,1)}, u32[]{:S(2)}, u32[]{:S(2)}) %collective-permute-start) | collective-permute-done | bytes 307232 | tf_op jit(solution)/shard_map/ppermute | solution.py:320
  34.3 8.3 %collective-permute-done.7 = bf16[200,768]{1,0:T(8,128)(2,1)S(1)} collective-permute-done((bf16[200,768]{1,0:T(8,128)(2,1)S(1)}, bf16[200,768]{1,0:T(8,128)(2,1)S(1)}, u32[]{:S(2)}, u32[]{:S(2)}) %collective-permute-start.7) | collective-permute-done | bytes 307232 | tf_op jit(solution)/shard_map/ppermute | solution.py:320
  42.7 3.1 collective-permute-start.10
  53.6 6.5 %collective-permute-done.10 = bf16[200,768]{1,0:T(8,128)(2,1)S(1)} collective-permute-done((bf16[200,768]{1,0:T(8,128)(2,1)S(1)}, bf16[200,768]{1,0:T(8,128)(2,1)S(1)}, u32[]{:S(2)}, u32[]{:S(2)}) %collective-permute-start.10) | collective-permute-done | bytes 307232 | tf_op jit(solution)/shard_map/ppermute | solution.py:320
  63.7 5.7 %add_convert_fusion.q_ref.k_ref.v_ref.refs_0_.refs_1_.refs_2_ = bf16[1024,1152]{1,0:T(8,128)(2,1)} fusion(bf16[1152,768]{1,0:T(8,128)(2,1)S(1)} %bitcast.176, f32[1152]{0:T(1024)S(1)} %add.286, bf16[512,768]{1,0:T(8,128)(2,1)} %collective-permute-done.4.refs_6_, bf16[512,768]{1,0:T(8,128)(2,1)} %fusion.18.refs_5_), kind=kOutput, calls=%fused_computation.16 | convolution fusion | flops 1817444352 | bytes 5706240 | tf_op jit(solution)/shard_map/dot_general | solution.py:42
  76.0 18.1 %attend.1 = (f32[1024,384]{1,0:T(8,128)}, f32[3,2,1024]{2,1,0:T(2,128)}) custom-call(bf16[1024,1152]{1,0:T(8,128)(2,1)} %add_convert_fusion.q_ref.k_ref.v_ref.refs_0_.refs_1_.refs_2_, bf16[1024,1152]{1,0:T(8,128)(2,1)} %add_convert_fusion.q_ref.k_ref.v_ref.refs_0_.refs_1_.refs_2_, ...), custom_call_target="tpu_custom_call" | custom-call | tf_op jit(solution)/shard_map/attend/pallas_call | solution.py:87
  109.8 7.3 %collective-permute-done.18 = bf16[3,96,768]{2,1,0:T(8,128)(2,1)S(1)} collective-permute-done((bf16[3,96,768]{2,1,0:T(8,128)(2,1)S(1)}, bf16[3,96,768]{2,1,0:T(8,128)(2,1)S(1)}, u32[]{:S(2)}, u32[]{:S(2)}) %collective-permute-start.18) | collective-permute-done | bytes 442400 | tf_op jit(solution)/shard_map/ppermute | solution.py:320
  126.2 4.0 %minimum_convert_fusion = (bf16[1024,1536]{1,0:T(8,128)(2,1)S(1)}, f32[1024,1536]{1,0:T(8,128)S(1)}) fusion(f32[1536]{0:T(1024)S(1)} %reshape.258, bf16[]{:T(256)S(6)} %neg.14, f32[]{:T(128)} %bitcast.36, bf16[1536,768]{1,0:T(8,128)(2,1)S(1)} %bitcast.171, bf16[512,768]{1,0:T(8,128)(2,1)S(1)} %collective-permute-done.17, ...), kind=kOutput, calls=%fused_computation.11 | convolution fusion | flops 2434793472 | bytes 13375494 | tf_op jit(solution)/shard_map/dot_general | solution.py:42
  132.2 3.0 collective-permute-done.20
  143.3 7.7 %fusion.76 = (bf16[1024,1536]{1,0:T(8,128)(2,1)}, bf16[1536]{0:T(1024)(128)(2,1)S(1)}) fusion(f32[]{:T(128)} %bitcast.36, f32[1024,1536]{1,0:T(8,128)S(1)} %get-tuple-element.248, f32[1536]{0:T(1024)S(1)} %reshape.258, bf16[1536,768]{1,0:T(8,128)(2,1)S(1)} %bitcast.170, bf16[512,768]{1,0:T(8,128)(2,1)S(1)} %collective-permute-done.22, ...), kind=kOutput, calls=%fused_computation.263 | convolution fusion | flops 2444229120 | bytes 13378564 | tf_op jit(solution)/shard_map/dot_general | solution.py:42
  151.1 5.1 %convolution_convert_fusion.1 = bf16[1536,768]{1,0:T(8,128)(2,1)S(1)} fusion(bf16[1024,1536]{1,0:T(8,128)(2,1)} %get-tuple-element.95, bf16[512,768]{1,0:T(8,128)(2,1)} %copy-done.54, bf16[512,768]{1,0:T(8,128)(2,1)} %copy-done.33), kind=kOutput, calls=%fused_computation.18 | convolution fusion | flops 2420244480 | bytes 7077888 | tf_op jit(solution)/shard_map/dot_general | solution.py:50
  156.3 3.1 convolution_convert_fusion
  178.6 19.9 %attend_back.2 = (bf16[1024,768]{1,0:T(8,128)(2,1)}, bf16[4,384,768]{2,1,0:T(8,128)(2,1)}, f32[2,2,128]{2,1,0:T(2,128)}) custom-call(bf16[1024,1152]{1,0:T(8,128)(2,1)} %add_convert_fusion.q_ref.k_ref.v_ref.refs_0_.refs_1_.refs_2_, bf16[1024,1152]{1,0:T(8,128)(2,1)} %add_convert_fusion.q_ref.k_ref.v_ref.refs_0_.refs_1_.refs_2_, ...), custom_call_target="tpu_custom_call" | custom-call | tf_op jit(solution)/shard_map/attend_back/pallas_call | solution.py:212
  202.0 11.7 %attend_back.3 = (bf16[1024,384]{1,0:T(8,128)(2,1)}, bf16[4,384,768]{2,1,0:T(8,128)(2,1)}, f32[1,2,128]{2,1,0:T(2,128)}) custom-call(bf16[1024,1152]{1,0:T(8,128)(2,1)} %add_convert_fusion.q_ref.k_ref.v_ref.refs_0_.refs_1_.refs_2_, bf16[1024,1152]{1,0:T(8,128)(2,1)} %add_convert_fusion.q_ref.k_ref.v_ref.refs_0_.refs_1_.refs_2_, ...), custom_call_target="tpu_custom_call", output_to_operand_aliasing={{1}: (13, {})} | custom-call | flops 9663676416 | bytes 4718592 | tf_op jit(solution)/shard_map/attend_back/pallas_call | solution.py:212
  228.9 7.5 %collective-permute-done.30 = bf16[408,768]{1,0:T(8,128)(2,1)S(1)} collective-permute-done((bf16[408,768]{1,0:T(8,128)(2,1)S(1)}, bf16[408,768]{1,0:T(8,128)(2,1)S(1)}, u32[]{:S(2)}, u32[]{:S(2)}) %collective-permute-start.30) | collective-permute-done | bytes 626720 | tf_op jit(solution)/shard_map/ppermute | solution.py:320
  236.9 13.0 %collective-permute-done.32 = bf16[408,768]{1,0:T(8,128)(2,1)S(1)} collective-permute-done((bf16[408,768]{1,0:T(8,128)(2,1)S(1)}, bf16[408,768]{1,0:T(8,128)(2,1)S(1)}, u32[]{:S(2)}, u32[]{:S(2)}) %collective-permute-start.32) | collective-permute-done | bytes 626720 | tf_op jit(solution)/shard_map/ppermute | solution.py:320
  251.5 4.0 %collective-permute-start.34 = (bf16[216,768]{1,0:T(8,128)(2,1)S(1)}, bf16[216,768]{1,0:T(8,128)(2,1)S(1)}, u32[]{:S(2)}, u32[]{:S(2)}) collective-permute-start(bf16[216,768]{1,0:T(8,128)(2,1)S(1)} %get-tuple-element.231), channel_id=1, source_target_pairs={{2,0},{3,1},{4,6},{5,7},{10,8},{11,9},{12,14},{13,15},{18,16},{19,... | collective-permute-start | bytes 995336 | tf_op jit(solution)/shard_map/ppermute | solution.py:320
  259.3 3.5 %collective-permute-done.34 = bf16[216,768]{1,0:T(8,128)(2,1)S(1)} collective-permute-done((bf16[216,768]{1,0:T(8,128)(2,1)S(1)}, bf16[216,768]{1,0:T(8,128)(2,1)S(1)}, u32[]{:S(2)}, u32[]{:S(2)}) %collective-permute-start.34) | collective-permute-done | bytes 331808 | tf_op jit(solution)/shard_map/ppermute | solution.py:320
  263.5 5.6 %collective-permute-done.35 = bf16[216,768]{1,0:T(8,128)(2,1)S(1)} collective-permute-done((bf16[216,768]{1,0:T(8,128)(2,1)S(1)}, bf16[216,768]{1,0:T(8,128)(2,1)S(1)}, u32[]{:S(2)}, u32[]{:S(2)}) %collective-permute-start.35) | collective-permute-done | bytes 331808 | tf_op jit(solution)/shard_map/ppermute | solution.py:320
  275.0 15.6 %collective-permute-start.21 = (bf16[512,768]{1,0:T(8,128)(2,1)S(1)}, bf16[512,768]{1,0:T(8,128)(2,1)S(1)}, u32[]{:S(2)}, u32[]{:S(2)}) collective-permute-start(bf16[512,768]{1,0:T(8,128)(2,1)S(1)} %copy-done.17), channel_id=1, source_target_pairs={{1,4},{3,6},{4,1},{6,3},{9,12},{11,14},{12,9},{14,11},{17,20},{19,... | collective-permute-start | bytes 2359304 | tf_op jit(solution)/shard_map/ppermute | solution.py:320
  296.3 4.9 %collective-permute-start.37 = (bf16[512,768]{1,0:T(8,128)(2,1)}, bf16[512,768]{1,0:T(8,128)(2,1)S(1)}, u32[]{:S(2)}, u32[]{:S(2)}) collective-permute-start(bf16[512,768]{1,0:T(8,128)(2,1)} %add_convert_fusion.1), channel_id=1, source_target_pairs={{1,4},{3,6},{4,1},{6,3},{9,12},{11,14},{12,9},{14,11},{17,20},{19,... | collective-permute-start | bytes 2359304 | tf_op jit(solution)/shard_map/ppermute | solution.py:320
  305.2 5.8 %collective-permute-done.37 = bf16[512,768]{1,0:T(8,128)(2,1)S(1)} collective-permute-done((bf16[512,768]{1,0:T(8,128)(2,1)}, bf16[512,768]{1,0:T(8,128)(2,1)S(1)}, u32[]{:S(2)}, u32[]{:S(2)}) %collective-permute-start.37) | collective-permute-done | bytes 786464 | tf_op jit(solution)/shard_map/ppermute | solution.py:320
  314.4 3.8 %unpack.1 = (f32[3,192,768]{2,1,0:T(8,128)}, f32[192,768]{1,0:T(8,128)}) custom-call(s32[2]{0:T(128)} %pad_add_fusion.where_ref, bf16[792,768]{1,0:T(8,128)(2,1)} %get-tuple-element.183.own_ref, bf16[792,768]{1,0:T(8,128)(2,1)} %collective-permute-done.46.other_ref), custom_call_target="tpu_custom_call" | custom-call | tf_op jit(solution)/shard_map/unpack/pallas_call | solution.py:281
  (372 shorter events, 137.6 us)
Async XLA Ops:
  5.2 19.9 %collective-permute-start = (bf16[200,768]{1,0:T(8,128)(2,1)S(1)}, bf16[200,768]{1,0:T(8,128)(2,1)}, u32[]{:S(2)}, u32[]{:S(2)}) collective-permute-start(bf16[200,768]{1,0:T(8,128)(2,1)S(1)} %fusion.54), channel_id=1, source_target_pairs={{0,2},{1,3},{6,4},{7,5},{8,10},{9,11},{14,12},{15,13},{16,18},{17,... | collective-permute-start | bytes 921608 | tf_op jit(solution)/shard_map/ppermute | solution.py:320
  25.1 23.4 %collective-permute-start.3 = (bf16[512,768]{1,0:T(8,128)(2,1)S(1)}, bf16[512,768]{1,0:T(8,128)(2,1)}, u32[]{:S(2)}, u32[]{:S(2)}) collective-permute-start(bf16[512,768]{1,0:T(8,128)(2,1)S(1)} %copy-done.32), channel_id=1, source_target_pairs={{1,4},{3,6},{4,1},{6,3},{9,12},{11,14},{12,9},{14,11},{17,20},{19,... | collective-permute-start | bytes 2359304 | tf_op jit(solution)/shard_map/ppermute | solution.py:320
  42.7 17.3 %collective-permute-start.10 = (bf16[200,768]{1,0:T(8,128)(2,1)S(1)}, bf16[200,768]{1,0:T(8,128)(2,1)S(1)}, u32[]{:S(2)}, u32[]{:S(2)}) collective-permute-start(bf16[200,768]{1,0:T(8,128)(2,1)S(1)} %bitcast.182), channel_id=1, source_target_pairs={{0,1},{1,0},{2,3},{3,2},{4,5},{5,4},{6,7},{7,6},{8,9},{9,8},{10,11... | collective-permute-start | bytes 921608 | tf_op jit(solution)/shard_map/ppermute | solution.py:320
  45.8 15.3 %collective-permute-start.8 = (bf16[2,96,768]{2,1,0:T(8,128)(2,1)S(1)}, bf16[2,96,768]{2,1,0:T(8,128)(2,1)S(1)}, u32[]{:S(2)}, u32[]{:S(2)}) collective-permute-start(bf16[2,96,768]{2,1,0:T(8,128)(2,1)S(1)} %slice.291), channel_id=1, source_target_pairs={{0,8},{1,9},{2,10},{3,11},{4,12},{5,13},{6,14},{7,15},{8,0},{9,1},... | collective-permute-start | bytes 884744 | tf_op jit(solution)/shard_map/ppermute | solution.py:320
  69.4 24.8 %collective-permute-start.13 = (bf16[512,768]{1,0:T(8,128)(2,1)}, bf16[512,768]{1,0:T(8,128)(2,1)}, u32[]{:S(2)}, u32[]{:S(2)}) collective-permute-start(bf16[512,768]{1,0:T(8,128)(2,1)} %param.33), channel_id=1, source_target_pairs={{1,4},{3,6},{4,1},{6,3},{9,12},{11,14},{12,9},{14,11},{17,20},{19,... | collective-permute-start | bytes 2359304 | tf_op jit(solution)/shard_map/ppermute | solution.py:320
  73.4 26.5 %collective-permute-start.15 = (bf16[3,200,768]{2,1,0:T(8,128)(2,1)S(1)}, bf16[3,200,768]{2,1,0:T(8,128)(2,1)}, u32[]{:S(2)}, u32[]{:S(2)}) collective-permute-start(bf16[3,200,768]{2,1,0:T(8,128)(2,1)S(1)} %copy-done.16), channel_id=1, source_target_pairs={{0,16},{1,17},{2,18},{3,19},{4,20},{5,21},{6,22},{7,23},{8,24},{9,... | collective-permute-start | bytes 2764808 | tf_op jit(solution)/shard_map/ppermute | solution.py:320
  74.5 25.3 %collective-permute-start.14 = (bf16[3,200,768]{2,1,0:T(8,128)(2,1)S(1)}, bf16[3,200,768]{2,1,0:T(8,128)(2,1)}, u32[]{:S(2)}, u32[]{:S(2)}) collective-permute-start(bf16[3,200,768]{2,1,0:T(8,128)(2,1)S(1)} %copy-done.16), channel_id=1, source_target_pairs={{0,8},{1,9},{2,10},{3,11},{4,12},{5,13},{6,14},{7,15},{8,0},{9,1},... | collective-permute-start | bytes 2764808 | tf_op jit(solution)/shard_map/ppermute | solution.py:320
  99.8 18.5 %collective-permute-start.16 = (f32[512,768]{1,0:T(8,128)}, f32[512,768]{1,0:T(8,128)}, u32[]{:S(2)}, u32[]{:S(2)}) collective-permute-start(f32[512,768]{1,0:T(8,128)} %fusion.49), channel_id=1, source_target_pairs={{0,4},{1,5},{2,6},{3,7},{4,0},{5,1},{6,2},{7,3},{8,12},{9,13},{10,... | collective-permute-start | bytes 4718600 | tf_op jit(solution)/shard_map/ppermute | solution.py:320
  165.9 32.6 %collective-permute-start.26 = (bf16[2,2,200,768]{3,2,1,0:T(8,128)(2,1)}, bf16[2,2,200,768]{3,2,1,0:T(8,128)(2,1)}, u32[]{:S(2)}, u32[]{:S(2)}) collective-permute-start(bf16[2,2,200,768]{3,2,1,0:T(8,128)(2,1)} %get-tuple-element.207), channel_id=1, source_target_pairs={{0,16},{1,17},{2,18},{3,19},{4,20},{5,21},{6,22},{7,23},{8,24},{9,... | collective-permute-start | bytes 3686408 | tf_op jit(solution)/shard_map/ppermute | solution.py:320
  166.2 32.4 %collective-permute-start.25 = (bf16[2,2,200,768]{3,2,1,0:T(8,128)(2,1)}, bf16[2,2,200,768]{3,2,1,0:T(8,128)(2,1)}, u32[]{:S(2)}, u32[]{:S(2)}) collective-permute-start(bf16[2,2,200,768]{3,2,1,0:T(8,128)(2,1)} %get-tuple-element.208), channel_id=1, source_target_pairs={{0,8},{1,9},{2,10},{3,11},{4,12},{5,13},{6,14},{7,15},{8,0},{9,1},... | collective-permute-start | bytes 3686408 | tf_op jit(solution)/shard_map/ppermute | solution.py:320
  200.5 15.5 %collective-permute-start.27 = (bf16[2,200,768]{2,1,0:T(8,128)(2,1)S(1)}, bf16[2,200,768]{2,1,0:T(8,128)(2,1)S(1)}, u32[]{:S(2)}, u32[]{:S(2)}) collective-permute-start(bf16[2,200,768]{2,1,0:T(8,128)(2,1)S(1)} %get-tuple-element.107), channel_id=1, source_target_pairs={{0,8},{1,9},{2,10},{3,11},{4,12},{5,13},{6,14},{7,15},{8,0},{9,1},... | collective-permute-start | bytes 1843208 | tf_op jit(solution)/shard_map/ppermute | solution.py:320
  201.1 15.1 %collective-permute-start.28 = (bf16[2,200,768]{2,1,0:T(8,128)(2,1)S(1)}, bf16[2,200,768]{2,1,0:T(8,128)(2,1)}, u32[]{:S(2)}, u32[]{:S(2)}) collective-permute-start(bf16[2,200,768]{2,1,0:T(8,128)(2,1)S(1)} %get-tuple-element.108), channel_id=1, source_target_pairs={{0,16},{1,17},{2,18},{3,19},{4,20},{5,21},{6,22},{7,23},{8,24},{9,... | collective-permute-start | bytes 1843208 | tf_op jit(solution)/shard_map/ppermute | solution.py:320
  220.8 29.4 %collective-permute-start.41 = (bf16[2,200,768]{2,1,0:T(8,128)(2,1)S(1)}, bf16[2,200,768]{2,1,0:T(8,128)(2,1)S(1)}, u32[]{:S(2)}, u32[]{:S(2)}) collective-permute-start(bf16[2,200,768]{2,1,0:T(8,128)(2,1)S(1)} %get-tuple-element.203), channel_id=1, source_target_pairs={{0,2},{1,3},{2,0},{3,1},{4,6},{5,7},{6,4},{7,5},{8,10},{9,11},{10,... | collective-permute-start | bytes 1843208 | tf_op jit(solution)/shard_map/ppermute | solution.py:320
  223.1 26.8 %collective-permute-start.32 = (bf16[408,768]{1,0:T(8,128)(2,1)S(1)}, bf16[408,768]{1,0:T(8,128)(2,1)S(1)}, u32[]{:S(2)}, u32[]{:S(2)}) collective-permute-start(bf16[408,768]{1,0:T(8,128)(2,1)S(1)} %get-tuple-element.235), channel_id=1, source_target_pairs={{0,24},{1,25},{2,26},{3,27},{4,28},{5,29},{6,30},{7,31},{8,16},{9,... | collective-permute-start | bytes 1880072 | tf_op jit(solution)/shard_map/ppermute | solution.py:320
  226.5 43.5 %collective-permute-start.36 = (f32[512,768]{1,0:T(8,128)S(1)}, f32[512,768]{1,0:T(8,128)S(1)}, u32[]{:S(2)}, u32[]{:S(2)}) collective-permute-start(f32[512,768]{1,0:T(8,128)S(1)} %fusion.40), channel_id=1, source_target_pairs={{0,4},{1,5},{2,6},{3,7},{4,0},{5,1},{6,2},{7,3},{8,12},{9,13},{10,... | collective-permute-start | bytes 4718600 | tf_op jit(solution)/shard_map/ppermute | solution.py:320
  258.1 16.2 %collective-permute-start.45 = (bf16[200,768]{1,0:T(8,128)(2,1)S(1)}, bf16[200,768]{1,0:T(8,128)(2,1)S(1)}, u32[]{:S(2)}, u32[]{:S(2)}) collective-permute-start(bf16[200,768]{1,0:T(8,128)(2,1)S(1)} %fusion.47), channel_id=1, source_target_pairs={{0,24},{1,25},{2,26},{3,27},{4,28},{5,29},{6,30},{7,31},{8,16},{9,... | collective-permute-start | bytes 921608 | tf_op jit(solution)/shard_map/ppermute | solution.py:320
  269.1 21.6 %collective-permute-start.43 = (bf16[200,768]{1,0:T(8,128)(2,1)S(1)}, bf16[200,768]{1,0:T(8,128)(2,1)S(1)}, u32[]{:S(2)}, u32[]{:S(2)}) collective-permute-start(bf16[200,768]{1,0:T(8,128)(2,1)S(1)} %fusion.47), channel_id=1, source_target_pairs={{0,8},{1,9},{2,10},{3,11},{4,12},{5,13},{6,14},{7,15},{8,0},{9,1},... | collective-permute-start | bytes 921608 | tf_op jit(solution)/shard_map/ppermute | solution.py:320
  272.9 17.8 %collective-permute-start.40 = (bf16[192,768]{1,0:T(8,128)(2,1)S(1)}, bf16[192,768]{1,0:T(8,128)(2,1)S(1)}, u32[]{:S(2)}, u32[]{:S(2)}) collective-permute-start(bf16[192,768]{1,0:T(8,128)(2,1)S(1)} %add_convert_fusion.5), channel_id=1, source_target_pairs={{0,24},{1,25},{6,30},{7,31},{8,16},{9,17},{14,22},{15,23},{16,8},{... | collective-permute-start | bytes 884744 | tf_op jit(solution)/shard_map/ppermute | solution.py:320
  273.5 17.1 %collective-permute-start.39 = (bf16[192,768]{1,0:T(8,128)(2,1)S(1)}, bf16[192,768]{1,0:T(8,128)(2,1)S(1)}, u32[]{:S(2)}, u32[]{:S(2)}) collective-permute-start(bf16[192,768]{1,0:T(8,128)(2,1)S(1)} %add_convert_fusion.5), channel_id=1, source_target_pairs={{0,16},{1,17},{6,22},{7,23},{8,24},{9,25},{14,30},{15,31},{16,0},{... | collective-permute-start | bytes 884744 | tf_op jit(solution)/shard_map/ppermute | solution.py:320
  274.3 16.4 %collective-permute-start.38 = (bf16[192,768]{1,0:T(8,128)(2,1)S(1)}, bf16[192,768]{1,0:T(8,128)(2,1)S(1)}, u32[]{:S(2)}, u32[]{:S(2)}) collective-permute-start(bf16[192,768]{1,0:T(8,128)(2,1)S(1)} %add_convert_fusion.5), channel_id=1, source_target_pairs={{0,8},{1,9},{6,14},{7,15},{8,0},{9,1},{14,6},{15,7},{16,24},{17,25... | collective-permute-start | bytes 884744 | tf_op jit(solution)/shard_map/ppermute | solution.py:320
  275.0 29.3 %collective-permute-start.21 = (bf16[512,768]{1,0:T(8,128)(2,1)S(1)}, bf16[512,768]{1,0:T(8,128)(2,1)S(1)}, u32[]{:S(2)}, u32[]{:S(2)}) collective-permute-start(bf16[512,768]{1,0:T(8,128)(2,1)S(1)} %copy-done.17), channel_id=1, source_target_pairs={{1,4},{3,6},{4,1},{6,3},{9,12},{11,14},{12,9},{14,11},{17,20},{19,... | collective-permute-start | bytes 2359304 | tf_op jit(solution)/shard_map/ppermute | solution.py:320
  295.5 16.8 %collective-permute-start.46 = (bf16[792,768]{1,0:T(8,128)(2,1)}, bf16[792,768]{1,0:T(8,128)(2,1)}, u32[]{:S(2)}, u32[]{:S(2)}) collective-permute-start(bf16[792,768]{1,0:T(8,128)(2,1)} %get-tuple-element.183.own_ref), channel_id=1, source_target_pairs={{0,4},{1,5},{2,6},{3,7},{4,0},{5,1},{6,2},{7,3},{8,12},{9,13},{10,... | collective-permute-start | bytes 3649544 | tf_op jit(solution)/shard_map/ppermute | solution.py:320
  296.3 14.8 %collective-permute-start.37 = (bf16[512,768]{1,0:T(8,128)(2,1)}, bf16[512,768]{1,0:T(8,128)(2,1)S(1)}, u32[]{:S(2)}, u32[]{:S(2)}) collective-permute-start(bf16[512,768]{1,0:T(8,128)(2,1)} %add_convert_fusion.1), channel_id=1, source_target_pairs={{1,4},{3,6},{4,1},{6,3},{9,12},{11,14},{12,9},{14,11},{17,20},{19,... | collective-permute-start | bytes 2359304 | tf_op jit(solution)/shard_map/ppermute | solution.py:320
  304.3 14.5 %collective-permute-start.47 = (bf16[4,200,768]{2,1,0:T(8,128)(2,1)}, bf16[4,200,768]{2,1,0:T(8,128)(2,1)}, u32[]{:S(2)}, u32[]{:S(2)}) collective-permute-start(bf16[4,200,768]{2,1,0:T(8,128)(2,1)} %pad_maximum_fusion.7), channel_id=1, source_target_pairs={{0,4},{1,5},{2,6},{3,7},{4,0},{5,1},{6,2},{7,3},{8,12},{9,13},{10,... | collective-permute-start | bytes 3686408 | tf_op jit(solution)/shard_map/ppermute | solution.py:320
  (86 other events, 634.2 us)

commit v3 on v2

--- a/solution.py
+++ b/solution.py
@@ -250,41 +250,39 @@
     )
 
 
-def unpack_kernel(where_ref, own_ref, other_ref, qkv_ref, out_ref):
-    inside, plane = where_ref[0], where_ref[1]
+def unpack_kernel(plane_ref, *refs):
+    pieces, (qkv_ref, out_ref) = refs[:4], refs[4:]
     kind = pl.program_id(0)
     chunk = HEAD // 4
-    tall = own_ref.shape[0] // 4
-    heads = tall // HEAD
-
-    def rows_of(ref):
-        parts = []
-        for head in range(heads):
-            for j in range(4):
-                at = (j ^ plane) * tall + head * HEAD + kind * chunk
-                parts.append(ref[pl.ds(pl.multiple_of(at, chunk), chunk), :])
-        return jnp.concatenate(parts, axis=0).astype(F32)
-
-    for flag, ref in ((1, own_ref), (0, other_ref)):
-
-        @pl.when(jnp.logical_and(inside == flag, kind < 3))
-        def _(ref=ref):
-            qkv_ref[0] = rows_of(ref)
-
-        @pl.when(jnp.logical_and(inside == flag, kind == 3))
-        def _(ref=ref):
-            out_ref[...] = rows_of(ref)
-
-
-def unpack(inside, plane, own, other, tall):
-    width = own.shape[1]
+    heads = pieces[0].shape[0] // HEAD
+
+    for plane in range(4):
+
+        @pl.when(plane_ref[0] == plane)
+        def _(plane=plane):
+            parts = []
+            for head in range(heads):
+                at = pl.multiple_of(head * HEAD + kind * chunk, chunk)
+                parts += [pieces[j ^ plane][pl.ds(at, chunk), :] for j in range(4)]
+            rows = jnp.concatenate(parts, axis=0).astype(F32)
+
+            @pl.when(kind < 3)
+            def _():
+                qkv_ref[0] = rows
+
+            @pl.when(kind == 3)
+            def _():
+                out_ref[...] = rows
+
+
+def unpack(plane, pieces):
+    tall, width = pieces[0].shape
     return pl.pallas_call(
         unpack_kernel,
         grid=(4,),
         in_specs=[
             pl.BlockSpec(memory_space=pltpu.SMEM),
-            pl.BlockSpec((4 * tall, width), lambda i: (0, 0)),
-            pl.BlockSpec((4 * tall, width), lambda i: (0, 0)),
+            *[pl.BlockSpec((tall, width), lambda i: (0, 0)) for _ in pieces],
         ],
         out_specs=[
             pl.BlockSpec((1, tall, width), lambda i: (jnp.minimum(i, 2), 0, 0)),
@@ -295,7 +293,45 @@
             jax.ShapeDtypeStruct((tall, width), F32),
         ],
         name="unpack",
-    )(jnp.stack([inside.astype(jnp.int32), plane]), own, other)
+    )(plane[None], *pieces)
+
+
+def unpack_ffn_kernel(where_ref, own_ref, other_ref, up_ref, down_ref):
+    half, plane = where_ref[0], where_ref[1]
+    quarter = up_ref.shape[1] // 4
+
+    def rows_of(ref, first):
+        parts = [ref[j ^ plane, first : first + quarter, :] for j in range(4)]
+        return jnp.concatenate(parts, axis=0).astype(F32)
+
+    for mine, ref in ((True, own_ref), (False, other_ref)):
+
+        @pl.when((pl.program_id(0) == half) == mine)
+        def _(ref=ref):
+            up_ref[...] = jnp.transpose(rows_of(ref, 0))
+            down_ref[...] = rows_of(ref, quarter)
+
+
+def unpack_ffn(half, plane, own, other, quarter):
+    width = own.shape[2]
+    return pl.pallas_call(
+        unpack_ffn_kernel,
+        grid=(2,),
+        in_specs=[
+            pl.BlockSpec(memory_space=pltpu.SMEM),
+            pl.BlockSpec(own.shape, lambda i: (0, 0, 0)),
+            pl.BlockSpec(own.shape, lambda i: (0, 0, 0)),
+        ],
+        out_specs=[
+            pl.BlockSpec((width, 4 * quarter), lambda i: (0, i)),
+            pl.BlockSpec((4 * quarter, width), lambda i: (i, 0)),
+        ],
+        out_shape=[
+            jax.ShapeDtypeStruct((width, 8 * quarter), F32),
+            jax.ShapeDtypeStruct((8 * quarter, width), F32),
+        ],
+        name="unpack_ffn",
+    )(jnp.stack([half, plane]), own, other)
 
 
 class Links:
@@ -387,8 +423,7 @@
     def pair_cross(self, array):
         return self.permute(array, lambda e, c, z: (e, c, z ^ 3) if z // 2 != c else None)
 
-    def halves_in_order(self, mine):
-        other = self.other_half(mine)
+    def halves_in_order(self, mine, other):
         first = self.half == 0
         return jnp.stack([jnp.where(first, mine, other), jnp.where(first, other, mine)])
 
@@ -684,18 +719,26 @@
             mine = mine + part[:tall].astype(F32)
             sums = merge(sums, exact_sum(part[tall:]))
         mine, input_part = sync(mine.astype(BF16), input_part)
-        proj_all = links.spread(mine, lambda c, z: z // 2 == c)
+        sent = jnp.concatenate([mine, exact_parts(sums)])
+        sent = jnp.where(links.inside, sent, links.other_half(sent))
+        sums = exact_sum(sent[tall:])
+        proj_all = links.spread(sent[:tall])
         ffn_mine = (ffn_low[0] + ffn_in.astype(F32)).astype(BF16)
-        ffn_all = links.spread(ffn_mine)
-        proj_all, ffn_all = sync(proj_all, ffn_all)
-        proj_all = jnp.concatenate([*proj_all, exact_parts(sums)])
-        proj_other = links.other_half(proj_all)
-        sums = exact_sum(jnp.where(links.inside, proj_all[4 * tall :], proj_other[4 * tall :]))
-        grad_qkv, grad_out = unpack(links.inside, links.plane, proj_all, proj_other, tall)
+        ffn_all = jnp.stack(links.spread(ffn_mine))
+        ffn_other = links.other_half(ffn_all)
+        proj_all, ffn_all, ffn_other = sync(proj_all, ffn_all, ffn_other)
+        grad_qkv, grad_out = unpack(links.plane, proj_all)
         grad_qkv = jnp.swapaxes(grad_qkv, 1, 2)
-        ffn_all = links.halves_in_order(links.in_order(ffn_all))
+        grad_in, grad_down = unpack_ffn(links.half, links.plane, ffn_all, ffn_other, quarter)
+        grad_b_in = links.halves_in_order(
+            links.in_order(list(ffn_all[:, 2 * quarter, :quarter])),
+            links.in_order(list(ffn_other[:, 2 * quarter, :quarter])),
+        ).reshape(units)
     else:
         ffn_all = plain_all(links, ffn_grads.swapaxes(0, 1))
+        grad_in = ffn_all[:, :, :quarter].reshape(units, width).T
+        grad_down = ffn_all[:, :, quarter : 2 * quarter].reshape(units, width)
+        grad_b_in = ffn_all[:, :, 2 * quarter, :quarter].reshape(units)
         grads = plain_pair(links, grad_w.reshape(4, 2, -1, width))
         grads = grads.reshape(4, heads, 4, chunk, width).transpose(2, 1, 0, 3, 4)
         grads = grads.reshape(4, local, width)
@@ -712,7 +755,6 @@
     maxima = sums[6, :4]
     new_scale = DECAY * act_scale + (1.0 - DECAY) * maxima
 
-    up_grads, down_grads = ffn_all[:, :, :quarter], ffn_all[:, :, quarter : 2 * quarter]
     grad_bias_qv = lax.dynamic_index_in_dim(
         sums[7].reshape(2, 2, local), links.depth % 2, 1, False
     )
@@ -725,9 +767,9 @@
         sums[0],
         sums[1],
         sums[2],
-        up_grads.reshape(units, width).astype(F32).T,
-        ffn_all[:, :, 2 * quarter, :quarter].reshape(units).astype(F32),
-        down_grads.reshape(units, width).astype(F32),
+        grad_in,
+        grad_b_in.astype(F32),
+        grad_down,
         sums[3],
         sums[4],
         sums[5],

time: 331 us -> 319 us (0.964)
  waiting for transfers between devices: 83.9 us -> 72.9 us
  other arithmetic: 49.1 us -> 45.1 us
  Pallas kernels: 53.6 us -> 57.3 us
  local copies, waits for them, and re-layouts: 25.5 us -> 22.1 us
    ppermute x48, waiting for transfers between devices: 83.9 us -> 72.9 us  [permute(): return lax.ppermute(array, JOINT, pairs)]
    unnamed x133 -> x124, local copies, waits for them, and re-layouts: 13.1 us -> 8.62 us
    pallas_call x0 -> x1, Pallas kernels: none -> 4.12 us  [unpack_ffn(): pl.pallas_call(unpack_ffn_kernel, grid=(2,), in_specs=[pl.BlockSpec(memor...]
  transfers between devices with their start and end apart: 48 -> 48, of which waited for: 18 -> 18; matrix products, arithmetic and copies ran while one was open for 17% -> 19% of each run, Pallas kernels for 16% -> 16%
where the time goes in v3:
time: 319 us; the launch traced here: 313 us
  waiting for transfers between devices  72.9 us (23%)
  starting transfers between devices  70.7 us (22%)
  Pallas kernels  57.3 us (18%)
  other arithmetic  45.1 us (14%)
  matrix products  39.4 us (12%)
  local copies, waits for them, and re-layouts  22.1 us (7%)
  between operations  5.05 us (2%)
    ppermute x48, waiting for transfers between devices, permute(): return lax.ppermute(array, JOINT, pairs)  72.9 us
    ppermute x48, starting transfers between devices, permute(): return lax.ppermute(array, JOINT, pairs)  70.7 us
    pallas_call x2, Pallas kernels, attend_back(): pl.pallas_call(body, grid=(n,), in_specs=[pl.BlockSpec((LEN, 2 * HEAD), l...  31.6 us
    pallas_call x1, Pallas kernels, attend(): pl.pallas_call(attend_kernel, grid=(n,), in_specs=[pl.BlockSpec((LEN, 2 *...  18.2 us
    dot_general x3, matrix products, nt(): lax.dot_general(a, b, (((1,), (1,)), ((), ())), preferred_element_type=F32)  17.4 us
    dot_general x8, matrix products, nn(): lax.dot_general(a, b, (((1,), (0,)), ((), ())), preferred_element_type=F32)  13.5 us
    unnamed x124, local copies, waits for them, and re-layouts  8.62 us
    dot_general x2, matrix products, tn(): lax.dot_general(a, b, (((0,), (0,)), ((), ())), preferred_element_type=F32)  8.5 us
  transfers between devices with their start and end apart: 48, of which 18 were waited for; matrix products, arithmetic and copies ran while one was open for 19% of the time, Pallas kernels for 16%

profile of v3, /device:TPU:1, one launch (start us, length us, event | category | flops | bytes accessed | tf_op | source)
XLA Modules:
  0.0 312.5 jit_solution(7780497833966324678)
XLA Ops:
  10.2 6.9 %collective-permute-done.1 = bf16[200,768]{1,0:T(8,128)(2,1)} collective-permute-done((bf16[200,768]{1,0:T(8,128)(2,1)S(1)}, bf16[200,768]{1,0:T(8,128)(2,1)}, u32[]{:S(2)}, u32[]{:S(2)}) %collective-permute-start.1) | collective-permute-done | bytes 307232 | tf_op jit(solution)/shard_map/ppermute | solution.py:356
  17.1 7.9 %collective-permute-done = bf16[200,768]{1,0:T(8,128)(2,1)} collective-permute-done((bf16[200,768]{1,0:T(8,128)(2,1)S(1)}, bf16[200,768]{1,0:T(8,128)(2,1)}, u32[]{:S(2)}, u32[]{:S(2)}) %collective-permute-start) | collective-permute-done | bytes 307232 | tf_op jit(solution)/shard_map/ppermute | solution.py:356
  31.6 3.1 collective-permute-start.7
  36.0 6.7 %collective-permute-done.7 = bf16[200,768]{1,0:T(8,128)(2,1)S(1)} collective-permute-done((bf16[200,768]{1,0:T(8,128)(2,1)S(1)}, bf16[200,768]{1,0:T(8,128)(2,1)S(1)}, u32[]{:S(2)}, u32[]{:S(2)}) %collective-permute-start.7) | collective-permute-done | bytes 307232 | tf_op jit(solution)/shard_map/ppermute | solution.py:356
  42.7 3.1 %collective-permute-start.10 = (bf16[200,768]{1,0:T(8,128)(2,1)S(1)}, bf16[200,768]{1,0:T(8,128)(2,1)S(1)}, u32[]{:S(2)}, u32[]{:S(2)}) collective-permute-start(bf16[200,768]{1,0:T(8,128)(2,1)S(1)} %bitcast.203), channel_id=1, source_target_pairs={{0,1},{1,0},{2,3},{3,2},{4,5},{5,4},{6,7},{7,6},{8,9},{9,8},{10,11... | collective-permute-start | bytes 921608 | tf_op jit(solution)/shard_map/ppermute | solution.py:356
  58.3 5.7 %add_convert_fusion.q_ref.k_ref.v_ref.refs_0_.refs_1_.refs_2_ = bf16[1024,1152]{1,0:T(8,128)(2,1)} fusion(bf16[1152,768]{1,0:T(8,128)(2,1)S(1)} %bitcast.197, f32[1152]{0:T(1024)S(1)} %add.291, bf16[512,768]{1,0:T(8,128)(2,1)} %collective-permute-done.4.refs_6_, bf16[512,768]{1,0:T(8,128)(2,1)} %fusion.18.refs_5_), kind=kOutput, calls=%fused_computation.16 | convolution fusion | flops 1817444352 | bytes 5706240 | tf_op jit(solution)/shard_map/dot_general | solution.py:42
  64.0 9.1 %collective-permute-start.13 = (bf16[512,768]{1,0:T(8,128)(2,1)}, bf16[512,768]{1,0:T(8,128)(2,1)}, u32[]{:S(2)}, u32[]{:S(2)}) collective-permute-start(bf16[512,768]{1,0:T(8,128)(2,1)} %param.33), channel_id=1, source_target_pairs={{1,4},{3,6},{4,1},{6,3},{9,12},{11,14},{12,9},{14,11},{17,20},{19,... | collective-permute-start | bytes 2359304 | tf_op jit(solution)/shard_map/ppermute | solution.py:356
  76.4 18.2 %attend.1 = (f32[1024,384]{1,0:T(8,128)}, f32[3,2,1024]{2,1,0:T(2,128)}) custom-call(bf16[1024,1152]{1,0:T(8,128)(2,1)} %add_convert_fusion.q_ref.k_ref.v_ref.refs_0_.refs_1_.refs_2_, bf16[1024,1152]{1,0:T(8,128)(2,1)} %add_convert_fusion.q_ref.k_ref.v_ref.refs_0_.refs_1_.refs_2_, ...), custom_call_target="tpu_custom_call" | custom-call | tf_op jit(solution)/shard_map/attend/pallas_call | solution.py:87
  111.0 6.5 %collective-permute-done.18 = bf16[3,96,768]{2,1,0:T(8,128)(2,1)S(1)} collective-permute-done((bf16[3,96,768]{2,1,0:T(8,128)(2,1)S(1)}, bf16[3,96,768]{2,1,0:T(8,128)(2,1)S(1)}, u32[]{:S(2)}, u32[]{:S(2)}) %collective-permute-start.18) | collective-permute-done | bytes 442400 | tf_op jit(solution)/shard_map/ppermute | solution.py:356
  126.5 4.0 %minimum_convert_fusion = (bf16[1024,1536]{1,0:T(8,128)(2,1)S(1)}, f32[1024,1536]{1,0:T(8,128)S(1)}) fusion(f32[1536]{0:T(1024)S(1)} %reshape.475, bf16[]{:T(256)S(6)} %neg.14, f32[]{:T(128)} %bitcast.36, bf16[1536,768]{1,0:T(8,128)(2,1)S(1)} %bitcast.192, bf16[512,768]{1,0:T(8,128)(2,1)S(1)} %collective-permute-done.17, ...), kind=kOutput, calls=%fused_computation.11 | convolution fusion | flops 2434793472 | bytes 13375494 | tf_op jit(solution)/shard_map/dot_general | solution.py:42
  143.6 7.7 %fusion.80 = (bf16[1024,1536]{1,0:T(8,128)(2,1)}, bf16[1536]{0:T(1024)(128)(2,1)S(1)}) fusion(f32[]{:T(128)} %bitcast.36, f32[1024,1536]{1,0:T(8,128)S(1)} %get-tuple-element.223, f32[1536]{0:T(1024)S(1)} %reshape.475, bf16[1536,768]{1,0:T(8,128)(2,1)S(1)} %bitcast.191, bf16[512,768]{1,0:T(8,128)(2,1)S(1)} %collective-permute-done.22, ...), kind=kOutput, calls=%fused_computation.271 | convolution fusion | flops 2444229120 | bytes 13378564 | tf_op jit(solution)/shard_map/dot_general | solution.py:42
  151.4 5.1 %convolution_convert_fusion.1 = bf16[1536,768]{1,0:T(8,128)(2,1)S(1)} fusion(bf16[1024,1536]{1,0:T(8,128)(2,1)} %get-tuple-element.95, bf16[512,768]{1,0:T(8,128)(2,1)} %copy-done.52, bf16[512,768]{1,0:T(8,128)(2,1)} %copy-done.33), kind=kOutput, calls=%fused_computation.18 | convolution fusion | flops 2420244480 | bytes 7077888 | tf_op jit(solution)/shard_map/dot_general | solution.py:50
  156.6 3.4 %convolution_convert_fusion = bf16[1536,768]{1,0:T(8,128)(2,1)S(1)} fusion(bf16[1024,1536]{1,0:T(8,128)(2,1)S(1)} %copy-done.56, bf16[512,768]{1,0:T(8,128)(2,1)S(1)} %copy-done.54, bf16[512,768]{1,0:T(8,128)(2,1)S(1)} %copy-done.35), kind=kOutput, calls=%fused_computation.17 | convolution fusion | flops 2420244480 | bytes 7077888 | tf_op jit(solution)/shard_map/dot_general | solution.py:50
  177.1 3.4 %collective-permute-start.21 = (bf16[512,768]{1,0:T(8,128)(2,1)S(1)}, bf16[512,768]{1,0:T(8,128)(2,1)}, u32[]{:S(2)}, u32[]{:S(2)}) collective-permute-start(bf16[512,768]{1,0:T(8,128)(2,1)S(1)} %copy-done.19), channel_id=1, source_target_pairs={{1,4},{3,6},{4,1},{6,3},{9,12},{11,14},{12,9},{14,11},{17,20},{19,... | collective-permute-start | bytes 2359304 | tf_op jit(solution)/shard_map/ppermute | solution.py:356
  180.6 19.9 %attend_back.2 = (bf16[1024,768]{1,0:T(8,128)(2,1)}, bf16[4,384,768]{2,1,0:T(8,128)(2,1)}, f32[2,2,128]{2,1,0:T(2,128)}) custom-call(bf16[1024,1152]{1,0:T(8,128)(2,1)} %add_convert_fusion.q_ref.k_ref.v_ref.refs_0_.refs_1_.refs_2_, bf16[1024,1152]{1,0:T(8,128)(2,1)} %add_convert_fusion.q_ref.k_ref.v_ref.refs_0_.refs_1_.refs_2_, ...), custom_call_target="tpu_custom_call" | custom-call | tf_op jit(solution)/shard_map/attend_back/pallas_call | solution.py:212
  204.8 11.7 %attend_back.3 = (bf16[1024,384]{1,0:T(8,128)(2,1)}, bf16[4,384,768]{2,1,0:T(8,128)(2,1)}, f32[1,2,128]{2,1,0:T(2,128)}) custom-call(bf16[1024,1152]{1,0:T(8,128)(2,1)} %add_convert_fusion.q_ref.k_ref.v_ref.refs_0_.refs_1_.refs_2_, bf16[1024,1152]{1,0:T(8,128)(2,1)} %add_convert_fusion.q_ref.k_ref.v_ref.refs_0_.refs_1_.refs_2_, ...), custom_call_target="tpu_custom_call", output_to_operand_aliasing={{1}: (13, {})} | custom-call | flops 9663676416 | bytes 4718592 | tf_op jit(solution)/shard_map/attend_back/pallas_call | solution.py:212
  229.5 9.1 %collective-permute-done.30 = bf16[408,768]{1,0:T(8,128)(2,1)S(1)} collective-permute-done((bf16[408,768]{1,0:T(8,128)(2,1)S(1)}, bf16[408,768]{1,0:T(8,128)(2,1)S(1)}, u32[]{:S(2)}, u32[]{:S(2)}) %collective-permute-start.30) | collective-permute-done | bytes 626720 | tf_op jit(solution)/shard_map/ppermute | solution.py:356
  239.1 13.4 %collective-permute-done.32 = bf16[408,768]{1,0:T(8,128)(2,1)S(1)} collective-permute-done((bf16[408,768]{1,0:T(8,128)(2,1)S(1)}, bf16[408,768]{1,0:T(8,128)(2,1)S(1)}, u32[]{:S(2)}, u32[]{:S(2)}) %collective-permute-start.32) | collective-permute-done | bytes 626720 | tf_op jit(solution)/shard_map/ppermute | solution.py:356
  259.5 6.5 %collective-permute-start.35 = (bf16[216,768]{1,0:T(8,128)(2,1)S(1)}, bf16[216,768]{1,0:T(8,128)(2,1)S(1)}, u32[]{:S(2)}, u32[]{:S(2)}) collective-permute-start(bf16[216,768]{1,0:T(8,128)(2,1)S(1)} %get-tuple-element.195), channel_id=1, source_target_pairs={{2,1},{3,0},{4,7},{5,6},{10,9},{11,8},{12,15},{13,14},{18,17},{19,... | collective-permute-start | bytes 995336 | tf_op jit(solution)/shard_map/ppermute | solution.py:356
  275.3 6.7 %collective-permute-start.38 = (bf16[216,768]{1,0:T(8,128)(2,1)S(1)}, bf16[216,768]{1,0:T(8,128)(2,1)S(1)}, u32[]{:S(2)}, u32[]{:S(2)}) collective-permute-start(bf16[216,768]{1,0:T(8,128)(2,1)S(1)} %pad_maximum_fusion.28), channel_id=1, source_target_pairs={{0,4},{1,5},{2,6},{3,7},{4,0},{5,1},{6,2},{7,3},{8,12},{9,13},{10,... | collective-permute-start | bytes 995336 | tf_op jit(solution)/shard_map/ppermute | solution.py:356
  284.9 3.0 collective-permute-start.37
  292.7 6.0 %collective-permute-done.37 = bf16[512,768]{1,0:T(8,128)(2,1)S(1)} collective-permute-done((bf16[512,768]{1,0:T(8,128)(2,1)}, bf16[512,768]{1,0:T(8,128)(2,1)S(1)}, u32[]{:S(2)}, u32[]{:S(2)}) %collective-permute-start.37) | collective-permute-done | bytes 786464 | tf_op jit(solution)/shard_map/ppermute | solution.py:356
  304.7 4.1 %unpack_ffn.1 = (f32[768,768]{1,0:T(8,128)}, f32[768,768]{1,0:T(8,128)}) custom-call(s32[2]{0:T(128)} %pad_add_fusion.where_ref, bf16[4,200,768]{2,1,0:T(8,128)(2,1)} %copy-done.14, bf16[4,200,768]{2,1,0:T(8,128)(2,1)} %collective-permute-done.47.other_ref), custom_call_target="tpu_custom_call" | custom-call | tf_op jit(solution)/shard_map/unpack_ffn/pallas_call | solution.py:317
  308.8 3.4 %unpack.1 = (f32[3,192,768]{2,1,0:T(8,128)}, f32[192,768]{1,0:T(8,128)}) custom-call(s32[1]{0:T(128)} %bitcast.57.plane_ref, bf16[192,768]{1,0:T(8,128)(2,1)} %copy-done.30, bf16[192,768]{1,0:T(8,128)(2,1)} %copy-done.38, bf16[192,768]{1,0:T(8,128)(2,1)} %copy-done.37, bf16[192,768]{1,0:T(8,128)(2,1)} %copy-done.36), custom_call_target="tpu_custom_call" | custom-call | tf_op jit(solution)/shard_map/unpack/pallas_call | solution.py:280
  (368 shorter events, 132.9 us)
Async XLA Ops:
  5.9 19.2 %collective-permute-start = (bf16[200,768]{1,0:T(8,128)(2,1)S(1)}, bf16[200,768]{1,0:T(8,128)(2,1)}, u32[]{:S(2)}, u32[]{:S(2)}) collective-permute-start(bf16[200,768]{1,0:T(8,128)(2,1)S(1)} %fusion.53), channel_id=1, source_target_pairs={{0,2},{1,3},{6,4},{7,5},{8,10},{9,11},{14,12},{15,13},{16,18},{17,... | collective-permute-start | bytes 921608 | tf_op jit(solution)/shard_map/ppermute | solution.py:356
  25.0 23.4 %collective-permute-start.3 = (bf16[512,768]{1,0:T(8,128)(2,1)S(1)}, bf16[512,768]{1,0:T(8,128)(2,1)}, u32[]{:S(2)}, u32[]{:S(2)}) collective-permute-start(bf16[512,768]{1,0:T(8,128)(2,1)S(1)} %copy-done.32), channel_id=1, source_target_pairs={{1,4},{3,6},{4,1},{6,3},{9,12},{11,14},{12,9},{14,11},{17,20},{19,... | collective-permute-start | bytes 2359304 | tf_op jit(solution)/shard_map/ppermute | solution.py:356
  29.1 13.5 %collective-permute-start.5 = (bf16[2,200,768]{2,1,0:T(8,128)(2,1)}, bf16[2,200,768]{2,1,0:T(8,128)(2,1)S(1)}, u32[]{:S(2)}, u32[]{:S(2)}) collective-permute-start(bf16[2,200,768]{2,1,0:T(8,128)(2,1)} %get-tuple-element.193), channel_id=1, source_target_pairs={{0,8},{1,9},{2,10},{3,11},{4,12},{5,13},{6,14},{7,15},{8,0},{9,1},... | collective-permute-start | bytes 1843208 | tf_op jit(solution)/shard_map/ppermute | solution.py:356
  64.0 30.6 %collective-permute-start.13 = (bf16[512,768]{1,0:T(8,128)(2,1)}, bf16[512,768]{1,0:T(8,128)(2,1)}, u32[]{:S(2)}, u32[]{:S(2)}) collective-permute-start(bf16[512,768]{1,0:T(8,128)(2,1)} %param.33), channel_id=1, source_target_pairs={{1,4},{3,6},{4,1},{6,3},{9,12},{11,14},{12,9},{14,11},{17,20},{19,... | collective-permute-start | bytes 2359304 | tf_op jit(solution)/shard_map/ppermute | solution.py:356
  74.5 24.6 %collective-permute-start.15 = (bf16[3,200,768]{2,1,0:T(8,128)(2,1)}, bf16[3,200,768]{2,1,0:T(8,128)(2,1)}, u32[]{:S(2)}, u32[]{:S(2)}) collective-permute-start(bf16[3,200,768]{2,1,0:T(8,128)(2,1)} %pad_maximum_fusion.20), channel_id=1, source_target_pairs={{0,16},{1,17},{2,18},{3,19},{4,20},{5,21},{6,22},{7,23},{8,24},{9,... | collective-permute-start | bytes 2764808 | tf_op jit(solution)/shard_map/ppermute | solution.py:356
  75.0 24.2 %collective-permute-start.14 = (bf16[3,200,768]{2,1,0:T(8,128)(2,1)}, bf16[3,200,768]{2,1,0:T(8,128)(2,1)}, u32[]{:S(2)}, u32[]{:S(2)}) collective-permute-start(bf16[3,200,768]{2,1,0:T(8,128)(2,1)} %pad_maximum_fusion.20), channel_id=1, source_target_pairs={{0,8},{1,9},{2,10},{3,11},{4,12},{5,13},{6,14},{7,15},{8,0},{9,1},... | collective-permute-start | bytes 2764808 | tf_op jit(solution)/shard_map/ppermute | solution.py:356
  99.1 19.7 %collective-permute-start.16 = (f32[512,768]{1,0:T(8,128)S(1)}, f32[512,768]{1,0:T(8,128)}, u32[]{:S(2)}, u32[]{:S(2)}) collective-permute-start(f32[512,768]{1,0:T(8,128)S(1)} %fusion.48), channel_id=1, source_target_pairs={{0,4},{1,5},{2,6},{3,7},{4,0},{5,1},{6,2},{7,3},{8,12},{9,13},{10,... | collective-permute-start | bytes 4718600 | tf_op jit(solution)/shard_map/ppermute | solution.py:356
  102.3 15.2 %collective-permute-start.19 = (bf16[3,104,768]{2,1,0:T(8,128)(2,1)S(1)}, bf16[3,104,768]{2,1,0:T(8,128)(2,1)S(1)}, u32[]{:S(2)}, u32[]{:S(2)}) collective-permute-start(bf16[3,104,768]{2,1,0:T(8,128)(2,1)S(1)} %slice.319), channel_id=1, source_target_pairs={{0,16},{1,17},{2,18},{3,19},{4,20},{5,21},{6,22},{7,23},{8,24},{9,... | collective-permute-start | bytes 1437704 | tf_op jit(solution)/shard_map/ppermute | solution.py:356
  166.0 34.5 %collective-permute-start.26 = (bf16[2,2,200,768]{3,2,1,0:T(8,128)(2,1)}, bf16[2,2,200,768]{3,2,1,0:T(8,128)(2,1)}, u32[]{:S(2)}, u32[]{:S(2)}) collective-permute-start(bf16[2,2,200,768]{3,2,1,0:T(8,128)(2,1)} %get-tuple-element.170), channel_id=1, source_target_pairs={{0,16},{1,17},{2,18},{3,19},{4,20},{5,21},{6,22},{7,23},{8,24},{9,... | collective-permute-start | bytes 3686408 | tf_op jit(solution)/shard_map/ppermute | solution.py:356
  166.4 34.1 %collective-permute-start.25 = (bf16[2,2,200,768]{3,2,1,0:T(8,128)(2,1)}, bf16[2,2,200,768]{3,2,1,0:T(8,128)(2,1)}, u32[]{:S(2)}, u32[]{:S(2)}) collective-permute-start(bf16[2,2,200,768]{3,2,1,0:T(8,128)(2,1)} %get-tuple-element.171), channel_id=1, source_target_pairs={{0,8},{1,9},{2,10},{3,11},{4,12},{5,13},{6,14},{7,15},{8,0},{9,1},... | collective-permute-start | bytes 3686408 | tf_op jit(solution)/shard_map/ppermute | solution.py:356
  177.1 104.9 %collective-permute-start.21 = (bf16[512,768]{1,0:T(8,128)(2,1)S(1)}, bf16[512,768]{1,0:T(8,128)(2,1)}, u32[]{:S(2)}, u32[]{:S(2)}) collective-permute-start(bf16[512,768]{1,0:T(8,128)(2,1)S(1)} %copy-done.19), channel_id=1, source_target_pairs={{1,4},{3,6},{4,1},{6,3},{9,12},{11,14},{12,9},{14,11},{17,20},{19,... | collective-permute-start | bytes 2359304 | tf_op jit(solution)/shard_map/ppermute | solution.py:356
  203.2 15.3 %collective-permute-start.27 = (bf16[2,200,768]{2,1,0:T(8,128)(2,1)}, bf16[2,200,768]{2,1,0:T(8,128)(2,1)}, u32[]{:S(2)}, u32[]{:S(2)}) collective-permute-start(bf16[2,200,768]{2,1,0:T(8,128)(2,1)} %get-tuple-element.107), channel_id=1, source_target_pairs={{0,8},{1,9},{2,10},{3,11},{4,12},{5,13},{6,14},{7,15},{8,0},{9,1},... | collective-permute-start | bytes 1843208 | tf_op jit(solution)/shard_map/ppermute | solution.py:356
  203.9 15.4 %collective-permute-start.28 = (bf16[2,200,768]{2,1,0:T(8,128)(2,1)S(1)}, bf16[2,200,768]{2,1,0:T(8,128)(2,1)}, u32[]{:S(2)}, u32[]{:S(2)}) collective-permute-start(bf16[2,200,768]{2,1,0:T(8,128)(2,1)S(1)} %get-tuple-element.108), channel_id=1, source_target_pairs={{0,16},{1,17},{2,18},{3,19},{4,20},{5,21},{6,22},{7,23},{8,24},{9,... | collective-permute-start | bytes 1843208 | tf_op jit(solution)/shard_map/ppermute | solution.py:356
  223.2 15.4 %collective-permute-start.30 = (bf16[408,768]{1,0:T(8,128)(2,1)S(1)}, bf16[408,768]{1,0:T(8,128)(2,1)S(1)}, u32[]{:S(2)}, u32[]{:S(2)}) collective-permute-start(bf16[408,768]{1,0:T(8,128)(2,1)S(1)} %get-tuple-element.196), channel_id=1, source_target_pairs={{0,8},{1,9},{2,10},{3,11},{4,12},{5,13},{6,14},{7,15},{8,0},{9,1},... | collective-permute-start | bytes 1880072 | tf_op jit(solution)/shard_map/ppermute | solution.py:356
  223.8 15.4 %collective-permute-start.31 = (bf16[408,768]{1,0:T(8,128)(2,1)S(1)}, bf16[408,768]{1,0:T(8,128)(2,1)S(1)}, u32[]{:S(2)}, u32[]{:S(2)}) collective-permute-start(bf16[408,768]{1,0:T(8,128)(2,1)S(1)} %get-tuple-element.197), channel_id=1, source_target_pairs={{0,16},{1,17},{2,18},{3,19},{4,20},{5,21},{6,22},{7,23},{8,24},{9,... | collective-permute-start | bytes 1880072 | tf_op jit(solution)/shard_map/ppermute | solution.py:356
  224.9 27.6 %collective-permute-start.32 = (bf16[408,768]{1,0:T(8,128)(2,1)S(1)}, bf16[408,768]{1,0:T(8,128)(2,1)S(1)}, u32[]{:S(2)}, u32[]{:S(2)}) collective-permute-start(bf16[408,768]{1,0:T(8,128)(2,1)S(1)} %get-tuple-element.198), channel_id=1, source_target_pairs={{0,24},{1,25},{2,26},{3,27},{4,28},{5,29},{6,30},{7,31},{8,16},{9,... | collective-permute-start | bytes 1880072 | tf_op jit(solution)/shard_map/ppermute | solution.py:356
  228.3 27.5 %collective-permute-start.42 = (bf16[2,200,768]{2,1,0:T(8,128)(2,1)S(1)}, bf16[2,200,768]{2,1,0:T(8,128)(2,1)S(1)}, u32[]{:S(2)}, u32[]{:S(2)}) collective-permute-start(bf16[2,200,768]{2,1,0:T(8,128)(2,1)S(1)} %get-tuple-element.166), channel_id=1, source_target_pairs={{0,2},{1,3},{2,0},{3,1},{4,6},{5,7},{6,4},{7,5},{8,10},{9,11},{10,... | collective-permute-start | bytes 1843208 | tf_op jit(solution)/shard_map/ppermute | solution.py:356
  258.9 13.5 %collective-permute-start.36 = (f32[512,768]{1,0:T(8,128)S(1)}, f32[512,768]{1,0:T(8,128)S(1)}, u32[]{:S(2)}, u32[]{:S(2)}) collective-permute-start(f32[512,768]{1,0:T(8,128)S(1)} %fusion.39), channel_id=1, source_target_pairs={{0,4},{1,5},{2,6},{3,7},{4,0},{5,1},{6,2},{7,3},{8,12},{9,13},{10,... | collective-permute-start | bytes 4718600 | tf_op jit(solution)/shard_map/ppermute | solution.py:356
  267.2 16.9 %collective-permute-start.46 = (bf16[200,768]{1,0:T(8,128)(2,1)S(1)}, bf16[200,768]{1,0:T(8,128)(2,1)S(1)}, u32[]{:S(2)}, u32[]{:S(2)}) collective-permute-start(bf16[200,768]{1,0:T(8,128)(2,1)S(1)} %fusion.46), channel_id=1, source_target_pairs={{0,24},{1,25},{2,26},{3,27},{4,28},{5,29},{6,30},{7,31},{8,16},{9,... | collective-permute-start | bytes 921608 | tf_op jit(solution)/shard_map/ppermute | solution.py:356
  270.8 13.3 %collective-permute-start.45 = (bf16[200,768]{1,0:T(8,128)(2,1)S(1)}, bf16[200,768]{1,0:T(8,128)(2,1)S(1)}, u32[]{:S(2)}, u32[]{:S(2)}) collective-permute-start(bf16[200,768]{1,0:T(8,128)(2,1)S(1)} %fusion.46), channel_id=1, source_target_pairs={{0,16},{1,17},{2,18},{3,19},{4,20},{5,21},{6,22},{7,23},{8,24},{9,... | collective-permute-start | bytes 921608 | tf_op jit(solution)/shard_map/ppermute | solution.py:356
  275.3 12.6 %collective-permute-start.38 = (bf16[216,768]{1,0:T(8,128)(2,1)S(1)}, bf16[216,768]{1,0:T(8,128)(2,1)S(1)}, u32[]{:S(2)}, u32[]{:S(2)}) collective-permute-start(bf16[216,768]{1,0:T(8,128)(2,1)S(1)} %pad_maximum_fusion.28), channel_id=1, source_target_pairs={{0,4},{1,5},{2,6},{3,7},{4,0},{5,1},{6,2},{7,3},{8,12},{9,13},{10,... | collective-permute-start | bytes 995336 | tf_op jit(solution)/shard_map/ppermute | solution.py:356
  284.3 18.2 %collective-permute-start.47 = (bf16[4,200,768]{2,1,0:T(8,128)(2,1)S(1)}, bf16[4,200,768]{2,1,0:T(8,128)(2,1)}, u32[]{:S(2)}, u32[]{:S(2)}) collective-permute-start(bf16[4,200,768]{2,1,0:T(8,128)(2,1)S(1)} %pad_maximum_fusion.6.own_ref), channel_id=1, source_target_pairs={{0,4},{1,5},{2,6},{3,7},{4,0},{5,1},{6,2},{7,3},{8,12},{9,13},{10,... | collective-permute-start | bytes 3686408 | tf_op jit(solution)/shard_map/ppermute | solution.py:356
  284.9 13.8 %collective-permute-start.37 = (bf16[512,768]{1,0:T(8,128)(2,1)}, bf16[512,768]{1,0:T(8,128)(2,1)S(1)}, u32[]{:S(2)}, u32[]{:S(2)}) collective-permute-start(bf16[512,768]{1,0:T(8,128)(2,1)} %add_convert_fusion.1), channel_id=1, source_target_pairs={{1,4},{3,6},{4,1},{6,3},{9,12},{11,14},{12,9},{14,11},{17,20},{19,... | collective-permute-start | bytes 2359304 | tf_op jit(solution)/shard_map/ppermute | solution.py:356
  289.4 13.0 %collective-permute-start.40 = (bf16[192,768]{1,0:T(8,128)(2,1)S(1)}, bf16[192,768]{1,0:T(8,128)(2,1)S(1)}, u32[]{:S(2)}, u32[]{:S(2)}) collective-permute-start(bf16[192,768]{1,0:T(8,128)(2,1)S(1)} %slice.440.refs_0_), channel_id=1, source_target_pairs={{0,16},{1,17},{2,18},{3,19},{4,20},{5,21},{6,22},{7,23},{8,24},{9,... | collective-permute-start | bytes 884744 | tf_op jit(solution)/shard_map/ppermute | solution.py:356
  (84 other events, 590.0 us)

commit v4 on v3

--- a/solution.py
+++ b/solution.py
@@ -572,11 +572,12 @@
     upstream = links.rows_home(out_grad)
     context, lse = attend(proj, seg_col, seg_row, heads)
     context, upstream = sync(context, upstream)
+    if links.square:
+        context, ffn_near = sync(context, ffn_near)
     upstream = links.at_home(out_grad, upstream).astype(F32)
     ctx_quant = jnp.clip(context, -act_scale[1], act_scale[1]).astype(BF16)
     attn_part, attn_sent = nn(ctx_quant[:HALF], w_back), nn(ctx_quant[HALF:], w_back)
     if links.square:
-        attn_part, attn_sent, ffn_near = sync(attn_part, attn_sent, ffn_near)
         pieces = links.spread_far(ffn_in, ffn_near)
         ffn_full = jnp.stack(
             [jnp.concatenate([ffn_own[i][None], pieces[j]]) for i, j in enumerate(ORDER)]
@@ -707,12 +708,9 @@
         other = jnp.where(links.even, total[tall:], total[:tall])
         sums_sent = exact_parts(sums)
         other = jnp.concatenate([other.astype(BF16), sums_sent])
-        proj_in = [
-            links.pair_near(other),
-            links.pair_back(jnp.concatenate([mine.astype(BF16), sums_sent])),
-            links.pair_cross(other),
-        ]
-        ffn_in, total = sync(ffn_in, total)
+        sent = jnp.concatenate([mine.astype(BF16), sums_sent])
+        ffn_in, other, sent = sync(ffn_in, other, sent)
+        proj_in = [links.pair_near(other), links.pair_back(sent), links.pair_cross(other)]
         ffn_low = ffn_low + ffn_in.astype(F32)
         ffn_in = links.along(ffn_low[1].astype(BF16), 1)
         for part in proj_in:
@@ -726,10 +724,11 @@
         ffn_mine = (ffn_low[0] + ffn_in.astype(F32)).astype(BF16)
         ffn_all = jnp.stack(links.spread(ffn_mine))
         ffn_other = links.other_half(ffn_all)
-        proj_all, ffn_all, ffn_other = sync(proj_all, ffn_all, ffn_other)
-        grad_qkv, grad_out = unpack(links.plane, proj_all)
+        ffn_all, ffn_other = sync(ffn_all, ffn_other)
+        grad_in, grad_down = unpack_ffn(links.half, links.plane, ffn_all, ffn_other, quarter)
+        own, grad_in, grad_down = sync(proj_all[0], grad_in, grad_down)
+        grad_qkv, grad_out = unpack(links.plane, [own, *proj_all[1:]])
         grad_qkv = jnp.swapaxes(grad_qkv, 1, 2)
-        grad_in, grad_down = unpack_ffn(links.half, links.plane, ffn_all, ffn_other, quarter)
         grad_b_in = links.halves_in_order(
             links.in_order(list(ffn_all[:, 2 * quarter, :quarter])),
             links.in_order(list(ffn_other[:, 2 * quarter, :quarter])),

time: 319 us -> 315 us (0.987)
  waiting for transfers between devices: 72.9 us -> 68.1 us
    ppermute x48, waiting for transfers between devices: 72.9 us -> 68.1 us  [permute(): return lax.ppermute(array, JOINT, pairs)]
    unnamed x124 -> x122, local copies, waits for them, and re-layouts: 8.62 us -> 9 us
  transfers between devices with their start and end apart: 48 -> 48, of which waited for: 18 -> 15; matrix products, arithmetic and copies ran while one was open for 19% -> 18% of each run, Pallas kernels for 16% -> 17%
where the time goes in v4:
time: 315 us; the launch traced here: 309 us
  starting transfers between devices  71.9 us (23%)
  waiting for transfers between devices  68.1 us (22%)
  Pallas kernels  57.2 us (18%)
  other arithmetic  43.7 us (14%)
  matrix products  41 us (13%)
  local copies, waits for them, and re-layouts  22.4 us (7%)
  between operations  5.06 us (2%)
    ppermute x48, starting transfers between devices, permute(): return lax.ppermute(array, JOINT, pairs)  71.9 us
    ppermute x48, waiting for transfers between devices, permute(): return lax.ppermute(array, JOINT, pairs)  68.1 us
    pallas_call x2, Pallas kernels, attend_back(): pl.pallas_call(body, grid=(n,), in_specs=[pl.BlockSpec((LEN, 2 * HEAD), l...  31.6 us
    pallas_call x1, Pallas kernels, attend(): pl.pallas_call(attend_kernel, grid=(n,), in_specs=[pl.BlockSpec((LEN, 2 *...  18.1 us
    dot_general x3, matrix products, nt(): lax.dot_general(a, b, (((1,), (1,)), ((), ())), preferred_element_type=F32)  17.4 us
    dot_general x8, matrix products, nn(): lax.dot_general(a, b, (((1,), (0,)), ((), ())), preferred_element_type=F32)  15.2 us
    unnamed x122, local copies, waits for them, and re-layouts  9 us
    dot_general x2, matrix products, tn(): lax.dot_general(a, b, (((0,), (0,)), ((), ())), preferred_element_type=F32)  8.5 us
  transfers between devices with their start and end apart: 48, of which 15 were waited for; matrix products, arithmetic and copies ran while one was open for 18% of the time, Pallas kernels for 17%

profile of v4, /device:TPU:1, one launch (start us, length us, event | category | flops | bytes accessed | tf_op | source)
XLA Modules:
  0.0 309.4 jit_solution(15448713390442341832)
XLA Ops:
  10.2 7.0 %collective-permute-done.1 = bf16[200,768]{1,0:T(8,128)(2,1)} collective-permute-done((bf16[200,768]{1,0:T(8,128)(2,1)S(1)}, bf16[200,768]{1,0:T(8,128)(2,1)}, u32[]{:S(2)}, u32[]{:S(2)}) %collective-permute-start.1) | collective-permute-done | bytes 307232 | tf_op jit(solution)/shard_map/ppermute | solution.py:356
  17.1 7.9 %collective-permute-done = bf16[200,768]{1,0:T(8,128)(2,1)} collective-permute-done((bf16[200,768]{1,0:T(8,128)(2,1)S(1)}, bf16[200,768]{1,0:T(8,128)(2,1)}, u32[]{:S(2)}, u32[]{:S(2)}) %collective-permute-start) | collective-permute-done | bytes 307232 | tf_op jit(solution)/shard_map/ppermute | solution.py:356
  31.6 3.1 collective-permute-start.7
  36.0 6.6 %collective-permute-done.7 = bf16[200,768]{1,0:T(8,128)(2,1)S(1)} collective-permute-done((bf16[200,768]{1,0:T(8,128)(2,1)S(1)}, bf16[200,768]{1,0:T(8,128)(2,1)S(1)}, u32[]{:S(2)}, u32[]{:S(2)}) %collective-permute-start.7) | collective-permute-done | bytes 307232 | tf_op jit(solution)/shard_map/ppermute | solution.py:356
  42.7 3.1 %collective-permute-start.10 = (bf16[200,768]{1,0:T(8,128)(2,1)S(1)}, bf16[200,768]{1,0:T(8,128)(2,1)S(1)}, u32[]{:S(2)}, u32[]{:S(2)}) collective-permute-start(bf16[200,768]{1,0:T(8,128)(2,1)S(1)} %bitcast.203), channel_id=1, source_target_pairs={{0,1},{1,0},{2,3},{3,2},{4,5},{5,4},{6,7},{7,6},{8,9},{9,8},{10,11... | collective-permute-start | bytes 921608 | tf_op jit(solution)/shard_map/ppermute | solution.py:356
  58.3 5.7 %add_convert_fusion.q_ref.k_ref.v_ref.refs_0_.refs_1_.refs_2_ = bf16[1024,1152]{1,0:T(8,128)(2,1)} fusion(bf16[1152,768]{1,0:T(8,128)(2,1)S(1)} %bitcast.197, f32[1152]{0:T(1024)S(1)} %add.291, bf16[512,768]{1,0:T(8,128)(2,1)} %collective-permute-done.4.refs_6_, bf16[512,768]{1,0:T(8,128)(2,1)} %fusion.18.refs_5_), kind=kOutput, calls=%fused_computation.16 | convolution fusion | flops 1817444352 | bytes 5706240 | tf_op jit(solution)/shard_map/dot_general | solution.py:42
  64.0 6.5 %collective-permute-start.15 = (bf16[3,200,768]{2,1,0:T(8,128)(2,1)}, bf16[3,200,768]{2,1,0:T(8,128)(2,1)}, u32[]{:S(2)}, u32[]{:S(2)}) collective-permute-start(bf16[3,200,768]{2,1,0:T(8,128)(2,1)} %pad_maximum_fusion.20), channel_id=1, source_target_pairs={{0,16},{1,17},{2,18},{3,19},{4,20},{5,21},{6,22},{7,23},{8,24},{9,... | collective-permute-start | bytes 2764808 | tf_op jit(solution)/shard_map/ppermute | solution.py:356
  70.7 3.6 %collective-permute-start.13 = (bf16[512,768]{1,0:T(8,128)(2,1)}, bf16[512,768]{1,0:T(8,128)(2,1)}, u32[]{:S(2)}, u32[]{:S(2)}) collective-permute-start(bf16[512,768]{1,0:T(8,128)(2,1)} %param.33), channel_id=1, source_target_pairs={{1,4},{3,6},{4,1},{6,3},{9,12},{11,14},{12,9},{14,11},{17,20},{19,... | collective-permute-start | bytes 2359304 | tf_op jit(solution)/shard_map/ppermute | solution.py:356
  76.9 18.1 %attend.1 = (f32[1024,384]{1,0:T(8,128)}, f32[3,2,1024]{2,1,0:T(2,128)}) custom-call(bf16[1024,1152]{1,0:T(8,128)(2,1)} %add_convert_fusion.q_ref.k_ref.v_ref.refs_0_.refs_1_.refs_2_, bf16[1024,1152]{1,0:T(8,128)(2,1)} %add_convert_fusion.q_ref.k_ref.v_ref.refs_0_.refs_1_.refs_2_, ...), custom_call_target="tpu_custom_call" | custom-call | tf_op jit(solution)/shard_map/attend/pallas_call | solution.py:87
  95.1 3.1 %minimum_convert_fusion.2 = bf16[1024,384]{1,0:T(8,128)(2,1)} fusion(f32[1024,384]{1,0:T(8,128)} %get-tuple-element.89.refs_8_, bf16[]{:T(256)S(6)} %neg.12, f32[]{:T(128)} %bitcast.14), kind=kLoop, calls=%fused_computation.66 | loop fusion | flops 1966080 | bytes 2359302 | tf_op jit(solution)/shard_map/convert_element_type | solution.py:578
  111.6 5.7 %collective-permute-done.18 = bf16[3,96,768]{2,1,0:T(8,128)(2,1)S(1)} collective-permute-done((bf16[3,96,768]{2,1,0:T(8,128)(2,1)S(1)}, bf16[3,96,768]{2,1,0:T(8,128)(2,1)S(1)}, u32[]{:S(2)}, u32[]{:S(2)}) %collective-permute-start.18) | collective-permute-done | bytes 442400 | tf_op jit(solution)/shard_map/ppermute | solution.py:356
  126.7 4.0 %minimum_convert_fusion = (bf16[1024,1536]{1,0:T(8,128)(2,1)S(1)}, f32[1024,1536]{1,0:T(8,128)S(1)}) fusion(f32[1536]{0:T(1024)S(1)} %reshape.475, bf16[]{:T(256)S(6)} %neg.14, f32[]{:T(128)} %bitcast.36, bf16[1536,768]{1,0:T(8,128)(2,1)S(1)} %bitcast.192, bf16[512,768]{1,0:T(8,128)(2,1)S(1)} %collective-permute-done.17, ...), kind=kOutput, calls=%fused_computation.11 | convolution fusion | flops 2434793472 | bytes 13375494 | tf_op jit(solution)/shard_map/dot_general | solution.py:42
  143.7 7.7 %fusion.78 = (bf16[1024,1536]{1,0:T(8,128)(2,1)}, bf16[1536]{0:T(1024)(128)(2,1)S(1)}) fusion(f32[]{:T(128)} %bitcast.36, f32[1024,1536]{1,0:T(8,128)S(1)} %get-tuple-element.223, f32[1536]{0:T(1024)S(1)} %reshape.475, bf16[1536,768]{1,0:T(8,128)(2,1)S(1)} %bitcast.191, bf16[512,768]{1,0:T(8,128)(2,1)S(1)} %collective-permute-done.22, ...), kind=kOutput, calls=%fused_computation.269 | convolution fusion | flops 2444229120 | bytes 13378564 | tf_op jit(solution)/shard_map/dot_general | solution.py:42
  151.6 5.1 %convolution_convert_fusion.1 = bf16[1536,768]{1,0:T(8,128)(2,1)S(1)} fusion(bf16[1024,1536]{1,0:T(8,128)(2,1)} %get-tuple-element.94, bf16[512,768]{1,0:T(8,128)(2,1)} %copy-done.51, bf16[512,768]{1,0:T(8,128)(2,1)} %copy-done.33), kind=kOutput, calls=%fused_computation.18 | convolution fusion | flops 2420244480 | bytes 7077888 | tf_op jit(solution)/shard_map/dot_general | solution.py:50
  156.7 3.4 %convolution_convert_fusion = bf16[1536,768]{1,0:T(8,128)(2,1)S(1)} fusion(bf16[1024,1536]{1,0:T(8,128)(2,1)S(1)} %copy-done.55, bf16[512,768]{1,0:T(8,128)(2,1)S(1)} %copy-done.53, bf16[512,768]{1,0:T(8,128)(2,1)S(1)} %copy-done.35), kind=kOutput, calls=%fused_computation.17 | convolution fusion | flops 2420244480 | bytes 7077888 | tf_op jit(solution)/shard_map/dot_general | solution.py:50
  180.1 19.9 %attend_back.2 = (bf16[1024,768]{1,0:T(8,128)(2,1)}, bf16[4,384,768]{2,1,0:T(8,128)(2,1)}, f32[2,2,128]{2,1,0:T(2,128)}) custom-call(bf16[1024,1152]{1,0:T(8,128)(2,1)} %add_convert_fusion.q_ref.k_ref.v_ref.refs_0_.refs_1_.refs_2_, bf16[1024,1152]{1,0:T(8,128)(2,1)} %add_convert_fusion.q_ref.k_ref.v_ref.refs_0_.refs_1_.refs_2_, ...), custom_call_target="tpu_custom_call" | custom-call | tf_op jit(solution)/shard_map/attend_back/pallas_call | solution.py:212
  204.3 11.7 %attend_back.3 = (bf16[1024,384]{1,0:T(8,128)(2,1)}, bf16[4,384,768]{2,1,0:T(8,128)(2,1)}, f32[1,2,128]{2,1,0:T(2,128)}) custom-call(bf16[1024,1152]{1,0:T(8,128)(2,1)} %add_convert_fusion.q_ref.k_ref.v_ref.refs_0_.refs_1_.refs_2_, bf16[1024,1152]{1,0:T(8,128)(2,1)} %add_convert_fusion.q_ref.k_ref.v_ref.refs_0_.refs_1_.refs_2_, ...), custom_call_target="tpu_custom_call", output_to_operand_aliasing={{1}: (13, {})} | custom-call | flops 9663676416 | bytes 4718592 | tf_op jit(solution)/shard_map/attend_back/pallas_call | solution.py:212
  228.8 9.3 %collective-permute-done.30 = bf16[408,768]{1,0:T(8,128)(2,1)S(1)} collective-permute-done((bf16[408,768]{1,0:T(8,128)(2,1)S(1)}, bf16[408,768]{1,0:T(8,128)(2,1)S(1)}, u32[]{:S(2)}, u32[]{:S(2)}) %collective-permute-start.30) | collective-permute-done | bytes 626720 | tf_op jit(solution)/shard_map/ppermute | solution.py:356
  239.2 13.2 %collective-permute-done.32 = bf16[408,768]{1,0:T(8,128)(2,1)S(1)} collective-permute-done((bf16[408,768]{1,0:T(8,128)(2,1)S(1)}, bf16[408,768]{1,0:T(8,128)(2,1)S(1)}, u32[]{:S(2)}, u32[]{:S(2)}) %collective-permute-start.32) | collective-permute-done | bytes 626720 | tf_op jit(solution)/shard_map/ppermute | solution.py:356
  258.7 6.5 %collective-permute-start.36 = (bf16[216,768]{1,0:T(8,128)(2,1)S(1)}, bf16[216,768]{1,0:T(8,128)(2,1)S(1)}, u32[]{:S(2)}, u32[]{:S(2)}) collective-permute-start(bf16[216,768]{1,0:T(8,128)(2,1)S(1)} %get-tuple-element.115), channel_id=1, source_target_pairs={{2,1},{3,0},{4,7},{5,6},{10,9},{11,8},{12,15},{13,14},{18,17},{19,... | collective-permute-start | bytes 995336 | tf_op jit(solution)/shard_map/ppermute | solution.py:356
  274.5 6.3 %collective-permute-start.39 = (bf16[216,768]{1,0:T(8,128)(2,1)S(1)}, bf16[216,768]{1,0:T(8,128)(2,1)S(1)}, u32[]{:S(2)}, u32[]{:S(2)}) collective-permute-start(bf16[216,768]{1,0:T(8,128)(2,1)S(1)} %pad_maximum_fusion.28), channel_id=1, source_target_pairs={{0,4},{1,5},{2,6},{3,7},{4,0},{5,1},{6,2},{7,3},{8,12},{9,13},{10,... | collective-permute-start | bytes 995336 | tf_op jit(solution)/shard_map/ppermute | solution.py:356
  291.8 6.2 %collective-permute-done.38 = bf16[512,768]{1,0:T(8,128)(2,1)S(1)} collective-permute-done((bf16[512,768]{1,0:T(8,128)(2,1)}, bf16[512,768]{1,0:T(8,128)(2,1)S(1)}, u32[]{:S(2)}, u32[]{:S(2)}) %collective-permute-start.38) | collective-permute-done | bytes 786464 | tf_op jit(solution)/shard_map/ppermute | solution.py:356
  300.8 4.1 %unpack_ffn.1 = (f32[768,768]{1,0:T(8,128)}, f32[768,768]{1,0:T(8,128)}) custom-call(s32[2]{0:T(128)} %pad_add_fusion.where_ref, bf16[4,200,768]{2,1,0:T(8,128)(2,1)} %copy-done.14, bf16[4,200,768]{2,1,0:T(8,128)(2,1)} %collective-permute-done.44.other_ref), custom_call_target="tpu_custom_call" | custom-call | tf_op jit(solution)/shard_map/unpack_ffn/pallas_call | solution.py:317
  305.8 3.4 %unpack.1 = (f32[3,192,768]{2,1,0:T(8,128)}, f32[192,768]{1,0:T(8,128)}) custom-call(s32[1]{0:T(128)} %bitcast.58.plane_ref, bf16[192,768]{1,0:T(8,128)(2,1)} %copy-done.30, bf16[192,768]{1,0:T(8,128)(2,1)} %collective-permute-done.45.refs_1_, bf16[192,768]{1,0:T(8,128)(2,1)} %copy-done.37, bf16[192,768]{1,0:T(8,128)(2,1)} %copy-done.36), custom_call_target="tpu_custom_call" | custom-call | tf_op jit(solution)/shard_map/unpack/pallas_call | solution.py:280
  (365 shorter events, 133.2 us)
Async XLA Ops:
  5.9 19.1 %collective-permute-start = (bf16[200,768]{1,0:T(8,128)(2,1)S(1)}, bf16[200,768]{1,0:T(8,128)(2,1)}, u32[]{:S(2)}, u32[]{:S(2)}) collective-permute-start(bf16[200,768]{1,0:T(8,128)(2,1)S(1)} %fusion.52), channel_id=1, source_target_pairs={{0,2},{1,3},{6,4},{7,5},{8,10},{9,11},{14,12},{15,13},{16,18},{17,... | collective-permute-start | bytes 921608 | tf_op jit(solution)/shard_map/ppermute | solution.py:356
  25.0 23.4 %collective-permute-start.3 = (bf16[512,768]{1,0:T(8,128)(2,1)S(1)}, bf16[512,768]{1,0:T(8,128)(2,1)}, u32[]{:S(2)}, u32[]{:S(2)}) collective-permute-start(bf16[512,768]{1,0:T(8,128)(2,1)S(1)} %copy-done.32), channel_id=1, source_target_pairs={{1,4},{3,6},{4,1},{6,3},{9,12},{11,14},{12,9},{14,11},{17,20},{19,... | collective-permute-start | bytes 2359304 | tf_op jit(solution)/shard_map/ppermute | solution.py:356
  29.1 13.5 %collective-permute-start.5 = (bf16[2,200,768]{2,1,0:T(8,128)(2,1)}, bf16[2,200,768]{2,1,0:T(8,128)(2,1)S(1)}, u32[]{:S(2)}, u32[]{:S(2)}) collective-permute-start(bf16[2,200,768]{2,1,0:T(8,128)(2,1)} %get-tuple-element.191), channel_id=1, source_target_pairs={{0,8},{1,9},{2,10},{3,11},{4,12},{5,13},{6,14},{7,15},{8,0},{9,1},... | collective-permute-start | bytes 1843208 | tf_op jit(solution)/shard_map/ppermute | solution.py:356
  64.0 31.1 %collective-permute-start.15 = (bf16[3,200,768]{2,1,0:T(8,128)(2,1)}, bf16[3,200,768]{2,1,0:T(8,128)(2,1)}, u32[]{:S(2)}, u32[]{:S(2)}) collective-permute-start(bf16[3,200,768]{2,1,0:T(8,128)(2,1)} %pad_maximum_fusion.20), channel_id=1, source_target_pairs={{0,16},{1,17},{2,18},{3,19},{4,20},{5,21},{6,22},{7,23},{8,24},{9,... | collective-permute-start | bytes 2764808 | tf_op jit(solution)/shard_map/ppermute | solution.py:356
  70.5 24.6 %collective-permute-start.14 = (bf16[3,200,768]{2,1,0:T(8,128)(2,1)}, bf16[3,200,768]{2,1,0:T(8,128)(2,1)}, u32[]{:S(2)}, u32[]{:S(2)}) collective-permute-start(bf16[3,200,768]{2,1,0:T(8,128)(2,1)} %pad_maximum_fusion.20), channel_id=1, source_target_pairs={{0,8},{1,9},{2,10},{3,11},{4,12},{5,13},{6,14},{7,15},{8,0},{9,1},... | collective-permute-start | bytes 2764808 | tf_op jit(solution)/shard_map/ppermute | solution.py:356
  70.7 24.4 %collective-permute-start.13 = (bf16[512,768]{1,0:T(8,128)(2,1)}, bf16[512,768]{1,0:T(8,128)(2,1)}, u32[]{:S(2)}, u32[]{:S(2)}) collective-permute-start(bf16[512,768]{1,0:T(8,128)(2,1)} %param.33), channel_id=1, source_target_pairs={{1,4},{3,6},{4,1},{6,3},{9,12},{11,14},{12,9},{14,11},{17,20},{19,... | collective-permute-start | bytes 2359304 | tf_op jit(solution)/shard_map/ppermute | solution.py:356
  99.8 18.8 %collective-permute-start.16 = (f32[512,768]{1,0:T(8,128)S(1)}, f32[512,768]{1,0:T(8,128)}, u32[]{:S(2)}, u32[]{:S(2)}) collective-permute-start(f32[512,768]{1,0:T(8,128)S(1)} %fusion.48), channel_id=1, source_target_pairs={{0,4},{1,5},{2,6},{3,7},{4,0},{5,1},{6,2},{7,3},{8,12},{9,13},{10,... | collective-permute-start | bytes 4718600 | tf_op jit(solution)/shard_map/ppermute | solution.py:356
  102.5 14.9 %collective-permute-start.19 = (bf16[3,104,768]{2,1,0:T(8,128)(2,1)S(1)}, bf16[3,104,768]{2,1,0:T(8,128)(2,1)S(1)}, u32[]{:S(2)}, u32[]{:S(2)}) collective-permute-start(bf16[3,104,768]{2,1,0:T(8,128)(2,1)S(1)} %slice.319), channel_id=1, source_target_pairs={{0,16},{1,17},{2,18},{3,19},{4,20},{5,21},{6,22},{7,23},{8,24},{9,... | collective-permute-start | bytes 1437704 | tf_op jit(solution)/shard_map/ppermute | solution.py:356
  166.2 33.9 %collective-permute-start.26 = (bf16[2,2,200,768]{3,2,1,0:T(8,128)(2,1)}, bf16[2,2,200,768]{3,2,1,0:T(8,128)(2,1)}, u32[]{:S(2)}, u32[]{:S(2)}) collective-permute-start(bf16[2,2,200,768]{3,2,1,0:T(8,128)(2,1)} %get-tuple-element.168), channel_id=1, source_target_pairs={{0,16},{1,17},{2,18},{3,19},{4,20},{5,21},{6,22},{7,23},{8,24},{9,... | collective-permute-start | bytes 3686408 | tf_op jit(solution)/shard_map/ppermute | solution.py:356
  166.4 33.6 %collective-permute-start.25 = (bf16[2,2,200,768]{3,2,1,0:T(8,128)(2,1)}, bf16[2,2,200,768]{3,2,1,0:T(8,128)(2,1)}, u32[]{:S(2)}, u32[]{:S(2)}) collective-permute-start(bf16[2,2,200,768]{3,2,1,0:T(8,128)(2,1)} %get-tuple-element.169), channel_id=1, source_target_pairs={{0,8},{1,9},{2,10},{3,11},{4,12},{5,13},{6,14},{7,15},{8,0},{9,1},... | collective-permute-start | bytes 3686408 | tf_op jit(solution)/shard_map/ppermute | solution.py:356
  177.2 103.5 %collective-permute-start.21 = (bf16[512,768]{1,0:T(8,128)(2,1)S(1)}, bf16[512,768]{1,0:T(8,128)(2,1)}, u32[]{:S(2)}, u32[]{:S(2)}) collective-permute-start(bf16[512,768]{1,0:T(8,128)(2,1)S(1)} %copy-done.19), channel_id=1, source_target_pairs={{1,4},{3,6},{4,1},{6,3},{9,12},{11,14},{12,9},{14,11},{17,20},{19,... | collective-permute-start | bytes 2359304 | tf_op jit(solution)/shard_map/ppermute | solution.py:356
  202.8 15.8 %collective-permute-start.27 = (bf16[2,200,768]{2,1,0:T(8,128)(2,1)}, bf16[2,200,768]{2,1,0:T(8,128)(2,1)}, u32[]{:S(2)}, u32[]{:S(2)}) collective-permute-start(bf16[2,200,768]{2,1,0:T(8,128)(2,1)} %get-tuple-element.106), channel_id=1, source_target_pairs={{0,8},{1,9},{2,10},{3,11},{4,12},{5,13},{6,14},{7,15},{8,0},{9,1},... | collective-permute-start | bytes 1843208 | tf_op jit(solution)/shard_map/ppermute | solution.py:356
  203.3 15.7 %collective-permute-start.28 = (bf16[2,200,768]{2,1,0:T(8,128)(2,1)S(1)}, bf16[2,200,768]{2,1,0:T(8,128)(2,1)}, u32[]{:S(2)}, u32[]{:S(2)}) collective-permute-start(bf16[2,200,768]{2,1,0:T(8,128)(2,1)S(1)} %get-tuple-element.107), channel_id=1, source_target_pairs={{0,16},{1,17},{2,18},{3,19},{4,20},{5,21},{6,22},{7,23},{8,24},{9,... | collective-permute-start | bytes 1843208 | tf_op jit(solution)/shard_map/ppermute | solution.py:356
  223.0 15.1 %collective-permute-start.30 = (bf16[408,768]{1,0:T(8,128)(2,1)S(1)}, bf16[408,768]{1,0:T(8,128)(2,1)S(1)}, u32[]{:S(2)}, u32[]{:S(2)}) collective-permute-start(bf16[408,768]{1,0:T(8,128)(2,1)S(1)} %get-tuple-element.194), channel_id=1, source_target_pairs={{0,8},{1,9},{2,10},{3,11},{4,12},{5,13},{6,14},{7,15},{8,0},{9,1},... | collective-permute-start | bytes 1880072 | tf_op jit(solution)/shard_map/ppermute | solution.py:356
  224.1 15.1 %collective-permute-start.31 = (bf16[408,768]{1,0:T(8,128)(2,1)S(1)}, bf16[408,768]{1,0:T(8,128)(2,1)S(1)}, u32[]{:S(2)}, u32[]{:S(2)}) collective-permute-start(bf16[408,768]{1,0:T(8,128)(2,1)S(1)} %get-tuple-element.195), channel_id=1, source_target_pairs={{0,16},{1,17},{2,18},{3,19},{4,20},{5,21},{6,22},{7,23},{8,24},{9,... | collective-permute-start | bytes 1880072 | tf_op jit(solution)/shard_map/ppermute | solution.py:356
  227.3 26.7 %collective-permute-start.33 = (bf16[2,200,768]{2,1,0:T(8,128)(2,1)S(1)}, bf16[2,200,768]{2,1,0:T(8,128)(2,1)S(1)}, u32[]{:S(2)}, u32[]{:S(2)}) collective-permute-start(bf16[2,200,768]{2,1,0:T(8,128)(2,1)S(1)} %get-tuple-element.165), channel_id=1, source_target_pairs={{0,2},{1,3},{2,0},{3,1},{4,6},{5,7},{6,4},{7,5},{8,10},{9,11},{10,... | collective-permute-start | bytes 1843208 | tf_op jit(solution)/shard_map/ppermute | solution.py:356
  227.8 24.6 %collective-permute-start.32 = (bf16[408,768]{1,0:T(8,128)(2,1)S(1)}, bf16[408,768]{1,0:T(8,128)(2,1)S(1)}, u32[]{:S(2)}, u32[]{:S(2)}) collective-permute-start(bf16[408,768]{1,0:T(8,128)(2,1)S(1)} %get-tuple-element.196), channel_id=1, source_target_pairs={{0,24},{1,25},{2,26},{3,27},{4,28},{5,29},{6,30},{7,31},{8,16},{9,... | collective-permute-start | bytes 1880072 | tf_op jit(solution)/shard_map/ppermute | solution.py:356
  257.5 14.1 %collective-permute-start.37 = (f32[512,768]{1,0:T(8,128)S(1)}, f32[512,768]{1,0:T(8,128)S(1)}, u32[]{:S(2)}, u32[]{:S(2)}) collective-permute-start(f32[512,768]{1,0:T(8,128)S(1)} %fusion.39), channel_id=1, source_target_pairs={{0,4},{1,5},{2,6},{3,7},{4,0},{5,1},{6,2},{7,3},{8,12},{9,13},{10,... | collective-permute-start | bytes 4718600 | tf_op jit(solution)/shard_map/ppermute | solution.py:356
  266.2 16.7 %collective-permute-start.43 = (bf16[200,768]{1,0:T(8,128)(2,1)S(1)}, bf16[200,768]{1,0:T(8,128)(2,1)S(1)}, u32[]{:S(2)}, u32[]{:S(2)}) collective-permute-start(bf16[200,768]{1,0:T(8,128)(2,1)S(1)} %fusion.46), channel_id=1, source_target_pairs={{0,24},{1,25},{2,26},{3,27},{4,28},{5,29},{6,30},{7,31},{8,16},{9,... | collective-permute-start | bytes 921608 | tf_op jit(solution)/shard_map/ppermute | solution.py:356
  283.1 16.3 %collective-permute-start.44 = (bf16[4,200,768]{2,1,0:T(8,128)(2,1)S(1)}, bf16[4,200,768]{2,1,0:T(8,128)(2,1)}, u32[]{:S(2)}, u32[]{:S(2)}) collective-permute-start(bf16[4,200,768]{2,1,0:T(8,128)(2,1)S(1)} %pad_maximum_fusion.6.own_ref), channel_id=1, source_target_pairs={{0,4},{1,5},{2,6},{3,7},{4,0},{5,1},{6,2},{7,3},{8,12},{9,13},{10,... | collective-permute-start | bytes 3686408 | tf_op jit(solution)/shard_map/ppermute | solution.py:356
  284.2 13.9 %collective-permute-start.38 = (bf16[512,768]{1,0:T(8,128)(2,1)}, bf16[512,768]{1,0:T(8,128)(2,1)S(1)}, u32[]{:S(2)}, u32[]{:S(2)}) collective-permute-start(bf16[512,768]{1,0:T(8,128)(2,1)} %add_convert_fusion.1), channel_id=1, source_target_pairs={{1,4},{3,6},{4,1},{6,3},{9,12},{11,14},{12,9},{14,11},{17,20},{19,... | collective-permute-start | bytes 2359304 | tf_op jit(solution)/shard_map/ppermute | solution.py:356
  287.3 17.7 %collective-permute-start.47 = (bf16[192,768]{1,0:T(8,128)(2,1)S(1)}, bf16[192,768]{1,0:T(8,128)(2,1)S(1)}, u32[]{:S(2)}, u32[]{:S(2)}) collective-permute-start(bf16[192,768]{1,0:T(8,128)(2,1)S(1)} %slice.440.refs_0_), channel_id=1, source_target_pairs={{0,24},{1,25},{2,26},{3,27},{4,28},{5,29},{6,30},{7,31},{8,16},{9,... | collective-permute-start | bytes 884744 | tf_op jit(solution)/shard_map/ppermute | solution.py:356
  288.2 16.8 %collective-permute-start.46 = (bf16[192,768]{1,0:T(8,128)(2,1)S(1)}, bf16[192,768]{1,0:T(8,128)(2,1)S(1)}, u32[]{:S(2)}, u32[]{:S(2)}) collective-permute-start(bf16[192,768]{1,0:T(8,128)(2,1)S(1)} %slice.440.refs_0_), channel_id=1, source_target_pairs={{0,16},{1,17},{2,18},{3,19},{4,20},{5,21},{6,22},{7,23},{8,24},{9,... | collective-permute-start | bytes 884744 | tf_op jit(solution)/shard_map/ppermute | solution.py:356
  289.2 15.8 %collective-permute-start.45 = (bf16[192,768]{1,0:T(8,128)(2,1)S(1)}, bf16[192,768]{1,0:T(8,128)(2,1)}, u32[]{:S(2)}, u32[]{:S(2)}) collective-permute-start(bf16[192,768]{1,0:T(8,128)(2,1)S(1)} %slice.440.refs_0_), channel_id=1, source_target_pairs={{0,8},{1,9},{2,10},{3,11},{4,12},{5,13},{6,14},{7,15},{8,0},{9,1},... | collective-permute-start | bytes 884744 | tf_op jit(solution)/shard_map/ppermute | solution.py:356
  (83 other events, 601.9 us)

commit v5 on v4

--- a/solution.py
+++ b/solution.py
@@ -673,7 +673,9 @@
         tall = 2 * heads * HEAD // 2
         many = heads - 1
         early, grad_w, early_b = back(0, many, None)
-        early, go_other, ffn_x, ffn_y = sync(early, go_other, ffn_x, ffn_y)
+        early, go_other, ffn_x, ffn_y, layer_output = sync(
+            early, go_other, ffn_x, ffn_y, layer_output
+        )
         low = [ffn_grads[0, :2] + ffn_x[0].astype(F32), ffn_grads[3, :2] + ffn_x[1].astype(F32)]
         high = [ffn_grads[0, 2:] + ffn_y[1].astype(F32), ffn_grads[1, 2:] + ffn_y[0].astype(F32)]
         ffn_y, ffn_x = low[1].astype(BF16), high[1].astype(BF16)

time: 315 us -> 314 us (level)
    unnamed x122 -> x118, local copies, waits for them, and re-layouts: 9 us -> 9.11 us
  transfers between devices with their start and end apart: 48 -> 48, of which waited for: 15 -> 18; matrix products, arithmetic and copies ran while one was open for 18% -> 15% of each run, Pallas kernels for 17% -> 17%
where the time goes in v5:
time: 314 us; the launch traced here: 309 us
  waiting for transfers between devices  71.2 us (23%)
  starting transfers between devices  69.5 us (22%)
  Pallas kernels  57.3 us (18%)
  other arithmetic  42.7 us (14%)
  matrix products  40.2 us (13%)
  local copies, waits for them, and re-layouts  22.5 us (7%)
  between operations  5.06 us (2%)
    ppermute x48, waiting for transfers between devices, permute(): return lax.ppermute(array, JOINT, pairs)  71.2 us
    ppermute x48, starting transfers between devices, permute(): return lax.ppermute(array, JOINT, pairs)  69.5 us
    pallas_call x2, Pallas kernels, attend_back(): pl.pallas_call(body, grid=(n,), in_specs=[pl.BlockSpec((LEN, 2 * HEAD), l...  31.6 us
    pallas_call x1, Pallas kernels, attend(): pl.pallas_call(attend_kernel, grid=(n,), in_specs=[pl.BlockSpec((LEN, 2 *...  18.1 us
    dot_general x3, matrix products, nt(): lax.dot_general(a, b, (((1,), (1,)), ((), ())), preferred_element_type=F32)  17.4 us
    dot_general x8, matrix products, nn(): lax.dot_general(a, b, (((1,), (0,)), ((), ())), preferred_element_type=F32)  14.3 us
    unnamed x118, local copies, waits for them, and re-layouts  9.11 us
    dot_general x2, matrix products, tn(): lax.dot_general(a, b, (((0,), (0,)), ((), ())), preferred_element_type=F32)  8.5 us
  transfers between devices with their start and end apart: 48, of which 18 were waited for; matrix products, arithmetic and copies ran while one was open for 15% of the time, Pallas kernels for 17%

profile of v5, /device:TPU:1, one launch (start us, length us, event | category | flops | bytes accessed | tf_op | source)
XLA Modules:
  0.0 308.5 jit_solution(18161054384664841658)
XLA Ops:
  10.1 7.0 %collective-permute-done.1 = bf16[200,768]{1,0:T(8,128)(2,1)} collective-permute-done((bf16[200,768]{1,0:T(8,128)(2,1)S(1)}, bf16[200,768]{1,0:T(8,128)(2,1)}, u32[]{:S(2)}, u32[]{:S(2)}) %collective-permute-start.1) | collective-permute-done | bytes 307232 | tf_op jit(solution)/shard_map/ppermute | solution.py:356
  17.1 7.9 %collective-permute-done = bf16[200,768]{1,0:T(8,128)(2,1)} collective-permute-done((bf16[200,768]{1,0:T(8,128)(2,1)S(1)}, bf16[200,768]{1,0:T(8,128)(2,1)}, u32[]{:S(2)}, u32[]{:S(2)}) %collective-permute-start) | collective-permute-done | bytes 307232 | tf_op jit(solution)/shard_map/ppermute | solution.py:356
  36.0 6.7 %collective-permute-done.7 = bf16[200,768]{1,0:T(8,128)(2,1)S(1)} collective-permute-done((bf16[200,768]{1,0:T(8,128)(2,1)S(1)}, bf16[200,768]{1,0:T(8,128)(2,1)S(1)}, u32[]{:S(2)}, u32[]{:S(2)}) %collective-permute-start.7) | collective-permute-done | bytes 307232 | tf_op jit(solution)/shard_map/ppermute | solution.py:356
  58.3 5.7 %add_convert_fusion.q_ref.k_ref.v_ref.refs_0_.refs_1_.refs_2_ = bf16[1024,1152]{1,0:T(8,128)(2,1)} fusion(bf16[1152,768]{1,0:T(8,128)(2,1)S(1)} %bitcast.197, f32[1152]{0:T(1024)S(1)} %add.291, bf16[512,768]{1,0:T(8,128)(2,1)} %collective-permute-done.4.refs_6_, bf16[512,768]{1,0:T(8,128)(2,1)} %fusion.18.refs_5_), kind=kOutput, calls=%fused_computation.16 | convolution fusion | flops 1817444352 | bytes 5706240 | tf_op jit(solution)/shard_map/dot_general | solution.py:42
  64.0 6.4 %collective-permute-start.15 = (bf16[3,200,768]{2,1,0:T(8,128)(2,1)}, bf16[3,200,768]{2,1,0:T(8,128)(2,1)}, u32[]{:S(2)}, u32[]{:S(2)}) collective-permute-start(bf16[3,200,768]{2,1,0:T(8,128)(2,1)} %pad_maximum_fusion.20), channel_id=1, source_target_pairs={{0,16},{1,17},{2,18},{3,19},{4,20},{5,21},{6,22},{7,23},{8,24},{9,... | collective-permute-start | bytes 2764808 | tf_op jit(solution)/shard_map/ppermute | solution.py:356
  70.6 3.6 %collective-permute-start.13 = (bf16[512,768]{1,0:T(8,128)(2,1)}, bf16[512,768]{1,0:T(8,128)(2,1)}, u32[]{:S(2)}, u32[]{:S(2)}) collective-permute-start(bf16[512,768]{1,0:T(8,128)(2,1)} %param.33), channel_id=1, source_target_pairs={{1,4},{3,6},{4,1},{6,3},{9,12},{11,14},{12,9},{14,11},{17,20},{19,... | collective-permute-start | bytes 2359304 | tf_op jit(solution)/shard_map/ppermute | solution.py:356
  76.9 18.1 %attend.1 = (f32[1024,384]{1,0:T(8,128)}, f32[3,2,1024]{2,1,0:T(2,128)}) custom-call(bf16[1024,1152]{1,0:T(8,128)(2,1)} %add_convert_fusion.q_ref.k_ref.v_ref.refs_0_.refs_1_.refs_2_, bf16[1024,1152]{1,0:T(8,128)(2,1)} %add_convert_fusion.q_ref.k_ref.v_ref.refs_0_.refs_1_.refs_2_, ...), custom_call_target="tpu_custom_call" | custom-call | tf_op jit(solution)/shard_map/attend/pallas_call | solution.py:87
  95.1 3.1 %minimum_convert_fusion.2 = bf16[1024,384]{1,0:T(8,128)(2,1)} fusion(f32[1024,384]{1,0:T(8,128)} %get-tuple-element.90.refs_8_, bf16[]{:T(256)S(6)} %neg.12, f32[]{:T(128)} %bitcast.14), kind=kLoop, calls=%fused_computation.66 | loop fusion | flops 1966080 | bytes 2359302 | tf_op jit(solution)/shard_map/convert_element_type | solution.py:578
  111.6 5.7 %collective-permute-done.18 = bf16[3,96,768]{2,1,0:T(8,128)(2,1)S(1)} collective-permute-done((bf16[3,96,768]{2,1,0:T(8,128)(2,1)S(1)}, bf16[3,96,768]{2,1,0:T(8,128)(2,1)S(1)}, u32[]{:S(2)}, u32[]{:S(2)}) %collective-permute-start.18) | collective-permute-done | bytes 442400 | tf_op jit(solution)/shard_map/ppermute | solution.py:356
  126.7 4.0 %minimum_convert_fusion = (bf16[1024,1536]{1,0:T(8,128)(2,1)S(1)}, f32[1024,1536]{1,0:T(8,128)S(1)}) fusion(f32[1536]{0:T(1024)S(1)} %reshape.475, bf16[]{:T(256)S(6)} %neg.14, f32[]{:T(128)} %bitcast.36, bf16[1536,768]{1,0:T(8,128)(2,1)S(1)} %bitcast.192, bf16[512,768]{1,0:T(8,128)(2,1)S(1)} %collective-permute-done.17, ...), kind=kOutput, calls=%fused_computation.11 | convolution fusion | flops 2434793472 | bytes 13375494 | tf_op jit(solution)/shard_map/dot_general | solution.py:42
  143.7 7.7 %fusion.78 = (bf16[1024,1536]{1,0:T(8,128)(2,1)}, bf16[1536]{0:T(1024)(128)(2,1)S(1)}) fusion(f32[]{:T(128)} %bitcast.36, f32[1024,1536]{1,0:T(8,128)S(1)} %get-tuple-element.225, f32[1536]{0:T(1024)S(1)} %reshape.475, bf16[1536,768]{1,0:T(8,128)(2,1)S(1)} %bitcast.191, bf16[512,768]{1,0:T(8,128)(2,1)S(1)} %collective-permute-done.21, ...), kind=kOutput, calls=%fused_computation.269 | convolution fusion | flops 2444229120 | bytes 13378564 | tf_op jit(solution)/shard_map/dot_general | solution.py:42
  151.6 5.1 %convolution_convert_fusion.1 = bf16[1536,768]{1,0:T(8,128)(2,1)S(1)} fusion(bf16[1024,1536]{1,0:T(8,128)(2,1)} %get-tuple-element.95, bf16[512,768]{1,0:T(8,128)(2,1)} %copy-done.49, bf16[512,768]{1,0:T(8,128)(2,1)} %copy-done.32), kind=kOutput, calls=%fused_computation.18 | convolution fusion | flops 2420244480 | bytes 7077888 | tf_op jit(solution)/shard_map/dot_general | solution.py:50
  156.7 3.4 %convolution_convert_fusion = bf16[1536,768]{1,0:T(8,128)(2,1)S(1)} fusion(bf16[1024,1536]{1,0:T(8,128)(2,1)S(1)} %copy-done.53, bf16[512,768]{1,0:T(8,128)(2,1)S(1)} %copy-done.51, bf16[512,768]{1,0:T(8,128)(2,1)S(1)} %copy-done.34), kind=kOutput, calls=%fused_computation.17 | convolution fusion | flops 2420244480 | bytes 7077888 | tf_op jit(solution)/shard_map/dot_general | solution.py:50
  180.6 19.9 %attend_back.2 = (bf16[1024,768]{1,0:T(8,128)(2,1)}, bf16[4,384,768]{2,1,0:T(8,128)(2,1)}, f32[2,2,128]{2,1,0:T(2,128)}) custom-call(bf16[1024,1152]{1,0:T(8,128)(2,1)} %add_convert_fusion.q_ref.k_ref.v_ref.refs_0_.refs_1_.refs_2_, bf16[1024,1152]{1,0:T(8,128)(2,1)} %add_convert_fusion.q_ref.k_ref.v_ref.refs_0_.refs_1_.refs_2_, ...), custom_call_target="tpu_custom_call" | custom-call | tf_op jit(solution)/shard_map/attend_back/pallas_call | solution.py:212
  204.3 11.7 %attend_back.3 = (bf16[1024,384]{1,0:T(8,128)(2,1)}, bf16[4,384,768]{2,1,0:T(8,128)(2,1)}, f32[1,2,128]{2,1,0:T(2,128)}) custom-call(bf16[1024,1152]{1,0:T(8,128)(2,1)} %add_convert_fusion.q_ref.k_ref.v_ref.refs_0_.refs_1_.refs_2_, bf16[1024,1152]{1,0:T(8,128)(2,1)} %add_convert_fusion.q_ref.k_ref.v_ref.refs_0_.refs_1_.refs_2_, ...), custom_call_target="tpu_custom_call", output_to_operand_aliasing={{1}: (13, {})} | custom-call | flops 9663676416 | bytes 4718592 | tf_op jit(solution)/shard_map/attend_back/pallas_call | solution.py:212
  227.9 7.9 %collective-permute-done.30 = bf16[408,768]{1,0:T(8,128)(2,1)S(1)} collective-permute-done((bf16[408,768]{1,0:T(8,128)(2,1)S(1)}, bf16[408,768]{1,0:T(8,128)(2,1)S(1)}, u32[]{:S(2)}, u32[]{:S(2)}) %collective-permute-start.30) | collective-permute-done | bytes 626720 | tf_op jit(solution)/shard_map/ppermute | solution.py:356
  236.6 13.7 %collective-permute-done.32 = bf16[408,768]{1,0:T(8,128)(2,1)S(1)} collective-permute-done((bf16[408,768]{1,0:T(8,128)(2,1)S(1)}, bf16[408,768]{1,0:T(8,128)(2,1)S(1)}, u32[]{:S(2)}, u32[]{:S(2)}) %collective-permute-start.32) | collective-permute-done | bytes 626720 | tf_op jit(solution)/shard_map/ppermute | solution.py:356
  254.6 5.0 %collective-permute-start.35 = (bf16[216,768]{1,0:T(8,128)(2,1)S(1)}, bf16[216,768]{1,0:T(8,128)(2,1)S(1)}, u32[]{:S(2)}, u32[]{:S(2)}) collective-permute-start(bf16[216,768]{1,0:T(8,128)(2,1)S(1)} %get-tuple-element.118), channel_id=1, source_target_pairs={{2,0},{3,1},{4,6},{5,7},{10,8},{11,9},{12,14},{13,15},{18,16},{19,... | collective-permute-start | bytes 995336 | tf_op jit(solution)/shard_map/ppermute | solution.py:356
  261.0 4.9 %collective-permute-start.36 = (bf16[216,768]{1,0:T(8,128)(2,1)S(1)}, bf16[216,768]{1,0:T(8,128)(2,1)S(1)}, u32[]{:S(2)}, u32[]{:S(2)}) collective-permute-start(bf16[216,768]{1,0:T(8,128)(2,1)S(1)} %get-tuple-element.117), channel_id=1, source_target_pairs={{2,1},{3,0},{4,7},{5,6},{10,9},{11,8},{12,15},{13,14},{18,17},{19,... | collective-permute-start | bytes 995336 | tf_op jit(solution)/shard_map/ppermute | solution.py:356
  269.1 3.8 %collective-permute-done.36 = bf16[216,768]{1,0:T(8,128)(2,1)S(1)} collective-permute-done((bf16[216,768]{1,0:T(8,128)(2,1)S(1)}, bf16[216,768]{1,0:T(8,128)(2,1)S(1)}, u32[]{:S(2)}, u32[]{:S(2)}) %collective-permute-start.36) | collective-permute-done | bytes 331808 | tf_op jit(solution)/shard_map/ppermute | solution.py:356
  276.0 3.9 %collective-permute-start.39 = (bf16[216,768]{1,0:T(8,128)(2,1)S(1)}, bf16[216,768]{1,0:T(8,128)(2,1)S(1)}, u32[]{:S(2)}, u32[]{:S(2)}) collective-permute-start(bf16[216,768]{1,0:T(8,128)(2,1)S(1)} %pad_maximum_fusion.28), channel_id=1, source_target_pairs={{0,4},{1,5},{2,6},{3,7},{4,0},{5,1},{6,2},{7,3},{8,12},{9,13},{10,... | collective-permute-start | bytes 995336 | tf_op jit(solution)/shard_map/ppermute | solution.py:356
  291.6 6.4 %collective-permute-done.38 = bf16[512,768]{1,0:T(8,128)(2,1)S(1)} collective-permute-done((bf16[512,768]{1,0:T(8,128)(2,1)S(1)}, bf16[512,768]{1,0:T(8,128)(2,1)S(1)}, u32[]{:S(2)}, u32[]{:S(2)}) %collective-permute-start.38) | collective-permute-done | bytes 786464 | tf_op jit(solution)/shard_map/ppermute | solution.py:356
  300.7 4.1 %unpack_ffn.1 = (f32[768,768]{1,0:T(8,128)}, f32[768,768]{1,0:T(8,128)}) custom-call(s32[2]{0:T(128)} %pad_add_fusion.where_ref, bf16[4,200,768]{2,1,0:T(8,128)(2,1)} %copy-done.14, bf16[4,200,768]{2,1,0:T(8,128)(2,1)} %collective-permute-done.44.other_ref), custom_call_target="tpu_custom_call" | custom-call | tf_op jit(solution)/shard_map/unpack_ffn/pallas_call | solution.py:317
  304.8 3.4 %unpack.1 = (f32[3,192,768]{2,1,0:T(8,128)}, f32[192,768]{1,0:T(8,128)}) custom-call(s32[1]{0:T(128)} %bitcast.58.plane_ref, bf16[192,768]{1,0:T(8,128)(2,1)} %copy-done.29, bf16[192,768]{1,0:T(8,128)(2,1)} %collective-permute-done.45.refs_1_, bf16[192,768]{1,0:T(8,128)(2,1)} %collective-permute-done.46.refs_2_, bf16[192,768]{1,0:T(8,128)(2,1)} %collective-permute-done.47.refs_3_), custom_call_target="tpu_custom_call" | custom-call | tf_op jit(solution)/shard_map/unpack/pallas_call | solution.py:280
  (361 shorter events, 134.4 us)
Async XLA Ops:
  5.9 19.2 %collective-permute-start = (bf16[200,768]{1,0:T(8,128)(2,1)S(1)}, bf16[200,768]{1,0:T(8,128)(2,1)}, u32[]{:S(2)}, u32[]{:S(2)}) collective-permute-start(bf16[200,768]{1,0:T(8,128)(2,1)S(1)} %fusion.52), channel_id=1, source_target_pairs={{0,2},{1,3},{6,4},{7,5},{8,10},{9,11},{14,12},{15,13},{16,18},{17,... | collective-permute-start | bytes 921608 | tf_op jit(solution)/shard_map/ppermute | solution.py:356
  25.0 23.4 %collective-permute-start.3 = (bf16[512,768]{1,0:T(8,128)(2,1)S(1)}, bf16[512,768]{1,0:T(8,128)(2,1)}, u32[]{:S(2)}, u32[]{:S(2)}) collective-permute-start(bf16[512,768]{1,0:T(8,128)(2,1)S(1)} %copy-done.31), channel_id=1, source_target_pairs={{1,4},{3,6},{4,1},{6,3},{9,12},{11,14},{12,9},{14,11},{17,20},{19,... | collective-permute-start | bytes 2359304 | tf_op jit(solution)/shard_map/ppermute | solution.py:356
  29.1 13.5 %collective-permute-start.5 = (bf16[2,200,768]{2,1,0:T(8,128)(2,1)}, bf16[2,200,768]{2,1,0:T(8,128)(2,1)S(1)}, u32[]{:S(2)}, u32[]{:S(2)}) collective-permute-start(bf16[2,200,768]{2,1,0:T(8,128)(2,1)} %get-tuple-element.193), channel_id=1, source_target_pairs={{0,8},{1,9},{2,10},{3,11},{4,12},{5,13},{6,14},{7,15},{8,0},{9,1},... | collective-permute-start | bytes 1843208 | tf_op jit(solution)/shard_map/ppermute | solution.py:356
  64.0 31.1 %collective-permute-start.15 = (bf16[3,200,768]{2,1,0:T(8,128)(2,1)}, bf16[3,200,768]{2,1,0:T(8,128)(2,1)}, u32[]{:S(2)}, u32[]{:S(2)}) collective-permute-start(bf16[3,200,768]{2,1,0:T(8,128)(2,1)} %pad_maximum_fusion.20), channel_id=1, source_target_pairs={{0,16},{1,17},{2,18},{3,19},{4,20},{5,21},{6,22},{7,23},{8,24},{9,... | collective-permute-start | bytes 2764808 | tf_op jit(solution)/shard_map/ppermute | solution.py:356
  70.3 24.7 %collective-permute-start.14 = (bf16[3,200,768]{2,1,0:T(8,128)(2,1)}, bf16[3,200,768]{2,1,0:T(8,128)(2,1)}, u32[]{:S(2)}, u32[]{:S(2)}) collective-permute-start(bf16[3,200,768]{2,1,0:T(8,128)(2,1)} %pad_maximum_fusion.20), channel_id=1, source_target_pairs={{0,8},{1,9},{2,10},{3,11},{4,12},{5,13},{6,14},{7,15},{8,0},{9,1},... | collective-permute-start | bytes 2764808 | tf_op jit(solution)/shard_map/ppermute | solution.py:356
  70.6 24.4 %collective-permute-start.13 = (bf16[512,768]{1,0:T(8,128)(2,1)}, bf16[512,768]{1,0:T(8,128)(2,1)}, u32[]{:S(2)}, u32[]{:S(2)}) collective-permute-start(bf16[512,768]{1,0:T(8,128)(2,1)} %param.33), channel_id=1, source_target_pairs={{1,4},{3,6},{4,1},{6,3},{9,12},{11,14},{12,9},{14,11},{17,20},{19,... | collective-permute-start | bytes 2359304 | tf_op jit(solution)/shard_map/ppermute | solution.py:356
  99.8 18.8 %collective-permute-start.16 = (f32[512,768]{1,0:T(8,128)S(1)}, f32[512,768]{1,0:T(8,128)}, u32[]{:S(2)}, u32[]{:S(2)}) collective-permute-start(f32[512,768]{1,0:T(8,128)S(1)} %fusion.48), channel_id=1, source_target_pairs={{0,4},{1,5},{2,6},{3,7},{4,0},{5,1},{6,2},{7,3},{8,12},{9,13},{10,... | collective-permute-start | bytes 4718600 | tf_op jit(solution)/shard_map/ppermute | solution.py:356
  102.5 14.9 %collective-permute-start.19 = (bf16[3,104,768]{2,1,0:T(8,128)(2,1)S(1)}, bf16[3,104,768]{2,1,0:T(8,128)(2,1)S(1)}, u32[]{:S(2)}, u32[]{:S(2)}) collective-permute-start(bf16[3,104,768]{2,1,0:T(8,128)(2,1)S(1)} %slice.319), channel_id=1, source_target_pairs={{0,16},{1,17},{2,18},{3,19},{4,20},{5,21},{6,22},{7,23},{8,24},{9,... | collective-permute-start | bytes 1437704 | tf_op jit(solution)/shard_map/ppermute | solution.py:356
  164.6 35.9 %collective-permute-start.26 = (bf16[512,768]{1,0:T(8,128)(2,1)}, bf16[512,768]{1,0:T(8,128)(2,1)}, u32[]{:S(2)}, u32[]{:S(2)}) collective-permute-start(bf16[512,768]{1,0:T(8,128)(2,1)} %get-tuple-element.175), channel_id=1, source_target_pairs={{1,4},{3,6},{4,1},{6,3},{9,12},{11,14},{12,9},{14,11},{17,20},{19,... | collective-permute-start | bytes 2359304 | tf_op jit(solution)/shard_map/ppermute | solution.py:356
  168.7 31.8 %collective-permute-start.25 = (bf16[2,2,200,768]{3,2,1,0:T(8,128)(2,1)}, bf16[2,2,200,768]{3,2,1,0:T(8,128)(2,1)}, u32[]{:S(2)}, u32[]{:S(2)}) collective-permute-start(bf16[2,2,200,768]{3,2,1,0:T(8,128)(2,1)} %get-tuple-element.170), channel_id=1, source_target_pairs={{0,16},{1,17},{2,18},{3,19},{4,20},{5,21},{6,22},{7,23},{8,24},{9,... | collective-permute-start | bytes 3686408 | tf_op jit(solution)/shard_map/ppermute | solution.py:356
  168.9 31.6 %collective-permute-start.24 = (bf16[2,2,200,768]{3,2,1,0:T(8,128)(2,1)}, bf16[2,2,200,768]{3,2,1,0:T(8,128)(2,1)}, u32[]{:S(2)}, u32[]{:S(2)}) collective-permute-start(bf16[2,2,200,768]{3,2,1,0:T(8,128)(2,1)} %get-tuple-element.171), channel_id=1, source_target_pairs={{0,8},{1,9},{2,10},{3,11},{4,12},{5,13},{6,14},{7,15},{8,0},{9,1},... | collective-permute-start | bytes 3686408 | tf_op jit(solution)/shard_map/ppermute | solution.py:356
  202.4 15.3 %collective-permute-start.27 = (bf16[2,200,768]{2,1,0:T(8,128)(2,1)S(1)}, bf16[2,200,768]{2,1,0:T(8,128)(2,1)}, u32[]{:S(2)}, u32[]{:S(2)}) collective-permute-start(bf16[2,200,768]{2,1,0:T(8,128)(2,1)S(1)} %get-tuple-element.108), channel_id=1, source_target_pairs={{0,8},{1,9},{2,10},{3,11},{4,12},{5,13},{6,14},{7,15},{8,0},{9,1},... | collective-permute-start | bytes 1843208 | tf_op jit(solution)/shard_map/ppermute | solution.py:356
  202.9 14.9 %collective-permute-start.28 = (bf16[2,200,768]{2,1,0:T(8,128)(2,1)S(1)}, bf16[2,200,768]{2,1,0:T(8,128)(2,1)}, u32[]{:S(2)}, u32[]{:S(2)}) collective-permute-start(bf16[2,200,768]{2,1,0:T(8,128)(2,1)S(1)} %get-tuple-element.109), channel_id=1, source_target_pairs={{0,16},{1,17},{2,18},{3,19},{4,20},{5,21},{6,22},{7,23},{8,24},{9,... | collective-permute-start | bytes 1843208 | tf_op jit(solution)/shard_map/ppermute | solution.py:356
  221.6 14.2 %collective-permute-start.30 = (bf16[408,768]{1,0:T(8,128)(2,1)S(1)}, bf16[408,768]{1,0:T(8,128)(2,1)S(1)}, u32[]{:S(2)}, u32[]{:S(2)}) collective-permute-start(bf16[408,768]{1,0:T(8,128)(2,1)S(1)} %get-tuple-element.196), channel_id=1, source_target_pairs={{0,8},{1,9},{2,10},{3,11},{4,12},{5,13},{6,14},{7,15},{8,0},{9,1},... | collective-permute-start | bytes 1880072 | tf_op jit(solution)/shard_map/ppermute | solution.py:356
  222.8 13.8 %collective-permute-start.31 = (bf16[408,768]{1,0:T(8,128)(2,1)S(1)}, bf16[408,768]{1,0:T(8,128)(2,1)S(1)}, u32[]{:S(2)}, u32[]{:S(2)}) collective-permute-start(bf16[408,768]{1,0:T(8,128)(2,1)S(1)} %get-tuple-element.197), channel_id=1, source_target_pairs={{0,16},{1,17},{2,18},{3,19},{4,20},{5,21},{6,22},{7,23},{8,24},{9,... | collective-permute-start | bytes 1880072 | tf_op jit(solution)/shard_map/ppermute | solution.py:356
  226.0 27.9 %collective-permute-start.33 = (bf16[2,200,768]{2,1,0:T(8,128)(2,1)S(1)}, bf16[2,200,768]{2,1,0:T(8,128)(2,1)S(1)}, u32[]{:S(2)}, u32[]{:S(2)}) collective-permute-start(bf16[2,200,768]{2,1,0:T(8,128)(2,1)S(1)} %get-tuple-element.167), channel_id=1, source_target_pairs={{0,2},{1,3},{2,0},{3,1},{4,6},{5,7},{6,4},{7,5},{8,10},{9,11},{10,... | collective-permute-start | bytes 1843208 | tf_op jit(solution)/shard_map/ppermute | solution.py:356
  226.5 23.9 %collective-permute-start.32 = (bf16[408,768]{1,0:T(8,128)(2,1)S(1)}, bf16[408,768]{1,0:T(8,128)(2,1)S(1)}, u32[]{:S(2)}, u32[]{:S(2)}) collective-permute-start(bf16[408,768]{1,0:T(8,128)(2,1)S(1)} %get-tuple-element.198), channel_id=1, source_target_pairs={{0,24},{1,25},{2,26},{3,27},{4,28},{5,29},{6,30},{7,31},{8,16},{9,... | collective-permute-start | bytes 1880072 | tf_op jit(solution)/shard_map/ppermute | solution.py:356
  266.9 15.1 %collective-permute-start.43 = (bf16[200,768]{1,0:T(8,128)(2,1)S(1)}, bf16[200,768]{1,0:T(8,128)(2,1)S(1)}, u32[]{:S(2)}, u32[]{:S(2)}) collective-permute-start(bf16[200,768]{1,0:T(8,128)(2,1)S(1)} %fusion.46), channel_id=1, source_target_pairs={{0,24},{1,25},{2,26},{3,27},{4,28},{5,29},{6,30},{7,31},{8,16},{9,... | collective-permute-start | bytes 921608 | tf_op jit(solution)/shard_map/ppermute | solution.py:356
  267.9 15.6 %collective-permute-start.42 = (bf16[200,768]{1,0:T(8,128)(2,1)S(1)}, bf16[200,768]{1,0:T(8,128)(2,1)S(1)}, u32[]{:S(2)}, u32[]{:S(2)}) collective-permute-start(bf16[200,768]{1,0:T(8,128)(2,1)S(1)} %fusion.46), channel_id=1, source_target_pairs={{0,16},{1,17},{2,18},{3,19},{4,20},{5,21},{6,22},{7,23},{8,24},{9,... | collective-permute-start | bytes 921608 | tf_op jit(solution)/shard_map/ppermute | solution.py:356
  283.7 15.5 %collective-permute-start.44 = (bf16[4,200,768]{2,1,0:T(8,128)(2,1)S(1)}, bf16[4,200,768]{2,1,0:T(8,128)(2,1)}, u32[]{:S(2)}, u32[]{:S(2)}) collective-permute-start(bf16[4,200,768]{2,1,0:T(8,128)(2,1)S(1)} %pad_maximum_fusion.6.own_ref), channel_id=1, source_target_pairs={{0,4},{1,5},{2,6},{3,7},{4,0},{5,1},{6,2},{7,3},{8,12},{9,13},{10,... | collective-permute-start | bytes 3686408 | tf_op jit(solution)/shard_map/ppermute | solution.py:356
  284.2 13.7 %collective-permute-start.38 = (bf16[512,768]{1,0:T(8,128)(2,1)S(1)}, bf16[512,768]{1,0:T(8,128)(2,1)S(1)}, u32[]{:S(2)}, u32[]{:S(2)}) collective-permute-start(bf16[512,768]{1,0:T(8,128)(2,1)S(1)} %add_convert_fusion.1), channel_id=1, source_target_pairs={{1,4},{3,6},{4,1},{6,3},{9,12},{11,14},{12,9},{14,11},{17,20},{19,... | collective-permute-start | bytes 2359304 | tf_op jit(solution)/shard_map/ppermute | solution.py:356
  287.0 17.8 %collective-permute-start.47 = (bf16[192,768]{1,0:T(8,128)(2,1)S(1)}, bf16[192,768]{1,0:T(8,128)(2,1)}, u32[]{:S(2)}, u32[]{:S(2)}) collective-permute-start(bf16[192,768]{1,0:T(8,128)(2,1)S(1)} %slice.440.refs_0_), channel_id=1, source_target_pairs={{0,24},{1,25},{2,26},{3,27},{4,28},{5,29},{6,30},{7,31},{8,16},{9,... | collective-permute-start | bytes 884744 | tf_op jit(solution)/shard_map/ppermute | solution.py:356
  288.4 16.4 %collective-permute-start.46 = (bf16[192,768]{1,0:T(8,128)(2,1)S(1)}, bf16[192,768]{1,0:T(8,128)(2,1)}, u32[]{:S(2)}, u32[]{:S(2)}) collective-permute-start(bf16[192,768]{1,0:T(8,128)(2,1)S(1)} %slice.440.refs_0_), channel_id=1, source_target_pairs={{0,16},{1,17},{2,18},{3,19},{4,20},{5,21},{6,22},{7,23},{8,24},{9,... | collective-permute-start | bytes 884744 | tf_op jit(solution)/shard_map/ppermute | solution.py:356
  289.0 15.8 %collective-permute-start.45 = (bf16[192,768]{1,0:T(8,128)(2,1)S(1)}, bf16[192,768]{1,0:T(8,128)(2,1)}, u32[]{:S(2)}, u32[]{:S(2)}) collective-permute-start(bf16[192,768]{1,0:T(8,128)(2,1)S(1)} %slice.440.refs_0_), channel_id=1, source_target_pairs={{0,8},{1,9},{2,10},{3,11},{4,12},{5,13},{6,14},{7,15},{8,0},{9,1},... | collective-permute-start | bytes 884744 | tf_op jit(solution)/shard_map/ppermute | solution.py:356
  (81 other events, 599.2 us)
